TPU v7x, 32 devices: a whole 2x2x4 slice. The times are simulated.
32 devices in a mesh: dp: 4 (over z), chan: 8 (over y, x, core).
Axes of the slice: x: 2, y: 2, z: 4, core: 2. Of those that a mesh axis runs over, the one named last changes fastest.
Arguments:
- images: float32 [3, 32768], P(None, 'dp'), may hold values from -56 to 56
- frame_kinds: int32 [8], P('dp'), may hold values from 1 to 2
- series_len: int32 [8, 4], P('dp'), may hold values from 1 to 4
- probes: float32 [3, 32768], P(None, 'dp'), may hold values from -6 to 6
- cot_z: float32 [3, 32768], P(None, 'dp'), may hold values from -6 to 6
- cot_logdet: float32 [8, 4], P('dp'), may hold values from -4 to 4
- weight1: float32 [512, 27], P('chan'), may hold values from -6 to 6
- weight2: float32 [512, 512], P(None, 'chan'), may hold values from -6 to 6
- weight3: float32 [27, 512], P(None, 'chan'), may hold values from -6 to 6
- biases: float32 [2, 512], P(None, 'chan'), may hold values from 0 to 2.5
- small_params: float32 [3, 3], replicated, may hold values from -2 to 2
- power_u1: float32 [512], P('chan'), may hold values from -6 to 6
- power_u2: float32 [512], replicated, may hold values from -6 to 6
- power_u3: float32 [3], replicated, may hold values from -3 to 3
- moment_w1: float32 [512, 27], P('chan'), may hold values from -0.0014648438 to 0.0014648438
- second_w1: float32 [512, 27], P('chan'), may hold values from 5.3405763e-08 to 2.0980835e-07
- moment_w2: float32 [512, 512], P(None, 'chan'), may hold values from -0.0017089844 to 0.0017089844
- second_w2: float32 [512, 512], P(None, 'chan'), may hold values from 6.866455e-08 to 2.822876e-07
- moment_w3: float32 [27, 512], P(None, 'chan'), may hold values from -0.0234375 to 0.0234375
- second_w3: float32 [27, 512], P(None, 'chan'), may hold values from 1.1328125e-05 to 4.4921875e-05
- moment_bias: float32 [2, 512], P(None, 'chan'), may hold values from -0.0017089844 to 0.0017089844
- second_bias: float32 [2, 512], P(None, 'chan'), may hold values from 6.866455e-08 to 2.822876e-07
- moment_small: float32 [3, 3], replicated, may hold values from -0.625 to 0.625
- second_small: float32 [3, 3], replicated, may hold values from 0.0082 to 0.033
Outputs:
- z_out: float32 [3, 32768], P(None, 'dp')
- logdet: float32 [8, 4], P('dp')
- grad_input: float32 [3, 32768], P(None, 'dp')
- grad_norm: float32 [], replicated
- new_weight1: float32 [512, 27], P('chan')
- new_moment1: float32 [512, 27], P('chan')
- new_second1: float32 [512, 27], P('chan')
- new_weight2: float32 [512, 512], P(None, 'chan')
- new_moment2: float32 [512, 512], P(None, 'chan')
- new_second2: float32 [512, 512], P(None, 'chan')
- new_weight3: float32 [27, 512], P(None, 'chan')
- new_moment3: float32 [27, 512], P(None, 'chan')
- new_second3: float32 [27, 512], P(None, 'chan')
- clipped_bias: float32 [2, 512], P(None, 'chan')
- new_moment_bias: float32 [2, 512], P(None, 'chan')
- new_second_bias: float32 [2, 512], P(None, 'chan')
- new_small: float32 [3, 3], replicated
- new_moment_small: float32 [3, 3], replicated
- new_second_small: float32 [3, 3], replicated
- low_weight1: bfloat16 [512, 27], P('chan')
- low_weight2: bfloat16 [512, 512], P(None, 'chan')
- low_weight3: bfloat16 [27, 512], P(None, 'chan')
- new_u1: float32 [512], P('chan')
- new_v1: float32 [27], replicated
- new_u2: float32 [512], replicated
- new_v2: float32 [512], P('chan')
- new_u3: float32 [3], replicated
- new_v3: float32 [9, 512], P(None, 'chan')
Inputs may be any that keep to these rules, and one draw needn't show every extreme that they name: `frame_kinds`: 1: one 64 x 64 image; 2: four 32 x 32 images. `series_len`: slots of kind-1 frames other than slot 0 hold no image.
All inputs are finite; a program needn't handle non-finite values.
Results may differ from a plain program's by a relative error of at most 0.0094.
Values may be sent and summed in bfloat16 or wider, within the bound.
No kernel may reach another device: no remote copies, remote signals or barrier semaphores. Data moves between devices by JAX's collectives and lax.ppermute only.
A program may use at most 192 MiB of HBM per device.

v0:
```python
import jax
import jax.numpy as jnp
from jax import lax
from jax.sharding import PartitionSpec as P

NMAX = 4
STEP = 7


SHRINK = 0.98
LR_RATE = 0.05
BETA_ONE = 0.5
BETA_TWO = 0.55
ADAM_EPS = 1e-08
DECAY = 0.01
CLIP_LIMIT = 1.0
TAP_SHIFTS = ((-1, -1), (-1, 0), (-1, 1), (0, -1), (0, 0), (0, 1), (1, -1), (1, 0), (1, 1))


def precise_dot(left_mat, right_mat):
    return jnp.dot(left_mat, right_mat, precision=lax.Precision.HIGHEST)


def dot_first(left_mat, right_mat):
    return lax.dot_general(
        left_mat, right_mat, (((0,), (0,)), ((), ())), preferred_element_type=jnp.float32
    )


def dot_last(left_mat, right_mat):
    return lax.dot_general(
        left_mat, right_mat, (((1,), (1,)), ((), ())), preferred_element_type=jnp.float32
    )


def lipswish(values):
    return values * jax.nn.sigmoid(values) / 1.1


def swish_slope(values):
    sigm = jax.nn.sigmoid(values)
    return (sigm + values * sigm * (1.0 - sigm)) / 1.1


def swish_curve(values):
    sigm = jax.nn.sigmoid(values)
    return sigm * (1.0 - sigm) * (2.0 + values * (1.0 - 2.0 * sigm)) / 1.1


def make_masks(frame_kinds):
    total_pix = frame_kinds.shape[0] * 4096
    positions = lax.iota(jnp.int32, total_pix)
    kind_pix = jnp.repeat(frame_kinds, 4096)
    whole = kind_pix == 1
    pix_row = positions // 64 % 64
    pix_col = positions % 64
    pix_row = jnp.where(whole, pix_row, pix_row % 32)
    pix_col = jnp.where(whole, pix_col, pix_col % 32)
    limit = jnp.where(whole, 64, 32)
    mask_list = []
    for shift_y, shift_x in TAP_SHIFTS:
        inside = (
            (pix_row + shift_y >= 0)
            & (pix_row + shift_y < limit)
            & (pix_col + shift_x >= 0)
            & (pix_col + shift_x < limit)
        )
        mask_list.append(inside.astype(jnp.float32))
    return jnp.stack(mask_list)


def gather_taps(planes, tap_masks):
    pieces = []
    for tap_index, shift_pair in enumerate(TAP_SHIFTS):
        offset = shift_pair[0] * 64 + shift_pair[1]
        pieces.append(jnp.roll(planes, -offset, axis=1) * tap_masks[tap_index])
    return jnp.stack(pieces, axis=1).reshape(planes.shape[0] * 9, planes.shape[1])


def spread_taps_back(grad_taps, tap_masks):
    shaped = grad_taps.reshape(-1, 9, grad_taps.shape[1])
    result = jnp.zeros((shaped.shape[0], shaped.shape[2]), jnp.float32)
    for tap_index, shift_pair in enumerate(TAP_SHIFTS):
        offset = shift_pair[0] * 64 + shift_pair[1]
        result = result + jnp.roll(shaped[:, tap_index] * tap_masks[tap_index], offset, axis=1)
    return result


def combine_taps(tap_values, tap_masks):
    shaped = tap_values.reshape(-1, 9, tap_values.shape[1])
    result = jnp.zeros((shaped.shape[0], shaped.shape[2]), jnp.float32)
    for tap_index, shift_pair in enumerate(TAP_SHIFTS):
        offset = shift_pair[0] * 64 + shift_pair[1]
        result = result + jnp.roll(shaped[:, tap_index], -offset, axis=1) * tap_masks[tap_index]
    return result


def combine_back(grad_planes, tap_masks):
    pieces = []
    for tap_index, shift_pair in enumerate(TAP_SHIFTS):
        offset = shift_pair[0] * 64 + shift_pair[1]
        pieces.append(jnp.roll(grad_planes * tap_masks[tap_index], offset, axis=1))
    return jnp.stack(pieces, axis=1).reshape(grad_planes.shape[0] * 9, grad_planes.shape[1])


def slot_sum(values, frame_kinds):
    frames = frame_kinds.shape[0]
    quads = values.reshape(frames, 2, 32, 2, 32).sum(axis=(2, 4)).reshape(frames, 4)
    whole = quads.sum(axis=1)
    first_slot = lax.iota(jnp.int32, 4) == 0
    return jnp.where(
        frame_kinds[:, None] == 2, quads, jnp.where(first_slot[None, :], whole[:, None], 0.0)
    )


def slot_spread(slot_values, frame_kinds):
    frames = frame_kinds.shape[0]
    quads = jnp.broadcast_to(slot_values.reshape(frames, 2, 1, 2, 1), (frames, 2, 32, 2, 32))
    whole = jnp.broadcast_to(slot_values[:, 0].reshape(frames, 1, 1, 1, 1), (frames, 2, 32, 2, 32))
    picked = jnp.where(frame_kinds.reshape(frames, 1, 1, 1, 1) == 2, quads, whole)
    return picked.reshape(frames * 4096)


def pixel_counts(frame_kinds):
    first_slot = lax.iota(jnp.int32, 4) == 0
    return jnp.where(
        frame_kinds[:, None] == 2, 1024.0, jnp.where(first_slot[None, :], 4096.0, 0.0)
    ).astype(jnp.float32)


def power_iterate(weight1, weight2, weight3, power_u1, power_u2, power_u3, combine_fn):
    weight_cube = weight3.reshape(3, 9, weight3.shape[1])
    for power_step in range(2):
        part_one = precise_dot(weight1.T, power_u1)
        vec_two = precise_dot(weight2.T, power_u2)
        vec_three = jnp.einsum("otc,o->tc", weight_cube, power_u3, precision=lax.Precision.HIGHEST)
        total_one, square_two, square_three = combine_fn(
            (part_one, jnp.sum(vec_two * vec_two), jnp.sum(vec_three * vec_three))
        )
        vec_one = total_one / jnp.sqrt(jnp.sum(total_one * total_one) + 1e-12)
        vec_two = vec_two / jnp.sqrt(square_two + 1e-12)
        vec_three = vec_three / jnp.sqrt(square_three + 1e-12)
        mapped_one = precise_dot(weight1, vec_one)
        part_two = precise_dot(weight2, vec_two)
        part_three = jnp.einsum(
            "otc,tc->o", weight_cube, vec_three, precision=lax.Precision.HIGHEST
        )
        square_one, total_two, total_three = combine_fn(
            (jnp.sum(mapped_one * mapped_one), part_two, part_three)
        )
        square_two = jnp.sum(total_two * total_two)
        square_three = jnp.sum(total_three * total_three)
        power_u1 = mapped_one / jnp.sqrt(square_one + 1e-12)
        power_u2 = total_two / jnp.sqrt(square_two + 1e-12)
        power_u3 = total_three / jnp.sqrt(square_three + 1e-12)
    spectra = (jnp.sqrt(square_one), jnp.sqrt(square_two), jnp.sqrt(square_three))
    return (power_u1, vec_one, power_u2, vec_two, power_u3, vec_three, spectra)


def run_block(
    mix_fwd,
    mix_back,
    out_fwd,
    in_back,
    take,
    w1_low,
    w3_low,
    bias_local,
    normed,
    taps_full,
    tap_masks,
    probes,
    adjoint_seeds,
    coef_pixels,
    cot_z,
):
    slope_zero = swish_slope(normed)
    curve_zero = swish_curve(normed)
    taps_own = take(taps_full)
    act_one = jnp.dot(w1_low, taps_own, preferred_element_type=jnp.float32) + bias_local[0][:, None]
    slope_one = swish_slope(act_one)
    curve_one = swish_curve(act_one)
    hidden_one = lipswish(act_one).astype(jnp.bfloat16)
    act_two = mix_fwd(hidden_one) + bias_local[1][:, None]
    slope_two = swish_slope(act_two)
    curve_two = swish_curve(act_two)
    hidden_two = lipswish(act_two).astype(jnp.bfloat16)
    branch = out_fwd(jnp.dot(w3_low, hidden_two, preferred_element_type=jnp.float32))
    z_part = normed + combine_taps(branch, tap_masks)
    current = probes
    density = jnp.zeros((probes.shape[1],), jnp.float32)
    saved_steps = []
    for series_step in range(len(adjoint_seeds)):
        tan_taps = take(gather_taps(slope_zero * current, tap_masks).astype(jnp.bfloat16))
        lin_one = jnp.dot(w1_low, tan_taps, preferred_element_type=jnp.float32)
        tan_one = (slope_one * lin_one).astype(jnp.bfloat16)
        lin_two = mix_fwd(tan_one)
        tan_two = (slope_two * lin_two).astype(jnp.bfloat16)
        following = combine_taps(
            out_fwd(jnp.dot(w3_low, tan_two, preferred_element_type=jnp.float32)), tap_masks
        )
        saved_steps.append((current, tan_taps, lin_one, tan_one, lin_two, tan_two))
        density = density + coef_pixels[series_step] * jnp.sum(probes * following, axis=0)
        current = following
    grad_a1 = jnp.zeros_like(act_one)
    grad_a2 = jnp.zeros_like(act_two)
    grad_h = jnp.zeros_like(normed)
    grad_w1 = jnp.zeros(w1_low.shape, jnp.float32)
    grad_w3 = jnp.zeros(w3_low.shape, jnp.float32)
    w2_terms = []
    adjoint = adjoint_seeds[-1]
    for series_step in reversed(range(len(adjoint_seeds))):
        earlier, tan_taps, lin_one, tan_one, lin_two, tan_two = saved_steps[series_step]
        grad_e3 = take(combine_back(adjoint, tap_masks)).astype(jnp.bfloat16)
        grad_t2 = dot_first(w3_low, grad_e3)
        grad_w3 = grad_w3 + dot_last(grad_e3, tan_two)
        grad_e2 = (slope_two * grad_t2).astype(jnp.bfloat16)
        grad_a2 = grad_a2 + grad_t2 * lin_two * curve_two
        grad_t1, part_w2 = mix_back(grad_e2, tan_one)
        w2_terms.append(part_w2)
        grad_e1 = (slope_one * grad_t1).astype(jnp.bfloat16)
        grad_a1 = grad_a1 + grad_t1 * lin_one * curve_one
        grad_taps = in_back(dot_first(w1_low, grad_e1))
        grad_w1 = grad_w1 + dot_last(grad_e1, tan_taps)
        grad_t0 = spread_taps_back(grad_taps, tap_masks)
        grad_h = grad_h + grad_t0 * earlier * curve_zero
        if series_step > 0:
            adjoint = adjoint_seeds[series_step - 1] + slope_zero * grad_t0
    grad_q = take(combine_back(cot_z, tap_masks)).astype(jnp.bfloat16)
    grad_s2 = dot_first(w3_low, grad_q)
    grad_w3 = grad_w3 + dot_last(grad_q, hidden_two)
    grad_a2 = grad_a2 + slope_two * grad_s2
    low_a2 = grad_a2.astype(jnp.bfloat16)
    grad_s1, part_w2 = mix_back(low_a2, hidden_one)
    w2_terms.append(part_w2)
    grad_a1 = grad_a1 + slope_one * grad_s1
    low_a1 = grad_a1.astype(jnp.bfloat16)
    grad_taps = in_back(dot_first(w1_low, low_a1))
    grad_w1 = grad_w1 + dot_last(low_a1, taps_own)
    grad_h = grad_h + cot_z + slope_zero * spread_taps_back(grad_taps, tap_masks)
    grad_w2 = w2_terms[0]
    for extra_term in w2_terms[1:]:
        grad_w2 = grad_w2 + extra_term
    grad_bias = jnp.stack([jnp.sum(grad_a1, axis=1), jnp.sum(grad_a2, axis=1)])
    return (z_part, density, grad_h, grad_w1, grad_w2, grad_w3, grad_bias)


def outer_list(vec_u1, vec_v1, vec_u2, vec_v2, vec_u3, vec_v3):
    outer_one = vec_u1[:, None] * vec_v1[None, :]
    outer_two = vec_u2[:, None] * vec_v2[None, :]
    outer_three = (vec_u3[:, None, None] * vec_v3[None, :, :]).reshape(27, vec_v3.shape[1])
    return (outer_one, outer_two, outer_three)


def moment_step(grad, moment, second):
    new_moment = BETA_ONE * moment + (1.0 - BETA_ONE) * grad
    new_second = BETA_TWO * second + (1.0 - BETA_TWO) * grad * grad
    return (new_moment, new_second)


def adam_step(param, grad, moment, second):
    new_moment, new_second = moment_step(grad, moment, second)
    fix_one = 1.0 - BETA_ONE**STEP
    fix_two = 1.0 - BETA_TWO**STEP
    update = new_moment / fix_one / (jnp.sqrt(new_second / fix_two) + ADAM_EPS) + DECAY * param
    return (param - LR_RATE * update, new_moment, new_second)


def local(
    images,
    frame_kinds,
    series_len,
    probes,
    cot_z,
    cot_logdet,
    weight1,
    weight2,
    weight3,
    biases,
    small_params,
    power_u1,
    power_u2,
    power_u3,
    moment_w1,
    second_w1,
    moment_w2,
    second_w2,
    moment_w3,
    second_w3,
    moment_bias,
    second_bias,
    moment_small,
    second_small,
):
    tap_masks = make_masks(frame_kinds)
    counts = pixel_counts(frame_kinds)
    act_scale = jnp.exp(small_params[1])[:, None]
    normed = (images + small_params[0][:, None]) * act_scale
    taps_full = gather_taps(lipswish(normed), tap_masks).astype(jnp.bfloat16)
    adjoint_seeds = []
    coef_pixels = []
    for series_step in range(NMAX):
        term_sign = (-1.0) ** series_step / (series_step + 1)
        slot_coef = jnp.where(series_len >= series_step + 1, term_sign, 0.0).astype(jnp.float32)
        coef_pixels.append(slot_spread(slot_coef, frame_kinds))
        adjoint_seeds.append(slot_spread(slot_coef * cot_logdet, frame_kinds)[None, :] * probes)
    rows_own = weight1.shape[0]
    cols_own = weight2.shape[1]
    total_pix = images.shape[1]
    full_one, full_two, full_three, full_bias, full_u1 = (
        lax.all_gather(weight1, "chan", axis=0, tiled=True),
        lax.all_gather(weight2, "chan", axis=1, tiled=True),
        lax.all_gather(weight3, "chan", axis=1, tiled=True),
        lax.all_gather(biases, "chan", axis=1, tiled=True),
        lax.all_gather(power_u1, "chan", axis=0, tiled=True),
    )

    def identity_sum(partials):
        return partials

    vec_u1, vec_v1, vec_u2, vec_v2, vec_u3, vec_v3, spectra = power_iterate(
        full_one, full_two, full_three, full_u1, power_u2, power_u3, identity_sum
    )
    w1_low = (SHRINK * full_one / spectra[0]).astype(jnp.bfloat16)
    w2_low = (SHRINK * full_two / spectra[1]).astype(jnp.bfloat16)
    w3_low = (SHRINK * full_three / spectra[2]).astype(jnp.bfloat16)
    chan_index = lax.axis_index("chan")
    own_width = total_pix // lax.axis_size("chan")

    def take(values):
        return lax.dynamic_slice_in_dim(values, chan_index * own_width, own_width, 1)

    def mix_fwd(hidden):
        return jnp.dot(w2_low, hidden, preferred_element_type=jnp.float32)

    def mix_back(grad_rows, kept_rows):
        return (dot_first(w2_low, grad_rows), dot_last(grad_rows, kept_rows))

    def out_fwd(partial_value):
        return lax.all_gather(partial_value, "chan", axis=1, tiled=True)

    def in_back(partial_value):
        return lax.all_gather(partial_value, "chan", axis=1, tiled=True)

    z_part, density, grad_h, grad_w1, grad_w2, grad_w3, grad_bias = run_block(
        mix_fwd,
        mix_back,
        out_fwd,
        in_back,
        take,
        w1_low,
        w3_low,
        full_bias,
        normed,
        taps_full,
        tap_masks,
        probes,
        adjoint_seeds,
        coef_pixels,
        cot_z,
    )
    lead = jnp.where(chan_index == 0, 1.0, 0.0)
    grad_small = jnp.stack(
        [
            jnp.sum(take(grad_h * act_scale), axis=1),
            jnp.sum(take(grad_h * normed), axis=1) + lead * jnp.sum(counts * cot_logdet),
            jnp.sum(take(cot_z), axis=1),
        ]
    )
    out_u1 = lax.dynamic_slice_in_dim(vec_u1, chan_index * rows_own, rows_own, 0)
    out_v2 = lax.dynamic_slice_in_dim(vec_v2, chan_index * cols_own, cols_own, 0)
    out_v3 = lax.dynamic_slice_in_dim(vec_v3, chan_index * cols_own, cols_own, 1)
    grad_w1, grad_w2, grad_w3, grad_bias, grad_small = lax.psum(
        (grad_w1, grad_w2, grad_w3, grad_bias, grad_small), ("dp", "chan")
    )
    outers = outer_list(vec_u1, vec_v1, vec_u2, vec_v2, vec_u3, vec_v3)
    weights_full = (full_one, full_two, full_three)
    grads_raw = (grad_w1, grad_w2, grad_w3)
    corrected = []
    square = jnp.sum(grad_bias * grad_bias) + jnp.sum(grad_small * grad_small)
    for slot_number in range(3):
        inner_value = jnp.sum(grads_raw[slot_number] * weights_full[slot_number])
        spec_value = spectra[slot_number]
        fixed = (
            SHRINK / spec_value * grads_raw[slot_number]
            - SHRINK * inner_value / (spec_value * spec_value) * outers[slot_number]
        )
        corrected.append(fixed)
        square = square + jnp.sum(fixed * fixed)
    grad_norm = jnp.sqrt(square)
    grad_one = lax.dynamic_slice_in_dim(corrected[0], chan_index * rows_own, rows_own, 0)
    grad_two = lax.dynamic_slice_in_dim(corrected[1], chan_index * cols_own, cols_own, 1)
    grad_three = lax.dynamic_slice_in_dim(corrected[2], chan_index * cols_own, cols_own, 1)
    grad_bias = lax.dynamic_slice_in_dim(grad_bias, chan_index * cols_own, cols_own, 1)
    z_out = z_part + small_params[2][:, None]
    logdet = slot_sum(density, frame_kinds) + counts * jnp.sum(small_params[1])
    grad_input = grad_h * act_scale
    factor = jnp.minimum(1.0, CLIP_LIMIT / (grad_norm + 1e-06))
    new_weight1, new_moment1, new_second1 = adam_step(
        weight1, factor * grad_one, moment_w1, second_w1
    )
    new_weight2, new_moment2, new_second2 = adam_step(
        weight2, factor * grad_two, moment_w2, second_w2
    )
    new_weight3, new_moment3, new_second3 = adam_step(
        weight3, factor * grad_three, moment_w3, second_w3
    )
    clipped_bias = factor * grad_bias
    new_moment_bias, new_second_bias = moment_step(clipped_bias, moment_bias, second_bias)
    new_small, new_moment_small, new_second_small = adam_step(
        small_params, factor * grad_small, moment_small, second_small
    )
    return (
        z_out,
        logdet,
        grad_input,
        grad_norm,
        new_weight1,
        new_moment1,
        new_second1,
        new_weight2,
        new_moment2,
        new_second2,
        new_weight3,
        new_moment3,
        new_second3,
        clipped_bias,
        new_moment_bias,
        new_second_bias,
        new_small,
        new_moment_small,
        new_second_small,
        new_weight1.astype(jnp.bfloat16),
        new_weight2.astype(jnp.bfloat16),
        new_weight3.astype(jnp.bfloat16),
        out_u1,
        vec_v1,
        vec_u2,
        out_v2,
        vec_u3,
        out_v3,
    )


def solution(mesh):
    return jax.shard_map(
        local,
        mesh=mesh,
        in_specs=(
            P(None, "dp"),
            P("dp"),
            P("dp", None),
            P(None, "dp"),
            P(None, "dp"),
            P("dp", None),
            P("chan", None),
            P(None, "chan"),
            P(None, "chan"),
            P(None, "chan"),
            P(),
            P("chan"),
            P(),
            P(),
            P("chan", None),
            P("chan", None),
            P(None, "chan"),
            P(None, "chan"),
            P(None, "chan"),
            P(None, "chan"),
            P(None, "chan"),
            P(None, "chan"),
            P(),
            P(),
        ),
        out_specs=(
            P(None, "dp"),
            P("dp", None),
            P(None, "dp"),
            P(),
            P("chan", None),
            P("chan", None),
            P("chan", None),
            P(None, "chan"),
            P(None, "chan"),
            P(None, "chan"),
            P(None, "chan"),
            P(None, "chan"),
            P(None, "chan"),
            P(None, "chan"),
            P(None, "chan"),
            P(None, "chan"),
            P(),
            P(),
            P(),
            P("chan", None),
            P(None, "chan"),
            P(None, "chan"),
            P("chan"),
            P(),
            P(),
            P("chan"),
            P(),
            P(None, "chan"),
        ),
        check_vma=False,
    )
```

profile of v0, /device:TPU:0, one launch (start us, length us, event | category | flops | bytes accessed | tf_op | source)
XLA Modules:
  0.0 779.1 jit_solution(9850526386530663048)
XLA Ops:
  29.1 15.1 %all-reduce = f32[512]{0:T(512)S(1)} all-reduce(f32[512]{0:T(512)S(1)} %dynamic-update-slice), channel_id=1, replica_groups=mesh['dp'=4,'chan'=8] {'chan'}, use_global_device_ids=true, to_apply=%add | all-reduce | flops 512 | bytes 4096
  44.2 8.2 %all-gather = f32[8,64,27]{1,2,0:T(8,128)S(1)} all-gather(f32[1,64,27]{1,2,0:T(8,128)S(1)} %bitcast.1058), channel_id=1, replica_groups=mesh['dp'=4,'chan'=8] {'chan'}, dimensions={0}, use_global_device_ids=true | all-gather | bytes 62208 | tf_op jit(solution)/shard_map/all_gather | solution.py:313
  59.9 9.2 %all-gather.1 = f32[8,64,27]{1,2,0:T(8,128)S(1)} all-gather(f32[1,64,27]{1,2,0:T(8,128)S(1)} %bitcast.1059), channel_id=1, replica_groups=mesh['dp'=4,'chan'=8] {'chan'}, dimensions={0}, use_global_device_ids=true | all-gather | bytes 62208 | tf_op jit(solution)/shard_map/all_gather | solution.py:311
  85.9 8.2 %all-gather.2 = f32[8,64,2]{1,2,0:T(2,128)S(1)} all-gather(f32[1,64,2]{1,2,0:T(2,128)S(1)} %bitcast.1093), channel_id=1, replica_groups=mesh['dp'=4,'chan'=8] {'chan'}, dimensions={0}, use_global_device_ids=true | all-gather | bytes 4608 | tf_op jit(solution)/shard_map/all_gather | solution.py:314
  114.7 2.7 fusion.224
  117.4 2.3 fusion.14
  130.2 3.8 multiply_convert_fusion.7
  134.1 2.4 multiply_convert_fusion.6
  137.8 12.6 %all_gather.55 = f32[27,8192]{1,0:T(8,128)} all-gather(f32[27,1024]{1,0:T(8,128)S(1)} %fusion.351), channel_id=1, replica_groups=mesh['dp'=4,'chan'=8] {'chan'}, dimensions={1}, use_global_device_ids=true | all-gather | bytes 995328 | tf_op jit(solution)/shard_map/all_gather | solution.py:343
  150.4 2.5 reshape.2329
  152.9 4.6 fusion.334
  166.3 2.8 multiply_convert_fusion.5
  169.1 2.4 multiply_convert_fusion.4
  172.8 12.6 %all_gather.56 = f32[27,8192]{1,0:T(8,128)} all-gather(f32[27,1024]{1,0:T(8,128)S(1)} %fusion.352), channel_id=1, replica_groups=mesh['dp'=4,'chan'=8] {'chan'}, dimensions={1}, use_global_device_ids=true | all-gather | bytes 995328 | tf_op jit(solution)/shard_map/all_gather | solution.py:343
  185.3 2.5 reshape.2331
  187.9 4.6 fusion.333
  201.3 2.8 multiply_convert_fusion.3
  204.1 2.8 multiply_convert_fusion.2
  208.2 12.0 %all_gather.57 = f32[27,8192]{1,0:T(8,128)} all-gather(f32[27,1024]{1,0:T(8,128)S(1)} %fusion.353), channel_id=1, replica_groups=mesh['dp'=4,'chan'=8] {'chan'}, dimensions={1}, use_global_device_ids=true | all-gather | bytes 995328 | tf_op jit(solution)/shard_map/all_gather | solution.py:343
  220.1 2.5 reshape.2333
  222.6 5.1 fusion.332
  238.6 3.2 multiply_convert_fusion.1
  243.1 12.0 %all_gather.51 = f32[27,8192]{1,0:T(8,128)} all-gather(f32[27,1024]{1,0:T(8,128)S(1)} %fusion.347), channel_id=1, replica_groups=mesh['dp'=4,'chan'=8] {'chan'}, dimensions={1}, use_global_device_ids=true | all-gather | bytes 995328 | tf_op jit(solution)/shard_map/all_gather | solution.py:340
  255.1 2.6 reshape.2323
  257.6 5.4 fusion.338
  272.4 5.3 multiply_convert_fusion
  281.0 12.0 %all_gather.52 = f32[27,8192]{1,0:T(8,128)} all-gather(f32[27,1024]{1,0:T(8,128)S(1)} %fusion.348), channel_id=1, replica_groups=mesh['dp'=4,'chan'=8] {'chan'}, dimensions={1}, use_global_device_ids=true | all-gather | bytes 995328 | tf_op jit(solution)/shard_map/all_gather | solution.py:340
  293.1 2.5 reshape.2324
  295.6 4.9 fusion.337
  308.4 3.9 multiply_convert_fusion.11
  315.7 12.3 %all_gather.53 = f32[27,8192]{1,0:T(8,128)} all-gather(f32[27,1024]{1,0:T(8,128)S(1)} %fusion.349), channel_id=1, replica_groups=mesh['dp'=4,'chan'=8] {'chan'}, dimensions={1}, use_global_device_ids=true | all-gather | bytes 995328 | tf_op jit(solution)/shard_map/all_gather | solution.py:340
  328.0 2.5 reshape.2325
  330.5 5.0 fusion.336
  346.0 4.0 multiply_convert_fusion.9
  356.9 12.0 %all_gather.58 = f32[27,8192]{1,0:T(8,128)} all-gather(f32[27,1024]{1,0:T(8,128)S(1)} %fusion.354), channel_id=1, replica_groups=mesh['dp'=4,'chan'=8] {'chan'}, dimensions={1}, use_global_device_ids=true | all-gather | bytes 995328 | tf_op jit(solution)/shard_map/all_gather | solution.py:343
  368.9 2.5 reshape.2335
  371.4 5.8 fusion.330
  377.2 9.2 %fusion.341 = (f32[512]{0:T(512)}, bf16[512,1024]{1,0:T(8,128)(2,1)S(1)}) fusion(f32[512,1024]{1,0:T(8,128)S(1)} %get-tuple-element.208, bf16[27,512]{1,0:T(8,128)(2,1)} %divide_convert_fusion.2, bf16[27,8192]{1,0:T(8,128)(2,1)} %reshape.2336, s32[]{:T(128)S(6)} %select_n.395, f32[512,1024]{1,0:T(8,128)} %copy-done.102, f32[512]{0:T(512)S(1)} %bitcast.1079, ...), kind=kOutput, calls=%fused_computation.934 | convolution fusion | flops 40893952 | bytes 22122500 | tf_op jit(solution)/shard_map/dot_general | solution.py:25
  389.6 3.2 fusion.342
  393.9 10.8 %all_gather.59 = f32[27,8192]{1,0:T(8,128)S(1)} all-gather(f32[27,1024]{1,0:T(8,128)S(1)} %fusion.17), channel_id=1, replica_groups=mesh['dp'=4,'chan'=8] {'chan'}, dimensions={1}, use_global_device_ids=true | all-gather | bytes 995328 | tf_op jit(solution)/shard_map/all_gather | solution.py:343
  405.9 5.4 fusion.331
  421.7 10.8 %all_gather.54 = f32[27,8192]{1,0:T(8,128)S(1)} all-gather(f32[27,1024]{1,0:T(8,128)S(1)} %copy-done.120), channel_id=1, replica_groups=mesh['dp'=4,'chan'=8] {'chan'}, dimensions={1}, use_global_device_ids=true | all-gather | bytes 995328 | tf_op jit(solution)/shard_map/all_gather | solution.py:340
  433.8 5.4 fusion.335
  445.3 12.0 %all_gather.50 = f32[27,8192]{1,0:T(8,128)} all-gather(f32[27,1024]{1,0:T(8,128)S(1)} %fusion.345), channel_id=1, replica_groups=mesh['dp'=4,'chan'=8] {'chan'}, dimensions={1}, use_global_device_ids=true | all-gather | bytes 995328 | tf_op jit(solution)/shard_map/all_gather | solution.py:340
  457.4 2.5 reshape.2322
  459.9 5.4 fusion.339
  504.8 118.3 %all-reduce.7.cloned.1.call-done = (f32[2,512]{1,0:T(2,128)}, f32[3,3]{1,0:T(4,128)}, f32[512,27]{0,1:T(8,128)}, f32[27,512]{1,0:T(8,128)}) async-done(((f32[2,512]{1,0:T(2,128)}, f32[3,3]{1,0:T(4,128)}, f32[512,27]{0,1:T(8,128)}, f32[27,512]{1,0:T(8,128)}), (f32[2,512]{1,0:T(2,128)}, f32[3,3]{1,0:T(4,128)}, f32[512,27]{0,1:T(8,128)}, f32[27,512]{1,0:T(8,128)})) %all-reduce.7.cloned.1.call-update) | async-done | bytes 114740 | tf_op jit(solution)/shard_map/psum | solution.py:373
  635.2 125.8 %all-reduce.5.cloned.1.call-done = f32[512,512]{0,1:T(8,128)} async-done(((f32[512,512]{0,1:T(8,128)}), f32[512,512]{0,1:T(8,128)}) %all-reduce.5.cloned.1.call-update) | async-done | bytes 1048592 | tf_op jit(solution)/shard_map/psum | solution.py:373
  (1076 shorter events, 216.2 us)
Async XLA Ops:
  7.2 110.2 %copy-start = (f32[512]{0:T(512)S(1)}, f32[512]{0:T(512)}, u32[]{:S(2)}) copy-start(f32[512]{0:T(512)} %param.36) | copy-start | bytes 6148
  7.2 110.2 %all-gather.5.cloned.1.call-start = ((), (), s32[]{:S(2)}) async-start(), calls=%async_computation | async-start | bytes 1179648 | tf_op jit(solution)/shard_map/all_gather | solution.py:312
  8.0 615.2 %all-reduce.7.cloned.1.call-start = ((), (), s32[]{:S(2)}) async-start(), calls=%async_computation.2 | async-start | bytes 274432 | tf_op jit(solution)/shard_map/psum | solution.py:373
  24.8 19.4 %copy-start.195 = (f32[27,64]{1,0:T(8,128)S(1)}, f32[27,64]{1,0:T(8,128)}, u32[]{:S(2)}) copy-start(f32[27,64]{1,0:T(8,128)} %param.32) | copy-start | bytes 20740
  25.0 58.9 %copy-start.12 = (f32[8192]{0:T(1024)}, f32[8192]{0:T(1024)S(1)}, u32[]{:S(2)}) copy-start(f32[8192]{0:T(1024)S(1)} %get-tuple-element.497) | copy-start | bytes 98308
  25.0 53.7 %copy-start.28 = (f32[8192]{0:T(1024)}, f32[8192]{0:T(1024)S(1)}, u32[]{:S(2)}) copy-start(f32[8192]{0:T(1024)S(1)} %get-tuple-element.493) | copy-start | bytes 98308
  25.0 59.0 %copy-start.20 = (f32[8192]{0:T(1024)}, f32[8192]{0:T(1024)S(1)}, u32[]{:S(2)}) copy-start(f32[8192]{0:T(1024)S(1)} %get-tuple-element.492) | copy-start | bytes 98308
  25.0 27.6 %copy-start.244 = (f32[3]{0:T(128)S(1)}, f32[3]{0:T(128)}, u32[]{:S(2)}) copy-start(f32[3]{0:T(128)} %param.37) | copy-start | bytes 40
  26.1 33.8 %copy-start.197 = (f32[64,27]{0,1:T(8,128)S(1)}, f32[64,27]{0,1:T(8,128)}, u32[]{:S(2)}) copy-start(f32[64,27]{0,1:T(8,128)} %param.30) | copy-start | bytes 20740
  26.1 51.3 %copy-start.44 = (f32[8192]{0:T(1024)}, f32[8192]{0:T(1024)S(1)}, u32[]{:S(2)}) copy-start(f32[8192]{0:T(1024)S(1)} %get-tuple-element.496) | copy-start | bytes 98308
  26.1 55.2 %copy-start.36 = (f32[8192]{0:T(1024)}, f32[8192]{0:T(1024)S(1)}, u32[]{:S(2)}) copy-start(f32[8192]{0:T(1024)S(1)} %get-tuple-element.495) | copy-start | bytes 98308
  26.5 49.7 %copy-start.167 = (bf16[3,8192]{1,0:T(4,128)(2,1)}, bf16[3,8192]{1,0:T(4,128)(2,1)S(1)}, u32[]{:S(2)}) copy-start(bf16[3,8192]{1,0:T(4,128)(2,1)S(1)} %get-tuple-element.348) | copy-start | bytes 147460
  26.5 49.7 %copy-start.169 = (bf16[3,8192]{1,0:T(4,128)(2,1)}, bf16[3,8192]{1,0:T(4,128)(2,1)S(1)}, u32[]{:S(2)}) copy-start(bf16[3,8192]{1,0:T(4,128)(2,1)S(1)} %get-tuple-element.344) | copy-start | bytes 147460
  26.6 49.7 %copy-start.171 = (bf16[3,8192]{1,0:T(4,128)(2,1)}, bf16[3,8192]{1,0:T(4,128)(2,1)S(1)}, u32[]{:S(2)}) copy-start(bf16[3,8192]{1,0:T(4,128)(2,1)S(1)} %get-tuple-element.345) | copy-start | bytes 147460
  26.6 49.7 %copy-start.173 = (bf16[3,8192]{1,0:T(4,128)(2,1)}, bf16[3,8192]{1,0:T(4,128)(2,1)S(1)}, u32[]{:S(2)}) copy-start(bf16[3,8192]{1,0:T(4,128)(2,1)S(1)} %get-tuple-element.346) | copy-start | bytes 147460
  26.6 49.7 %copy-start.175 = (bf16[3,8192]{1,0:T(4,128)(2,1)}, bf16[3,8192]{1,0:T(4,128)(2,1)S(1)}, u32[]{:S(2)}) copy-start(bf16[3,8192]{1,0:T(4,128)(2,1)S(1)} %get-tuple-element.337) | copy-start | bytes 147460
  26.6 49.7 %copy-start.177 = (bf16[3,8192]{1,0:T(4,128)(2,1)}, bf16[3,8192]{1,0:T(4,128)(2,1)S(1)}, u32[]{:S(2)}) copy-start(bf16[3,8192]{1,0:T(4,128)(2,1)S(1)} %get-tuple-element.338) | copy-start | bytes 147460
  26.6 49.8 %copy-start.179 = (bf16[3,8192]{1,0:T(4,128)(2,1)}, bf16[3,8192]{1,0:T(4,128)(2,1)S(1)}, u32[]{:S(2)}) copy-start(bf16[3,8192]{1,0:T(4,128)(2,1)S(1)} %get-tuple-element.339) | copy-start | bytes 147460
  26.6 49.8 %copy-start.181 = (bf16[3,8192]{1,0:T(4,128)(2,1)}, bf16[3,8192]{1,0:T(4,128)(2,1)S(1)}, u32[]{:S(2)}) copy-start(bf16[3,8192]{1,0:T(4,128)(2,1)S(1)} %get-tuple-element.340) | copy-start | bytes 147460
  52.6 60.1 %copy-start.111 = (f32[512,27]{0,1:T(8,128)}, f32[512,27]{0,1:T(8,128)S(1)}, u32[]{:S(2)}) copy-start(f32[512,27]{0,1:T(8,128)S(1)} %reshape.2342) | copy-start | bytes 165892
  69.2 44.1 %copy-start.84 = (f32[512,27]{0,1:T(8,128)}, f32[512,27]{0,1:T(8,128)S(1)}, u32[]{:S(2)}) copy-start(f32[512,27]{0,1:T(8,128)S(1)} %reshape.2344) | copy-start | bytes 165892
  80.1 14.0 %copy-start.203 = (f32[2,4]{1,0:T(2,128)S(1)}, f32[2,4]{1,0:T(2,128)}, u32[]{:S(2)}) copy-start(f32[2,4]{1,0:T(2,128)} %get-tuple-element.514) | copy-start | bytes 100
  83.2 19.0 %copy-start.115 = (bf16[3,9,8192]{2,0,1:T(4,128)(2,1)}, bf16[3,9,8192]{2,0,1:T(4,128)(2,1)S(1)}, u32[]{:S(2)}) copy-start(bf16[3,9,8192]{2,0,1:T(4,128)(2,1)S(1)} %constant_dynamic-update-slice_fusion.81) | copy-start | bytes 1327108
  84.4 17.9 %copy-start.245 = (f32[3]{0:T(128)}, f32[3]{0:T(128)S(1)}, u32[]{:S(2)}) copy-start(f32[3]{0:T(128)S(1)} %broadcast_divide_fusion.6) | copy-start | bytes 40
  112.7 273.7 %copy-start.232 = (f32[1,512]{1,0:T(1,128)}, f32[1,512]{1,0:T(1,128)S(1)}, u32[]{:S(2)}) copy-start(f32[1,512]{1,0:T(1,128)S(1)} %get-tuple-element.502) | copy-start | bytes 6148
  114.6 14.5 %copy-start.92 = (f32[512,1024]{1,0:T(8,128)}, f32[512,1024]{1,0:T(8,128)S(1)}, u32[]{:S(2)}) copy-start(f32[512,1024]{1,0:T(8,128)S(1)} %fusion.227) | copy-start | bytes 6291460
  405.9 12.9 %copy-start.35 = (f32[8192]{0:T(1024)S(1)}, f32[8192]{0:T(1024)}, u32[]{:S(2)}) copy-start(f32[8192]{0:T(1024)} %copy-done.28) | copy-start | bytes 98308
  405.9 12.9 %copy-start.161 = (f32[3,1,8192]{2,1,0:T(1,128)S(1)}, f32[3,1,8192]{2,1,0:T(1,128)}, u32[]{:S(2)}) copy-start(f32[3,1,8192]{2,1,0:T(1,128)} %get-tuple-element.245) | copy-start | bytes 294916
  501.2 259.8 %all-reduce.5.cloned.1.call-start = ((), (), s32[]{:S(2)}) async-start(), calls=%async_computation.1 | async-start | bytes 2097152 | tf_op jit(solution)/shard_map/psum | solution.py:373
  501.5 262.4 %copy-start.219 = (f32[512]{0:T(512)}, f32[512]{0:T(512)S(1)}, u32[]{:S(2)}) copy-start(f32[512]{0:T(512)S(1)} %broadcast_divide_fusion) | copy-start | bytes 6148
  502.9 120.3 %copy-start.112 = (f32[512,27]{0,1:T(8,128)S(1)}, f32[512,27]{0,1:T(8,128)}, u32[]{:S(2)}) copy-start(f32[512,27]{0,1:T(8,128)} %copy-done.111) | copy-start | bytes 165892
  503.0 122.3 %copy-start.85 = (f32[512,27]{0,1:T(8,128)S(1)}, f32[512,27]{0,1:T(8,128)}, u32[]{:S(2)}) copy-start(f32[512,27]{0,1:T(8,128)} %copy-done.84) | copy-start | bytes 165892
  503.0 128.3 %copy-start.204 = (f32[512]{0:T(512)S(1)}, f32[512]{0:T(512)}, u32[]{:S(2)}) copy-start(f32[512]{0:T(512)} %broadcast_divide_fusion.1) | copy-start | bytes 6148
  503.0 128.3 %copy-start.229 = (f32[27]{0:T(128)S(1)}, f32[27]{0:T(128)}, u32[]{:S(2)}) copy-start(f32[27]{0:T(128)} %copy-done.228) | copy-start | bytes 328
  503.1 130.4 %copy-start.185 = (f32[27,512]{1,0:T(8,128)S(1)}, f32[27,512]{1,0:T(8,128)}, u32[]{:S(2)}) copy-start(f32[27,512]{1,0:T(8,128)} %mul.2424) | copy-start | bytes 165892
  503.1 130.4 %copy-start.230 = (f32[27]{0:T(128)S(1)}, f32[27]{0:T(128)}, u32[]{:S(2)}) copy-start(f32[27]{0:T(128)} %mul.2421) | copy-start | bytes 328
  635.1 131.3 %copy-start.242 = (f32[2,64]{1,0:T(2,128)S(1)}, f32[2,64]{1,0:T(2,128)}, u32[]{:S(2)}) copy-start(f32[2,64]{1,0:T(2,128)} %param.45) | copy-start | bytes 1540
  635.1 132.5 %copy-start.243 = (f32[2,64]{1,0:T(2,128)S(1)}, f32[2,64]{1,0:T(2,128)}, u32[]{:S(2)}) copy-start(f32[2,64]{1,0:T(2,128)} %param.44) | copy-start | bytes 1540
  635.1 133.1 %copy-start.218 = (f32[3,3]{1,0:T(4,128)S(1)}, f32[3,3]{1,0:T(4,128)}, u32[]{:S(2)}) copy-start(f32[3,3]{1,0:T(4,128)} %get-tuple-element.174) | copy-start | bytes 112
  635.1 133.1 %copy-start.221 = (f32[3,3]{1,0:T(4,128)S(1)}, f32[3,3]{1,0:T(4,128)}, u32[]{:S(2)}) copy-start(f32[3,3]{1,0:T(4,128)} %param.34) | copy-start | bytes 112
  635.1 133.1 %copy-start.235 = (f32[3,3]{1,0:T(4,128)S(1)}, f32[3,3]{1,0:T(4,128)}, u32[]{:S(2)}) copy-start(f32[3,3]{1,0:T(4,128)} %param.46) | copy-start | bytes 112
  635.1 133.1 %copy-start.236 = (f32[3,3]{1,0:T(4,128)S(1)}, f32[3,3]{1,0:T(4,128)}, u32[]{:S(2)}) copy-start(f32[3,3]{1,0:T(4,128)} %param.47) | copy-start | bytes 112
  635.1 133.7 %copy-start.121 = (f32[512,64]{0,1:T(8,128)S(1)}, f32[512,64]{0,1:T(8,128)}, u32[]{:S(2)}) copy-start(f32[512,64]{0,1:T(8,128)} %param.31) | copy-start | bytes 393220
  635.1 133.7 %copy-start.193 = (f32[512,64]{0,1:T(8,128)S(1)}, f32[512,64]{0,1:T(8,128)}, u32[]{:S(2)}) copy-start(f32[512,64]{0,1:T(8,128)} %param.40) | copy-start | bytes 393220
  635.1 133.7 %copy-start.194 = (f32[512,64]{0,1:T(8,128)S(1)}, f32[512,64]{0,1:T(8,128)}, u32[]{:S(2)}) copy-start(f32[512,64]{0,1:T(8,128)} %param.41) | copy-start | bytes 393220
  635.2 134.5 %copy-start.196 = (f32[27,64]{1,0:T(8,128)S(1)}, f32[27,64]{1,0:T(8,128)}, u32[]{:S(2)}) copy-start(f32[27,64]{1,0:T(8,128)} %param.32) | copy-start | bytes 20740
  635.2 134.5 %copy-start.199 = (f32[27,64]{1,0:T(8,128)S(1)}, f32[27,64]{1,0:T(8,128)}, u32[]{:S(2)}) copy-start(f32[27,64]{1,0:T(8,128)} %param.42) | copy-start | bytes 20740
  635.2 134.5 %copy-start.200 = (f32[27,64]{1,0:T(8,128)S(1)}, f32[27,64]{1,0:T(8,128)}, u32[]{:S(2)}) copy-start(f32[27,64]{1,0:T(8,128)} %param.43) | copy-start | bytes 20740
  (215 other events, 1119.9 us)
Sparse Core Ops, SparseCore 0:
  9.9 26.2 all-gather.4
  501.3 121.7 all-reduce.6
  628.3 132.6 all-reduce.4
where the time goes:
time: 788 us; the launch traced here: 779 us
  waiting for transfers between devices  245 us (31%)
  local copies, waits for them, and re-layouts  171 us (22%)
  blocking collectives  160 us (20%)
  matrix products  99.6 us (13%)
  other arithmetic  67.4 us (9%)
  between operations  36.5 us (5%)
    psum x2, waiting for transfers between devices, local(): lax.psum((grad_w1, grad_w2, grad_w3, grad_bias, grad_small), ('dp', 'chan'))  244 us
    all_gather x5, blocking collectives, in_back(): return lax.all_gather(partial_value, 'chan', axis=1, tiled=True)  59.9 us
    all_gather x5, blocking collectives, out_fwd(): return lax.all_gather(partial_value, 'chan', axis=1, tiled=True)  59.2 us
    dot_general x15, matrix products, dot_first(): lax.dot_general(left_mat, right_mat, (((0,), (0,)), ((), ())), preferred_...  39.3 us
    slice x5, local copies, waits for them, and re-layouts, combine_taps(): shaped[:, tap_index]  26.1 us
    slice x5, local copies, waits for them, and re-layouts, spread_taps_back(): shaped[:, tap_index] * tap_masks[tap_index]  25.5 us
    dot_general x15, matrix products, dot_last(): lax.dot_general(left_mat, right_mat, (((1,), (1,)), ((), ())), preferred_...  24.8 us
    unnamed x566, local copies, waits for them, and re-layouts  16.1 us
  transfers between devices with their start and end apart: 3, of which 2 were waited for; matrix products, arithmetic and copies ran while one was open for 9% of the time, Pallas kernels for 0%

commit v1 on v0

v1 whole, which is shorter than its diff:
```python
import functools

import jax
import jax.numpy as jnp
from jax import lax
from jax.experimental import pallas as pl
from jax.experimental.pallas import tpu as pltpu
from jax.sharding import PartitionSpec as P

NMAX = 4
STEP = 7
SHRINK = 0.98
LR_RATE = 0.05
BETA_ONE = 0.5
BETA_TWO = 0.55
ADAM_EPS = 1e-08
DECAY = 0.01
CLIP_LIMIT = 1.0

WIDTH = 64
FRAME = 4096
BLOCK = 256
HALO = 2 * NMAX * WIDTH
LANES = 128
TAP_ROWS = 72
F32 = jnp.float32
BF16 = jnp.bfloat16
HIGH = lax.Precision.HIGHEST


def iota(shape, dim):
    return lax.broadcasted_iota(jnp.int32, shape, dim)


def dot_nn(left, right, precision=None):
    return lax.dot_general(
        left, right, (((1,), (0,)), ((), ())), precision=precision, preferred_element_type=F32
    )


def dot_nt(left, right, precision=None):
    return lax.dot_general(
        left, right, (((1,), (1,)), ((), ())), precision=precision, preferred_element_type=F32
    )


def dot_tn(left, right, precision=None):
    return lax.dot_general(
        left, right, (((0,), (0,)), ((), ())), precision=precision, preferred_element_type=F32
    )


def spread_one():
    row = iota((27, LANES), 0)
    return (iota((27, LANES), 1) == (row % 9) * 8 + row // 9).astype(F32)


def spread_three():
    row = iota((27, LANES), 0)
    return (iota((27, LANES), 1) == (8 - row % 9) * 8 + 4 + row // 9).astype(F32)


def lane_is_one(lane):
    return (lane % 8 < 3) & (lane < TAP_ROWS)


def lane_is_three(lane):
    return (lane % 8 >= 4) & (lane % 8 < 7) & (lane < TAP_ROWS)


def pack_kernel(w1_ref, w2_ref, w3_ref, bias_ref, u1_ref, out_ref):
    channels = w2_ref.shape[0]
    out_ref[:, 0:channels] = w2_ref[...].T
    tile = dot_nn(w1_ref[...], spread_one(), HIGH) + dot_tn(w3_ref[...], spread_three(), HIGH)
    lane = iota((1, LANES), 1)
    for index, row in enumerate((u1_ref[...], bias_ref[0:1, :], bias_ref[1:2, :])):
        column = jnp.broadcast_to(row, (8, row.shape[1])).T[:, 0:1]
        tile = jnp.where(lane == TAP_ROWS + index, column, tile)
    out_ref[:, channels:] = tile


def col_taps(state, masks):
    size = state.shape[1]
    row_up, row_down, col_left, col_right = masks
    left = col_left * pltpu.roll(state, 1, 1)
    right = col_right * pltpu.roll(state, size - 1, 1)
    pieces = []
    for shift_y in (-1, 0, 1):
        for plane in (left, state, right):
            if shift_y == -1:
                plane = row_up * pltpu.roll(plane, WIDTH, 1)
            if shift_y == 1:
                plane = row_down * pltpu.roll(plane, size - WIDTH, 1)
            pieces.append(plane)
    return pieces


def comb_taps(q_ref, lanes, masks):
    size = lanes.size
    row_up, row_down, col_left, col_right = masks
    result = None
    for shift_y in (-1, 0, 1):
        base = 24 * (shift_y + 1)
        line = (
            col_left * pltpu.roll(q_ref[base : base + 8, lanes], 1, 1)
            + q_ref[base + 8 : base + 16, lanes]
            + col_right * pltpu.roll(q_ref[base + 16 : base + 24, lanes], size - 1, 1)
        )
        if shift_y == -1:
            line = row_up * pltpu.roll(line, WIDTH, 1)
        if shift_y == 1:
            line = row_down * pltpu.roll(line, size - WIDTH, 1)
        result = line if result is None else result + line
    return result


def normed_by(values, square):
    return values / jnp.sqrt(square + 1e-12)


def main_kernel(
    index_ref, x0_ref, x1_ref, u2_ref, u3_ref, planes_ref, small_ref,
    keep_ref, send_ref, cols_ref, rows_ref, og_ref,
    w_s, w13_s, w2_s, w2t_s, wout_s, bias_s, taps_s, sl1_s, sl2_s, cv1_s, cv2_s,
    lin1_s, lin2_s, gt1_s, gt2_s, acc1_s, acc2_s, tan1_s, tan2_s, g1_s, g2_s, hid1_s, hid2_s,
    q_s, q0_s, comb_s, *, own, channels, chips,
):
    me = index_ref[0]
    rows_own = channels // (2 * chips)
    region = own + 2 * HALO
    all_sum = functools.partial(jnp.sum, keepdims=True)

    for m in range(chips):
        for b, ref in ((0, x0_ref), (1, x1_ref)):
            w_s[jnp.bitwise_xor(me, 2 * m + b)] = ref[m]
    tile = w_s[:, :, channels:].reshape(channels, LANES)
    w2t = w_s[:, :, 0:channels].reshape(channels, channels)
    lane = iota((1, LANES), 1)
    is_one = lane_is_one(lane)
    is_three = lane_is_three(lane)
    taps_one = jnp.where(is_one, tile, 0.0)
    taps_three = jnp.where(is_three, tile, 0.0)
    head = (lane % 8 == 4) & (lane < TAP_ROWS)
    u1 = tile[:, TAP_ROWS : TAP_ROWS + 1]
    u2 = u2_ref[...]
    u3 = u3_ref[...]
    for _ in range(2):
        v1 = all_sum(taps_one * u1, axis=0)
        v2 = all_sum(w2t * u2, axis=1)
        mixed = taps_three * u3
        mixed = mixed + pltpu.roll(mixed, LANES - 1, 1) + pltpu.roll(mixed, LANES - 2, 1)
        v3 = jnp.where(head, mixed, 0.0)
        v1 = normed_by(v1, all_sum(v1 * v1))
        v2 = normed_by(v2, all_sum(v2 * v2))
        v3 = normed_by(v3, all_sum(all_sum(v3 * v3, axis=0), axis=1))
        m1 = all_sum(taps_one * v1, axis=1)
        m2 = all_sum(w2t * v2, axis=0)
        spread = v3 + pltpu.roll(v3, 1, 1) + pltpu.roll(v3, 2, 1)
        m3 = all_sum(taps_three * spread, axis=0)
        for shift in (64, 32, 16, 8):
            m3 = m3 + pltpu.roll(m3, shift, 1)
        square1 = all_sum(m1 * m1)
        square2 = all_sum(m2 * m2)
        square3 = all_sum(jnp.where((lane >= 4) & (lane < 7), m3 * m3, 0.0))
        u1 = normed_by(m1, square1)
        u2 = normed_by(m2, square2)
        u3 = jnp.where(is_three, normed_by(m3, square3), 0.0)
    sigma1 = jnp.sqrt(square1)
    sigma2 = jnp.sqrt(square2)
    sigma3 = jnp.sqrt(square3)
    cols_ref[...] = jnp.where(lane == 0, u1, jnp.where(lane == 1, v2, v3)).reshape(cols_ref.shape)
    sigma_row = jnp.where(lane == 0, sigma1, jnp.where(lane == 1, sigma2, sigma3))
    rows_ref[...] = jnp.zeros(rows_ref.shape, F32)
    rows_ref[0:1, :] = u2
    rows_ref[1:2, 0:LANES] = v1
    rows_ref[2:3, 0:LANES] = u3
    rows_ref[3:4, 0:LANES] = sigma_row

    scaled = taps_one * (SHRINK / sigma1) + taps_three * (SHRINK / sigma3)
    w13_s[0:channels] = jnp.where(is_one, scaled, 0.0).astype(BF16)
    w13_s[channels:] = jnp.where(is_three, scaled, 0.0).astype(BF16)
    flipped = scaled.T
    blocks = [pltpu.roll(flipped[(8 - t) * 8 : (9 - t) * 8], 4, 0) for t in range(9)]
    flipped = jnp.concatenate(blocks + [jnp.zeros((8, channels), F32)], axis=0)
    first_rows = iota((TAP_ROWS + 8, 1), 0) % 8 < 4
    wout_s[:, 0:channels] = jnp.where(first_rows, flipped, 0.0).astype(BF16)
    wout_s[:, channels:] = jnp.where(first_rows, 0.0, flipped).astype(BF16)
    w2t_scaled = w2t * (SHRINK / sigma2)
    w2t_s[...] = w2t_scaled.astype(BF16)
    w2_s[...] = w2t_scaled.T.astype(BF16)
    for layer in range(2):
        column = tile[:, TAP_ROWS + 1 + layer : TAP_ROWS + 2 + layer]
        bias_s[layer] = jnp.broadcast_to(column, (channels, LANES))

    shift8 = small_ref[:, 0:1]
    scale8 = small_ref[:, 1:2]
    bias8 = small_ref[:, 2:3]
    extra8 = small_ref[:, 3:4]
    upper = iota((8, 1), 0) >= 4
    probes8 = planes_ref[8:16]
    cot8 = planes_ref[16:24]

    def masks_at(lanes):
        return [planes_ref[32 + i : 33 + i, lanes] for i in range(4)]

    def put_taps(slot, pieces, lanes):
        taps_s[slot, 0 : TAP_ROWS + 8, lanes] = jnp.concatenate(
            pieces + [jnp.zeros((8, lanes.size), F32)], axis=0
        ).astype(BF16)
        taps_s[slot, TAP_ROWS + 8 :, lanes] = jnp.zeros((LANES - TAP_ROWS - 8, lanes.size), BF16)

    whole = pl.ds(0, region)
    h8 = (planes_ref[0:8] + shift8) * scale8
    sig8 = 0.5 + 0.5 * jnp.tanh(0.5 * h8)
    rest8 = 1.0 - sig8
    slope0 = (sig8 + h8 * sig8 * rest8) / 1.1
    curve0 = sig8 * rest8 * (2.0 + h8 * (1.0 - 2.0 * sig8)) / 1.1
    state = jnp.where(upper, cot8, h8 * sig8 / 1.1)
    put_taps(0, col_taps(state, masks_at(whole)), whole)
    state = probes8 * jnp.where(upper, planes_ref[24 + 7 : 24 + 8], slope0)
    put_taps(1, col_taps(state, masks_at(whole)), whole)

    def activation(act, slope_ref, curve_ref, lanes, curve_lanes, in_curve):
        half = 0.5 * jnp.tanh(0.5 * act)
        sig = 0.5 + half
        rest = 0.5 - half
        hidden = act * sig * (1.0 / 1.1)
        slope_ref[:, lanes] = sig * (1.0 / 1.1) + hidden * rest
        sig2 = sig * (2.0 / 1.1)

        @pl.when(in_curve)
        def _():
            curve_ref[:, curve_lanes] = (rest * (sig2 - 2.0 * half * hidden)).astype(BF16)

        return hidden.astype(BF16)

    own_blocks = own // BLOCK

    def start_body(j, carry):
        lanes = pl.ds(pl.multiple_of(j * BLOCK, LANES), BLOCK)
        in_curve = (j >= 1) & (j < own_blocks + 3)
        curve_lanes = pl.ds(pl.multiple_of(jnp.clip(j - 1, 0, own_blocks + 1) * BLOCK, LANES), BLOCK)
        taps = taps_s[0, :, lanes]
        act1 = dot_nn(w13_s[0:channels], taps)
        bias1 = bias_s[0]
        hidden1 = activation(
            act1 + jnp.concatenate([bias1, bias1], axis=1), sl1_s, cv1_s, lanes, curve_lanes, in_curve
        )
        act2 = dot_nn(w2_s[...], hidden1)
        bias2 = bias_s[1]
        hidden2 = activation(
            act2 + jnp.concatenate([bias2, bias2], axis=1), sl2_s, cv2_s, lanes, curve_lanes, in_curve
        )
        q0_s[:, lanes] = dot_nn(wout_s[:, 0:channels], hidden2)[0:TAP_ROWS]

        @pl.when((j >= 2) & (j < own_blocks + 2))
        def _():
            own_lanes = pl.ds(pl.multiple_of((j - 2) * BLOCK, LANES), BLOCK)
            hid1_s[:, own_lanes] = hidden1
            hid2_s[:, own_lanes] = hidden2

        return carry

    lax.fori_loop(0, own_blocks + 4, start_body, 0)

    own_in_slot = pl.ds(LANES, own)

    def series_stage(stage):
        offset = LANES * (stage - 1)
        count = own_blocks + 5 - stage
        tan_slot = min(stage, 3) - 1
        aligned = stage % 2 == 1
        store_from = (HALO - offset) // BLOCK if aligned else (HALO - LANES - offset) // BLOCK
        store_count = own_blocks if aligned else own_blocks + 1

        def body(j, carry):
            start = pl.multiple_of(offset + j * BLOCK, LANES)
            lanes = pl.ds(start, BLOCK)
            both = dot_nn(w13_s[...], taps_s[stage, :, lanes])
            lin1 = both[0:channels]
            gt2 = both[channels:]
            slope1 = sl1_s[:, lanes]
            slope2 = sl2_s[:, lanes]
            tan1 = (slope1 * lin1).astype(BF16)
            g2 = (slope2 * gt2).astype(BF16)
            lin2 = dot_nn(w2_s[...], tan1)
            gt1 = dot_nn(w2t_s[...], g2)
            tan2 = (slope2 * lin2).astype(BF16)
            g1 = (slope1 * gt1).astype(BF16)
            q_s[:, lanes] = dot_nn(wout_s[...], jnp.concatenate([tan2, g1], axis=0))[0:TAP_ROWS]

            @pl.when((j >= store_from) & (j < store_from + store_count))
            def _():
                slot_lanes = pl.ds(pl.multiple_of(start - (HALO - LANES), LANES), BLOCK)
                tan1_s[tan_slot, :, slot_lanes] = tan1
                tan2_s[tan_slot, :, slot_lanes] = tan2
                g1_s[tan_slot, :, slot_lanes] = g1
                g2_s[tan_slot, :, slot_lanes] = g2

            wide_lanes = pl.ds(pl.multiple_of(jnp.maximum(start - BLOCK, 0), LANES), BLOCK)
            if stage <= 2:
                wide_count = own_blocks + 3 - stage

                @pl.when((j >= 1) & (j < 1 + wide_count))
                def _():
                    lin1_s[stage - 1, :, wide_lanes] = lin1.astype(BF16)
                    lin2_s[stage - 1, :, wide_lanes] = lin2.astype(BF16)
                    gt1_s[stage - 1, :, wide_lanes] = gt1.astype(BF16)
                    gt2_s[stage - 1, :, wide_lanes] = gt2.astype(BF16)
            else:
                slot = 4 - stage
                for acc_ref, lin_ref, gt_ref, lin, gt in (
                    (acc1_s, lin1_s, gt1_s, lin1, gt1),
                    (acc2_s, lin2_s, gt2_s, lin2, gt2),
                ):
                    total = lin * gt_ref[slot, :, wide_lanes].astype(F32)
                    total = total + gt * lin_ref[slot, :, wide_lanes].astype(F32)
                    if stage == 4:
                        total = total + acc_ref[:, wide_lanes]
                    acc_ref[:, wide_lanes] = total
            return carry

        lax.fori_loop(0, count, body, 0)

        inside = pl.ds(offset, count * BLOCK)
        result = comb_taps(q_s, inside, masks_at(inside))
        core_from = HALO - offset
        comb_s[stage - 1] = result[:, core_from : core_from + own]
        if stage < NMAX:
            nxt = result[:, LANES : count * BLOCK - LANES]
            lanes = pl.ds(offset + LANES, (count - 1) * BLOCK)
            seed = probes8[:, offset + LANES : offset + LANES + (count - 1) * BLOCK]
            coef = planes_ref[24 + 4 + 3 - stage : 24 + 4 + 4 - stage, lanes]
            following = slope0[:, offset + LANES : offset + LANES + (count - 1) * BLOCK] * nxt
            following = following + jnp.where(upper, seed * coef, 0.0)
            put_taps(stage + 1, col_taps(following, masks_at(lanes)), lanes)

    def own_taps(slot):
        return taps_s[slot, :, pl.ds(HALO, own)]

    def add_weight_grads(slot_pairs, tap_pairs, first):
        total = None
        for left, right in slot_pairs:
            part = dot_nt(left, right)
            total = part if total is None else total + part
        one = None
        three = None
        for left_one, left_three, slot in tap_pairs:
            part_one = dot_nt(left_one, own_taps(slot))
            part_three = dot_nt(left_three, own_taps(slot))
            one = part_one if one is None else one + part_one
            three = part_three if three is None else three + part_three
        tile_part = jnp.where(is_one, one, jnp.where(is_three, three, 0.0))
        w2_part = total.reshape(2 * chips, rows_own, channels)
        tile_part = tile_part.reshape(2 * chips, rows_own, LANES)
        if first:
            w_s[:, :, 0:channels] = w2_part
            w_s[:, :, channels:] = tile_part
        else:
            w_s[:, :, 0:channels] = w_s[:, :, 0:channels] + w2_part
            w_s[:, :, channels:] = w_s[:, :, channels:] + tile_part

    def slot_of(ref, slot):
        return ref[slot, :, own_in_slot]

    series_stage(1)
    series_stage(2)
    series_stage(3)
    add_weight_grads(
        ((slot_of(tan1_s, 1), slot_of(g2_s, 2)), (slot_of(tan1_s, 2), slot_of(g2_s, 1))),
        (
            (slot_of(g1_s, 2), slot_of(tan2_s, 2), 2),
            (slot_of(g1_s, 1), slot_of(tan2_s, 1), 3),
        ),
        True,
    )
    series_stage(4)
    add_weight_grads(
        ((slot_of(tan1_s, 0), slot_of(g2_s, 2)), (slot_of(tan1_s, 2), slot_of(g2_s, 0))),
        (
            (slot_of(g1_s, 2), slot_of(tan2_s, 2), 1),
            (slot_of(g1_s, 0), slot_of(tan2_s, 0), 4),
        ),
        False,
    )

    def final_body(j, carry):
        bias_one, bias_two = carry
        start = pl.multiple_of(HALO - LANES + j * BLOCK, LANES)
        lanes = pl.ds(start, BLOCK)
        wide_lanes = pl.ds(pl.multiple_of(LANES + j * BLOCK, LANES), BLOCK)
        slot_lanes = pl.ds(pl.multiple_of(j * BLOCK, LANES), BLOCK)
        low_lanes = (j > 0).astype(F32)
        high_lanes = (j < own_blocks).astype(F32)
        gs2 = dot_nn(w13_s[channels:], taps_s[0, :, lanes])
        ga2 = cv2_s[:, wide_lanes].astype(F32) * acc2_s[:, wide_lanes] + sl2_s[:, lanes] * gs2
        low2 = ga2.astype(BF16)
        gs1 = dot_nn(w2t_s[...], low2)
        ga1 = cv1_s[:, wide_lanes].astype(F32) * acc1_s[:, wide_lanes] + sl1_s[:, lanes] * gs1
        low1 = ga1.astype(BF16)
        q_s[:, lanes] = q0_s[:, lanes] + dot_nn(wout_s[:, channels:], low1)[0:TAP_ROWS]
        g2_s[0, :, slot_lanes] = low2
        g1_s[0, :, slot_lanes] = low1
        bias_one = bias_one + low_lanes * ga1[:, 0:LANES] + high_lanes * ga1[:, LANES:]
        bias_two = bias_two + low_lanes * ga2[:, 0:LANES] + high_lanes * ga2[:, LANES:]
        return bias_one, bias_two

    zero = jnp.zeros((channels, LANES), F32)
    bias_one, bias_two = lax.fori_loop(0, own_blocks + 1, final_body, (zero, zero))
    add_weight_grads(
        ((hid1_s[...], slot_of(g2_s, 0)),), ((slot_of(g1_s, 0), hid2_s[...], 0),), False
    )

    inside = pl.ds(HALO - LANES, own + BLOCK)
    result = comb_taps(q_s, inside, masks_at(inside))[:, LANES : LANES + own]
    mine = slice(HALO, HALO + own)
    h_own = h8[:, mine]
    cot_own = cot8[:, mine]
    probes_own = probes8[:, mine]
    mixed = comb_s[0] * pltpu.roll(comb_s[2], 4, 0)
    mixed = mixed + comb_s[1] * pltpu.roll(comb_s[1], 4, 0)
    mixed = mixed + comb_s[2] * pltpu.roll(comb_s[0], 4, 0)
    mixed = mixed + comb_s[3] * probes_own
    grad_h = cot_own + slope0[:, mine] * result + curve0[:, mine] * mixed
    grad_in = grad_h * scale8
    density = planes_ref[24:25, mine] * comb_s[0]
    for k in range(1, NMAX):
        density = density + planes_ref[24 + k : 25 + k, mine] * comb_s[k]
    density = density * probes_own
    density = density[0:1] + density[1:2] + density[2:3]
    row8 = iota((8, 1), 0)
    out = jnp.where(row8 < 3, h_own + result + bias8, jnp.where(row8 == 3, density, grad_in))
    og_ref[...] = jnp.where(row8 < 7, out, 0.0)

    sums = (
        all_sum(grad_in, axis=1),
        all_sum(grad_h * h_own, axis=1) + extra8,
        all_sum(cot_own, axis=1),
    )
    small_row = jnp.zeros((1, LANES), F32)
    for a, column in enumerate(sums):
        for i in range(3):
            small_row = jnp.where(lane == TAP_ROWS + 2 + 3 * a + i, column[4 + i : 5 + i], small_row)
    bias_one = all_sum(bias_one, axis=1)
    bias_two = all_sum(bias_two, axis=1)
    extras = jnp.where(lane == TAP_ROWS, bias_one, jnp.where(lane == TAP_ROWS + 1, bias_two, small_row))
    extras = extras.reshape(2 * chips, rows_own, LANES)
    w_s[:, :, channels:] = w_s[:, :, channels:] + extras

    core = jnp.bitwise_and(me, 1)
    chip = jnp.right_shift(me, 1)
    for m in range(chips):
        block = 2 * jnp.bitwise_xor(chip, m)
        keep_ref[m] = w_s[block + core]
        send_ref[m] = w_s[block + 1 - core]


def call_main(me, x0, x1, u2, u3, planes, small, own, channels, chips):
    rows_own = channels // (2 * chips)
    region = own + 2 * HALO
    wide = own + 2 * BLOCK
    slot = own + BLOCK
    width = channels + LANES
    out_shape = (
        jax.ShapeDtypeStruct((chips, rows_own, width), F32),
        jax.ShapeDtypeStruct((chips, rows_own, width), F32),
        jax.ShapeDtypeStruct((2 * chips, rows_own, LANES), F32),
        jax.ShapeDtypeStruct((8, channels), F32),
        jax.ShapeDtypeStruct((8, own), F32),
    )
    vmem = pltpu.VMEM
    scratch = [
        vmem((2 * chips, rows_own, width), F32),
        vmem((2 * channels, LANES), BF16),
        vmem((channels, channels), BF16),
        vmem((channels, channels), BF16),
        vmem((TAP_ROWS + 8, 2 * channels), BF16),
        vmem((2, channels, LANES), F32),
        vmem((NMAX + 1, LANES, region), BF16),
        vmem((channels, region), F32),
        vmem((channels, region), F32),
        vmem((channels, wide), BF16),
        vmem((channels, wide), BF16),
        vmem((2, channels, wide), BF16),
        vmem((2, channels, wide), BF16),
        vmem((2, channels, wide), BF16),
        vmem((2, channels, wide), BF16),
        vmem((channels, wide), F32),
        vmem((channels, wide), F32),
        vmem((3, channels, slot), BF16),
        vmem((3, channels, slot), BF16),
        vmem((3, channels, slot), BF16),
        vmem((3, channels, slot), BF16),
        vmem((channels, own), BF16),
        vmem((channels, own), BF16),
        vmem((TAP_ROWS, region), F32),
        vmem((TAP_ROWS, region), F32),
        vmem((NMAX, 8, own), F32),
    ]
    full = pl.BlockSpec(memory_space=pltpu.VMEM)
    return pl.pallas_call(
        functools.partial(main_kernel, own=own, channels=channels, chips=chips),
        out_shape=out_shape,
        in_specs=[pl.BlockSpec(memory_space=pltpu.SMEM)] + [full] * 6,
        out_specs=[full] * 5,
        scratch_shapes=scratch,
        compiler_params=pltpu.CompilerParams(vmem_limit_bytes=63 * 1024 * 1024),
        name="flow_block",
    )(me, x0, x1, u2, u3, planes, small)


def assemble_kernel(index_ref, kinds_ref, p0_ref, p1_ref, small_ref, z_ref, gin_ref, logdet_ref, dens_s, *, own, chips, frames):
    me = index_ref[0]
    for m in range(chips):
        for b, ref in ((0, p0_ref), (1, p1_ref)):
            shard = jnp.bitwise_xor(me, 2 * m + b)
            lanes = pl.ds(pl.multiple_of(shard * own, LANES), own)
            piece = ref[m]
            z_ref[:, lanes] = piece[0:3]
            gin_ref[:, lanes] = piece[4:7]
            dens_s[:, lanes] = piece[3:4]
    scale_sum = small_ref[0, 0]
    pixel = iota((1, FRAME), 1)
    bottom = (pixel // (WIDTH * 32)) % 2
    right = (pixel // 32) % 2
    lane = iota((1, 4), 1)
    for f in range(frames):
        line = dens_s[:, f * FRAME : (f + 1) * FRAME]
        quads = jnp.zeros((1, 4), F32)
        total = jnp.zeros((1, 1), F32)
        for slot in range(4):
            picked = jnp.where(bottom * 2 + right == slot, line, 0.0)
            picked = jnp.sum(picked, axis=1, keepdims=True)
            quads = jnp.where(lane == slot, picked, quads)
            total = total + picked
        split = kinds_ref[f] == 2
        whole = jnp.where(lane == 0, total + 4096.0 * scale_sum, 0.0)
        logdet_ref[f : f + 1, :] = jnp.where(split, quads + 1024.0 * scale_sum, whole)


def norm_kernel(index_ref, a_ref, b_ref, pack_ref, cols_ref, rows_ref, grad_ref, out_ref, *, channels):
    grad = a_ref[...].astype(F32) + b_ref[...].astype(F32)
    grad_ref[...] = grad
    lane = iota((1, LANES), 1)
    is_one = lane_is_one(lane)
    is_three = lane_is_three(lane)
    tile = grad[:, channels:]
    weights = pack_ref[:, channels:]
    cols = cols_ref[...]
    u1 = cols[:, 0:1]
    v2 = cols[:, 1:2]
    spread = jnp.where((lane % 8 == 4) & (lane < TAP_ROWS), cols, 0.0)
    spread = spread + pltpu.roll(spread, 1, 1) + pltpu.roll(spread, 2, 1)
    outer_one = u1 * rows_ref[1:2, 0:LANES]
    outer_three = spread * rows_ref[2:3, 0:LANES]
    outer_two = v2 * rows_ref[0:1, :]
    grad_two = grad[:, 0:channels]
    weight_two = pack_ref[:, 0:channels]

    def total(values):
        return jnp.sum(jnp.sum(values, axis=0, keepdims=True), axis=1, keepdims=True)

    bias = (lane == TAP_ROWS) | (lane == TAP_ROWS + 1)
    parts = (
        total(jnp.where(is_one, tile * tile, 0.0)),
        total(grad_two * grad_two),
        total(jnp.where(is_three, tile * tile, 0.0)),
        total(jnp.where(is_one, tile * weights, 0.0)),
        total(grad_two * weight_two),
        total(jnp.where(is_three, tile * weights, 0.0)),
        total(jnp.where(is_one, tile * outer_one, 0.0)),
        total(grad_two * outer_two),
        total(jnp.where(is_three, tile * outer_three, 0.0)),
        total(jnp.where(is_one, outer_one * outer_one, 0.0)),
        total(outer_two * outer_two),
        total(jnp.where(is_three, outer_three * outer_three, 0.0)),
        total(jnp.where(bias, tile * tile, 0.0)),
    )
    row = jnp.zeros((1, LANES), F32)
    for index, part in enumerate(parts):
        row = jnp.where(lane == index, part, row)
    small = (lane >= TAP_ROWS + 2) & (lane < TAP_ROWS + 11) & (index_ref[0] == 0)
    row = jnp.where(small, tile[0:1], row)
    out_ref[...] = jnp.broadcast_to(row, out_ref.shape)


def moment_step(grad, moment, second):
    new_moment = BETA_ONE * moment + (1.0 - BETA_ONE) * grad
    new_second = BETA_TWO * second + (1.0 - BETA_TWO) * grad * grad
    return (new_moment, new_second)


def adam_step(param, grad, moment, second):
    new_moment, new_second = moment_step(grad, moment, second)
    fix_one = 1.0 - BETA_ONE**STEP
    fix_two = 1.0 - BETA_TWO**STEP
    update = new_moment / fix_one / (jnp.sqrt(new_second / fix_two) + ADAM_EPS) + DECAY * param
    return (param - LR_RATE * update, new_moment, new_second)


def update_kernel(
    totals_ref, grad_ref, cols_ref, rows_ref,
    w1_ref, m1_ref, s1_ref, w2_ref, m2_ref, s2_ref, w3_ref, m3_ref, s3_ref,
    mb_ref, sb_ref, small_ref, msmall_ref, ssmall_ref,
    norm_out, nw1, nm1, ns1, nw2, nm2, ns2, nw3, nm3, ns3, cb, nmb, nsb, nsm, nmsm, nssm, lw1, lw2, lw3,
    u1_out, v1_out, u2_out, v2_out, u3_out, v3_out, *, channels,
):
    lane = iota((1, LANES), 1)
    lines = [totals_ref[m : m + 1] for m in range(totals_ref.shape[0])]
    while len(lines) > 1:
        lines = [lines[m] + lines[m + 1] for m in range(0, len(lines), 2)]
    row = lines[0]

    def pick(index):
        return jnp.sum(jnp.where(lane == index, row, 0.0), axis=1, keepdims=True)

    sigmas = rows_ref[3:4, 0:LANES]
    small_row = jnp.where((lane >= TAP_ROWS + 2) & (lane < TAP_ROWS + 11), row, 0.0)
    square = pick(12) + jnp.sum(small_row * small_row, axis=1, keepdims=True)
    scales = []
    for j in range(3):
        sigma = sigmas[:, j : j + 1]
        ratio = SHRINK / sigma
        factor = pick(3 + j) / sigma
        fixed = pick(j) - 2.0 * factor * pick(6 + j) + factor * factor * pick(9 + j)
        square = square + ratio * ratio * jnp.maximum(fixed, 0.0)
        scales.append((ratio, factor))
    norm = jnp.sqrt(square)
    norm_out[...] = norm
    clip = jnp.minimum(1.0, CLIP_LIMIT / (norm + 1e-06))

    cols = cols_ref[...]
    grad = grad_ref[...]
    tile = grad[:, channels:]
    is_one = lane_is_one(lane)
    is_three = lane_is_three(lane)
    spread = jnp.where((lane % 8 == 4) & (lane < TAP_ROWS), cols, 0.0)
    spread = spread + pltpu.roll(spread, 1, 1) + pltpu.roll(spread, 2, 1)
    outer_one = cols[:, 0:1] * rows_ref[1:2, 0:LANES]
    outer_three = spread * rows_ref[2:3, 0:LANES]
    outer_two = cols[:, 1:2] * rows_ref[0:1, :]
    fixed_one = jnp.where(is_one, scales[0][0] * (tile - scales[0][1] * outer_one) * clip, 0.0)
    fixed_two = scales[1][0] * (grad[:, 0:channels] - scales[1][1] * outer_two) * clip
    fixed_three = jnp.where(is_three, scales[2][0] * (tile - scales[2][1] * outer_three) * clip, 0.0)
    grad_one = dot_nt(fixed_one, spread_one(), HIGH)
    grad_two = fixed_two.T
    grad_three = dot_nt(spread_three(), fixed_three, HIGH)

    for grad_j, w_ref, m_ref, s_ref, nw, nm, ns, lw in (
        (grad_one, w1_ref, m1_ref, s1_ref, nw1, nm1, ns1, lw1),
        (grad_two, w2_ref, m2_ref, s2_ref, nw2, nm2, ns2, lw2),
        (grad_three, w3_ref, m3_ref, s3_ref, nw3, nm3, ns3, lw3),
    ):
        new, moment, second = adam_step(w_ref[...], grad_j, m_ref[...], s_ref[...])
        nw[...] = new
        nm[...] = moment
        ns[...] = second
        lw[...] = new.astype(BF16)

    bias = (tile * clip).T[TAP_ROWS : TAP_ROWS + 2, :]
    cb[...] = bias
    moment, second = moment_step(bias, mb_ref[...], sb_ref[...])
    nmb[...] = moment
    nsb[...] = second

    small_row = small_row * clip
    lane3 = iota((1, 3), 1)
    rows = []
    for a in range(3):
        line = jnp.zeros((1, 3), F32)
        for i in range(3):
            at = TAP_ROWS + 2 + 3 * a + i
            line = jnp.where(lane3 == i, small_row[:, at : at + 1], line)
        rows.append(line)
    small_grad = jnp.concatenate(rows, axis=0)
    new, moment, second = adam_step(small_ref[...], small_grad, msmall_ref[...], ssmall_ref[...])
    nsm[...] = new
    nmsm[...] = moment
    nssm[...] = second

    flipped = cols.T
    u1_out[...] = flipped[0:1]
    v2_out[...] = flipped[1:2]
    tap = iota((9, LANES), 0)
    select = (iota((9, LANES), 1) == (8 - tap) * 8 + 4).astype(F32)
    v3_out[...] = dot_nn(select, flipped, HIGH)
    v1_out[...] = dot_nt(rows_ref[1:2, 0:LANES], spread_one(), HIGH)
    u2_out[...] = rows_ref[0:1, :]
    u3_out[...] = rows_ref[2:3, 4:7]


def window_planes(images, frame_kinds, series_len, probes, cot_z, cot_logdet, first, region):
    frames = frame_kinds.shape[0]
    pixels = images.shape[1]
    position = lax.iota(jnp.int32, pixels)
    kind = jnp.broadcast_to(frame_kinds[:, None], (frames, FRAME)).reshape(pixels)
    limit = jnp.where(kind == 1, 64, 32)
    row = (position // WIDTH) % limit
    col = position % limit

    def spread(values):
        quads = jnp.broadcast_to(values.reshape(-1, frames, 2, 1, 2, 1), (values.shape[0], frames, 2, 32, 2, 32))
        single = values[:, :, 0].reshape(-1, frames, 1, 1, 1, 1)
        picked = jnp.where(frame_kinds.reshape(1, frames, 1, 1, 1, 1) == 2, quads, single)
        return picked.reshape(values.shape[0], pixels)

    coefs = []
    for k in range(NMAX):
        term = (-1.0) ** k / (k + 1)
        coefs.append(jnp.where(series_len >= k + 1, term, 0.0).astype(F32))
    coefs = jnp.stack(coefs)
    coefs = spread(jnp.concatenate([coefs, coefs * cot_logdet[None]], axis=0))
    masks = jnp.stack([row > 0, row < limit - 1, col > 0, col < limit - 1]).astype(F32)
    blank1 = jnp.zeros((1, pixels), F32)
    blank4 = jnp.zeros((4, pixels), F32)
    planes = jnp.concatenate(
        [images, blank1, images, blank1, probes, blank1, probes, blank1, blank4, cot_z, blank1, coefs, masks, blank4],
        axis=0,
    )
    planes = jnp.pad(planes, ((0, 0), (HALO, HALO)))
    return lax.dynamic_slice_in_dim(planes, first, region, 1)


def local(
    images, frame_kinds, series_len, probes, cot_z, cot_logdet, weight1, weight2, weight3, biases,
    small_params, power_u1, power_u2, power_u3, moment_w1, second_w1, moment_w2, second_w2,
    moment_w3, second_w3, moment_bias, second_bias, moment_small, second_small,
):
    shards = lax.axis_size("chan")
    replicas = lax.axis_size("dp")
    chips = shards // 2
    me = lax.axis_index("chan")
    channels = weight2.shape[0]
    rows_own = weight1.shape[0]
    pixels = images.shape[1]
    frames = frame_kinds.shape[0]
    own = pixels // shards
    width = channels + LANES
    full = pl.BlockSpec(memory_space=pltpu.VMEM)
    smem = pl.BlockSpec(memory_space=pltpu.SMEM)
    index = me.reshape(1).astype(jnp.int32)

    def swap(values, axis, size, bits):
        return lax.ppermute(values, axis, [(j, j ^ bits) for j in range(size)])

    def gather_shards(values):
        pieces = [values] + [swap(values, "chan", shards, 2 * m) for m in range(1, chips)]
        first = jnp.stack(pieces)
        return first, swap(first, "chan", shards, 1)

    pack = pl.pallas_call(
        pack_kernel,
        out_shape=jax.ShapeDtypeStruct((rows_own, width), F32),
        in_specs=[full] * 5,
        out_specs=full,
        name="pack_weights",
    )(weight1, weight2, weight3, biases, power_u1.reshape(1, rows_own))
    x0, x1 = gather_shards(pack)

    u3_row = jnp.tile(jnp.concatenate([jnp.zeros((4,), F32), power_u3, jnp.zeros((1,), F32)]), LANES // 8)
    planes = window_planes(
        images, frame_kinds, series_len, probes, cot_z, cot_logdet, me * own, own + 2 * HALO
    )
    slots = lax.broadcasted_iota(jnp.int32, (frames, 4), 1)
    counts = jnp.where(frame_kinds[:, None] == 2, 1024.0, jnp.where(slots == 0, 4096.0, 0.0))
    extra = jnp.where(me == 0, jnp.sum(counts * cot_logdet), 0.0)
    columns = jnp.stack(
        [small_params[0], jnp.exp(small_params[1]), small_params[2], jnp.broadcast_to(extra, (3,))], axis=1
    )
    small = jnp.zeros((8, LANES), F32).at[0:3, 0:4].set(columns).at[4:7, 0:4].set(columns)

    keep, send, cols, rows, og = call_main(
        index, x0, x1, power_u2.reshape(1, channels), u3_row.reshape(1, LANES), planes, small, own, channels, chips
    )

    got = swap(send, "chan", shards, 1)
    summed = keep + got
    low = summed.astype(BF16)
    total = summed[0]
    for m in range(1, chips):
        total = total + swap(low[m], "chan", shards, 2 * m).astype(F32)
    half = total.astype(BF16)
    bits = 1
    while 2 * bits < replicas:
        half = (half.astype(F32) + swap(half, "dp", replicas, bits).astype(F32)).astype(BF16)
        bits *= 2
    other = swap(half, "dp", replicas, bits) if replicas > 1 else jnp.zeros_like(half)

    p0, p1 = gather_shards(og)
    z_out, grad_input, logdet = pl.pallas_call(
        functools.partial(assemble_kernel, own=own, chips=chips, frames=frames),
        out_shape=(
            jax.ShapeDtypeStruct((3, pixels), F32),
            jax.ShapeDtypeStruct((3, pixels), F32),
            jax.ShapeDtypeStruct((frames, 4), F32),
        ),
        in_specs=[smem, smem, full, full, smem],
        out_specs=[full] * 3,
        scratch_shapes=[pltpu.VMEM((1, pixels), F32)],
        name="assemble_outputs",
    )(index, frame_kinds, p0, p1, jnp.sum(small_params[1]).reshape(1, 1))

    cols_own = lax.dynamic_index_in_dim(cols, me, 0, False)
    grad, parts = pl.pallas_call(
        functools.partial(norm_kernel, channels=channels),
        out_shape=(
            jax.ShapeDtypeStruct((rows_own, width), F32),
            jax.ShapeDtypeStruct((8, LANES), F32),
        ),
        in_specs=[smem] + [full] * 5,
        out_specs=[full] * 2,
        name="norm_parts",
    )(index, half, other, pack, cols_own, rows)
    pair = parts + swap(parts, "chan", shards, 1)
    totals = [pair[0:1]] + [swap(pair, "chan", shards, 2 * m)[0:1] for m in range(1, chips)]
    totals = jnp.concatenate(totals, axis=0)

    def like(value, dtype=F32):
        return jax.ShapeDtypeStruct(value.shape, dtype)

    out_shape = (
        [jax.ShapeDtypeStruct((1, 1), F32)]
        + [like(weight1)] * 3
        + [like(weight2)] * 3
        + [like(weight3)] * 3
        + [like(biases)] * 3
        + [like(small_params)] * 3
        + [like(weight1, BF16), like(weight2, BF16), like(weight3, BF16)]
        + [jax.ShapeDtypeStruct((1, rows_own), F32), jax.ShapeDtypeStruct((1, 27), F32)]
        + [jax.ShapeDtypeStruct((1, channels), F32), jax.ShapeDtypeStruct((1, rows_own), F32)]
        + [jax.ShapeDtypeStruct((1, 3), F32), jax.ShapeDtypeStruct((9, rows_own), F32)]
    )
    done = pl.pallas_call(
        functools.partial(update_kernel, channels=channels),
        out_shape=out_shape,
        in_specs=[full] * 18,
        out_specs=[full] * len(out_shape),
        name="adam_update",
    )(
        totals, grad, cols_own, rows,
        weight1, moment_w1, second_w1, weight2, moment_w2, second_w2, weight3, moment_w3, second_w3,
        moment_bias, second_bias, small_params, moment_small, second_small,
    )
    norm, updates, vectors = done[0], done[1:19], done[19:]
    return (
        z_out,
        logdet,
        grad_input,
        norm.reshape(()),
        *updates,
        vectors[0].reshape(rows_own),
        vectors[1].reshape(27),
        vectors[2].reshape(channels),
        vectors[3].reshape(rows_own),
        vectors[4].reshape(3),
        vectors[5],
    )


def solution(mesh):
    chan_rows = P("chan", None)
    chan_cols = P(None, "chan")
    return jax.shard_map(
        local,
        mesh=mesh,
        in_specs=(
            P(None, "dp"), P("dp"), P("dp", None), P(None, "dp"), P(None, "dp"), P("dp", None),
            chan_rows, chan_cols, chan_cols, chan_cols, P(), P("chan"), P(), P(),
            chan_rows, chan_rows, chan_cols, chan_cols, chan_cols, chan_cols, chan_cols, chan_cols, P(), P(),
        ),
        out_specs=(
            P(None, "dp"), P("dp", None), P(None, "dp"), P(),
            chan_rows, chan_rows, chan_rows, chan_cols, chan_cols, chan_cols, chan_cols, chan_cols, chan_cols,
            chan_cols, chan_cols, chan_cols, P(), P(), P(), chan_rows, chan_cols, chan_cols,
            P("chan"), P(), P(), P("chan"), P(), chan_cols,
        ),
        check_vma=False,
    )
```

time: 788 us -> 138 us (0.18); the launches traced: 779 us -> 138 us
  waiting for transfers between devices: 245 us -> 7.49 us
  blocking collectives: 160 us -> 0 us
  local copies, waits for them, and re-layouts: 171 us -> 28.7 us
  matrix products: 99.6 us -> 0 us
  Pallas kernels: 0 us -> 65.3 us
  other arithmetic: 67.4 us -> 12 us
  between operations: 36.5 us -> 1.77 us
  starting transfers between devices: 0.37 us -> 22.3 us
    psum x2 -> x0, waiting for transfers between devices: 244 us -> none  [local(): lax.psum((grad_w1, grad_w2, grad_w3, grad_bias, grad_small), ('dp', 'chan'))]
    all_gather x13 -> x0, blocking collectives: 145 us -> none  [the longest x5 59.9 us: in_back(): return lax.all_gather(partial_value, 'chan', axis=1, tiled=True)]
    dot_general x57 -> x0, matrix products: 99.6 us -> none  [the longest x15 39.3 us: dot_first(): lax.dot_general(left_mat, right_mat, (((0,), (0,)), ((), ())), preferred_...]
    slice x195 -> x5, local copies, waits for them, and re-layouts: 78.6 us -> 0.1 us  [the longest x1 0.09 us: spread(): single = values[:, :, 0].reshape(-1, frames, 1, 1, 1, 1)]
    pallas_call x0 -> x5, Pallas kernels: none -> 65.3 us  [the longest x1 56.2 us: call_main(): pl.pallas_call(functools.partial(main_kernel, own=own, channels=channels,...]
    reshape x17 -> x0, local copies, waits for them, and re-layouts: 30.9 us -> none  [the longest x5 11.3 us: combine_taps(): shaped = tap_values.reshape(-1, 9, tap_values.shape[1])]
    reduce_sum x24 -> x2, other arithmetic: 24.2 us -> 1.27 us  [the longest x1 0.67 us: local(): extra = jnp.where(me == 0, jnp.sum(counts * cot_logdet), 0.0)]
    ppermute x0 -> x18, starting transfers between devices: none -> 22.3 us  [swap(): return lax.ppermute(values, axis, [(j, j ^ bits) for j in range(size)])]
  transfers between devices with their start and end apart: 3 -> 18, of which waited for: 2 -> 5; matrix products, arithmetic and copies ran while one was open for 9% -> 17% of each run, Pallas kernels for 0% -> 3%
where the time goes in v1:
time: 138 us
  Pallas kernels  65.3 us (47%)
  local copies, waits for them, and re-layouts  28.7 us (21%)
  starting transfers between devices  22.3 us (16%)
  other arithmetic  12 us (9%)
  waiting for transfers between devices  7.49 us (5%)
  between operations  1.77 us (1%)
    pallas_call x1, Pallas kernels, call_main(): pl.pallas_call(functools.partial(main_kernel, own=own, channels=channels,...  56.2 us
    ppermute x18, starting transfers between devices, swap(): return lax.ppermute(values, axis, [(j, j ^ bits) for j in range(size)])  22.3 us
    unnamed x62, local copies, waits for them, and re-layouts  18.1 us
    ppermute x18, waiting for transfers between devices, swap(): return lax.ppermute(values, axis, [(j, j ^ bits) for j in range(size)])  7.49 us
    gt x1, other arithmetic, window_planes(): row > 0  5.02 us
    pallas_call x1, Pallas kernels, local(): pl.pallas_call(functools.partial(update_kernel, channels=channels), out_s...  2.91 us
  transfers between devices with their start and end apart: 18, of which 5 were waited for; matrix products, arithmetic and copies ran while one was open for 17% of the time, Pallas kernels for 3%

profile of v1, /device:TPU:0, one launch (start us, length us, event | category | flops | bytes accessed | tf_op | source)
XLA Modules:
  0.0 137.7 jit_solution(17838004649051958242)
XLA Ops:
  0.7 1.7 %copy.99.w2_ref = f32[512,64]{1,0:T(8,128)} copy(f32[512,64]{0,1:T(8,128)} %param.35) | data formatting | bytes 262144 | tf_op args[7]
  2.4 1.4 %copy.98.w1_ref = f32[64,27]{1,0:T(8,128)} copy(f32[64,27]{0,1:T(8,128)} %param.34) | data formatting | bytes 13824 | tf_op args[6]
  3.8 1.9 %pack_weights.1.pack_ref = f32[64,640]{1,0:T(8,128)} custom-call(f32[64,27]{1,0:T(8,128)} %copy.98.w1_ref, f32[512,64]{1,0:T(8,128)} %copy.99.w2_ref, f32[27,64]{1,0:T(8,128)} %w3_ref.3, f32[2,64]{1,0:T(2,128)} %bias_ref.1, f32[1,64]{1,0:T(1,128)} %bitcast.76), custom_call_target="tpu_custom_call" | custom-call | tf_op jit(solution)/shard_map/pack_weights/pallas_call | solution.py:751
  5.7 2.9 %collective-permute-start = (f32[64,640]{1,0:T(8,128)}, f32[64,640]{1,0:T(8,128)S(1)}, u32[]{:S(2)}, u32[]{:S(2)}) collective-permute-start(f32[64,640]{1,0:T(8,128)} %pack_weights.1.pack_ref), channel_id=1, source_target_pairs={{0,2},{1,3},{2,0},{3,1},{4,6},{5,7},{6,4},{7,5},{8,10},{9,11},{10,... | collective-permute-start | bytes 491528 | tf_op jit(solution)/shard_map/ppermute | solution.py:744
  8.6 1.5 %collective-permute-start.1 = (f32[64,640]{1,0:T(8,128)}, f32[64,640]{1,0:T(8,128)S(1)}, u32[]{:S(2)}, u32[]{:S(2)}) collective-permute-start(f32[64,640]{1,0:T(8,128)} %pack_weights.1.pack_ref), channel_id=1, source_target_pairs={{0,4},{1,5},{2,6},{3,7},{4,0},{5,1},{6,2},{7,3},{8,12},{9,13},{10,... | collective-permute-start | bytes 491528 | tf_op jit(solution)/shard_map/ppermute | solution.py:744
  10.2 0.7 fusion.4
  10.8 0.7 constant_dynamic-update-slice_fusion.4
  13.2 0.8 mul.27
  15.1 1.4 broadcast_in_dim.105
  17.0 1.4 broadcast_in_dim.108
  18.7 5.0 %broadcast_compare_fusion = (pred[1,8192]{1,0:T(4,128)(4,1)S(1)}, s32[1,8192]{1,0:T(1,128)S(1)}, pred[1,8192]{1,0:T(4,128)(4,1)S(1)}, s32[1,8192]{1,0:T(1,128)S(1)}) fusion(s32[1,8192]{1,0:T(1,128)S(1)} %bitcast.63), kind=kLoop, calls=%fused_computation.24 | loop fusion | flops 196608 | bytes 114688 | tf_op jit(solution)/shard_map/gt | solution.py:713
  27.6 1.6 %concatenate.42 = f32[40,8192]{1,0:T(8,128)S(1)} concatenate(f32[3,8192]{1,0:T(4,128)S(1)} %copy-done.3, f32[1,8192]{1,0:T(1,128)S(1)} %broadcast_in_dim.93, f32[3,8192]{1,0:T(4,128)S(1)} %copy-done.3, f32[1,8192]{1,0:T(1,128)S(1)} %broadcast_in_dim.93, f32[3,8192]{1,0:T(4,128)S(1)} %copy-done.4, f32[1,8192]{1,0:T(1,128)S(1)} %broadcast_in_dim.93, f32[3,8192]{1,0:T(4,128)S(1)} %copy-done.4, ...), dimensions={0} | concatenate | bytes 2621440 | tf_op jit(solution)/shard_map/concatenate | solution.py:716
  29.3 0.8 pad_dynamic-slice_fusion.planes_ref
  30.0 0.9 copy-done.2
  30.9 56.2 %flow_block.1 = (f32[4,64,640]{2,1,0:T(8,128)}, f32[4,64,640]{2,1,0:T(8,128)}, f32[8,64,128]{2,1,0:T(8,128)}, f32[8,512]{1,0:T(8,128)}, f32[8,1024]{1,0:T(8,128)}) custom-call(s32[1]{0:T(128)} %bitcast.index_ref, f32[4,64,640]{2,1,0:T(8,128)} %copy-done, f32[4,64,640]{2,1,0:T(8,128)} %copy-done.2, f32[1,512]{1,0:T(1,128)} %bitcast.75, ...), custom_call_target="tpu_custom_call" | custom-call | tf_op jit(solution)/shard_map/flow_block/pallas_call | solution.py:501
  87.6 1.9 %collective-permute-done.8 = f32[4,64,640]{2,1,0:T(8,128)S(1)} collective-permute-done((f32[4,64,640]{2,1,0:T(8,128)}, f32[4,64,640]{2,1,0:T(8,128)S(1)}, u32[]{:S(2)}, u32[]{:S(2)}) %collective-permute-start.8) | collective-permute-done | bytes 655392 | tf_op jit(solution)/shard_map/ppermute | solution.py:744
  89.6 1.2 fusion.8
  90.8 2.1 %collective-permute-start.10 = (bf16[64,640]{1,0:T(8,128)(2,1)S(1)}, bf16[64,640]{1,0:T(8,128)(2,1)S(1)}, u32[]{:S(2)}, u32[]{:S(2)}) collective-permute-start(bf16[64,640]{1,0:T(8,128)(2,1)S(1)} %get-tuple-element.214), channel_id=1, source_target_pairs={{0,4},{1,5},{2,6},{3,7},{4,0},{5,1},{6,2},{7,3},{8,12},{9,13},{10,... | collective-permute-start | bytes 245768 | tf_op jit(solution)/shard_map/ppermute | solution.py:744
  92.9 1.4 %collective-permute-start.11 = (bf16[64,640]{1,0:T(8,128)(2,1)S(1)}, bf16[64,640]{1,0:T(8,128)(2,1)S(1)}, u32[]{:S(2)}, u32[]{:S(2)}) collective-permute-start(bf16[64,640]{1,0:T(8,128)(2,1)S(1)} %get-tuple-element.213), channel_id=1, source_target_pairs={{0,6},{1,7},{2,4},{3,5},{4,2},{5,3},{6,0},{7,1},{8,14},{9,15},{10,... | collective-permute-start | bytes 245768 | tf_op jit(solution)/shard_map/ppermute | solution.py:744
  94.4 1.9 %collective-permute-start.4 = (f32[8,1024]{1,0:T(8,128)S(1)}, f32[8,1024]{1,0:T(8,128)S(1)}, u32[]{:S(2)}, u32[]{:S(2)}) collective-permute-start(f32[8,1024]{1,0:T(8,128)S(1)} %copy-done.14), channel_id=1, source_target_pairs={{0,2},{1,3},{2,0},{3,1},{4,6},{5,7},{6,4},{7,5},{8,10},{9,11},{10,... | collective-permute-start | bytes 98312 | tf_op jit(solution)/shard_map/ppermute | solution.py:744
  96.3 1.5 %collective-permute-start.5 = (f32[8,1024]{1,0:T(8,128)S(1)}, f32[8,1024]{1,0:T(8,128)S(1)}, u32[]{:S(2)}, u32[]{:S(2)}) collective-permute-start(f32[8,1024]{1,0:T(8,128)S(1)} %copy-done.14), channel_id=1, source_target_pairs={{0,4},{1,5},{2,6},{3,7},{4,0},{5,1},{6,2},{7,3},{8,12},{9,13},{10,... | collective-permute-start | bytes 98312 | tf_op jit(solution)/shard_map/ppermute | solution.py:744
  97.9 2.4 %collective-permute-start.6 = (f32[8,1024]{1,0:T(8,128)S(1)}, f32[8,1024]{1,0:T(8,128)S(1)}, u32[]{:S(2)}, u32[]{:S(2)}) collective-permute-start(f32[8,1024]{1,0:T(8,128)S(1)} %copy-done.14), channel_id=1, source_target_pairs={{0,6},{1,7},{2,4},{3,5},{4,2},{5,3},{6,0},{7,1},{8,14},{9,15},{10,... | collective-permute-start | bytes 98312 | tf_op jit(solution)/shard_map/ppermute | solution.py:744
  100.3 1.6 %collective-permute-start.12 = (bf16[64,640]{1,0:T(8,128)(2,1)S(1)}, bf16[64,640]{1,0:T(8,128)(2,1)S(1)}, u32[]{:S(2)}, u32[]{:S(2)}) collective-permute-start(bf16[64,640]{1,0:T(8,128)(2,1)S(1)} %fusion.3), channel_id=1, source_target_pairs={{0,8},{8,0},{16,24},{24,16},{1,9},{9,1},{17,25},{25,17},{2,10},{10... | collective-permute-start | bytes 245768 | tf_op jit(solution)/shard_map/ppermute | solution.py:744
  101.9 0.7 collective-permute-done.6
  102.8 2.0 %collective-permute-done.12 = bf16[64,640]{1,0:T(8,128)(2,1)S(1)} collective-permute-done((bf16[64,640]{1,0:T(8,128)(2,1)S(1)}, bf16[64,640]{1,0:T(8,128)(2,1)S(1)}, u32[]{:S(2)}, u32[]{:S(2)}) %collective-permute-start.12) | collective-permute-done | bytes 81952 | tf_op jit(solution)/shard_map/ppermute | solution.py:744
  104.8 2.7 %collective-permute-start.13 = (bf16[64,640]{1,0:T(8,128)(2,1)S(1)}, bf16[64,640]{1,0:T(8,128)(2,1)S(1)}, u32[]{:S(2)}, u32[]{:S(2)}) collective-permute-start(bf16[64,640]{1,0:T(8,128)(2,1)S(1)} %add_convert_fusion.a_ref), channel_id=1, source_target_pairs={{0,16},{8,24},{16,0},{24,8},{1,17},{9,25},{17,1},{25,9},{2,18},{10... | collective-permute-start | bytes 245768 | tf_op jit(solution)/shard_map/ppermute | solution.py:744
  107.5 1.4 dynamic-slice_bitcast_fusion.cols_ref
  108.9 1.4 %collective-permute-done.13.b_ref = bf16[64,640]{1,0:T(8,128)(2,1)S(1)} collective-permute-done((bf16[64,640]{1,0:T(8,128)(2,1)S(1)}, bf16[64,640]{1,0:T(8,128)(2,1)S(1)}, u32[]{:S(2)}, u32[]{:S(2)}) %collective-permute-start.13) | collective-permute-done | bytes 81952 | tf_op jit(solution)/shard_map/ppermute | solution.py:744
  110.9 1.8 %norm_parts.1 = (f32[64,640]{1,0:T(8,128)}, f32[8,128]{1,0:T(8,128)}) custom-call(s32[1]{0:T(128)} %bitcast.index_ref, bf16[64,640]{1,0:T(8,128)(2,1)} %copy-done.6, bf16[64,640]{1,0:T(8,128)(2,1)} %copy-done.10, f32[64,640]{1,0:T(8,128)} %pack_weights.1.pack_ref, f32[64,128]{1,0:T(8,128)} %dynamic-slice_bitcast_fusion.cols_ref, ...), custom_call_target="tpu_custom_call" | custom-call | tf_op jit(solution)/shard_map/norm_parts/pallas_call | solution.py:804
  112.7 1.4 collective-permute-done.14
  114.1 0.7 add.95
  114.8 0.7 collective-permute-start.15
  115.5 1.8 %collective-permute-start.16 = (f32[8,128]{1,0:T(8,128)S(1)}, f32[8,128]{1,0:T(8,128)S(1)}, u32[]{:S(2)}, u32[]{:S(2)}) collective-permute-start(f32[8,128]{1,0:T(8,128)S(1)} %add.95), channel_id=1, source_target_pairs={{0,4},{1,5},{2,6},{3,7},{4,0},{5,1},{6,2},{7,3},{8,12},{9,13},{10,... | collective-permute-start | bytes 12296 | tf_op jit(solution)/shard_map/ppermute | solution.py:744
  117.2 1.0 collective-permute-start.17
  118.3 0.8 copy.115.m2_ref
  119.1 0.8 copy.116.s2_ref
  119.9 0.7 copy.112.m1_ref
  120.7 0.7 copy.113.s1_ref
  122.0 2.5 %assemble_outputs.1 = (f32[3,8192]{1,0:T(4,128)}, f32[3,8192]{1,0:T(4,128)}, f32[2,4]{1,0:T(2,128)}) custom-call(s32[1]{0:T(128)} %bitcast.index_ref, s32[2]{0:T(128)} %kinds_ref.1, f32[4,8,1024]{2,1,0:T(8,128)} %copy-done.5, f32[4,8,1024]{2,1,0:T(8,128)} %copy-done.9, f32[1,1]{1,0:T(1,128)} %bitcast.20.small_ref), custom_call_target="tpu_custom_call" | custom-call | tf_op jit(solution)/shard_map/assemble_outputs/pallas_call | solution.py:790
  125.2 2.9 %adam_update.1 = (f32[1,1]{1,0:T(1,128)}, f32[64,27]{1,0:T(8,128)}, f32[64,27]{1,0:T(8,128)}, f32[64,27]{1,0:T(8,128)}, f32[512,64]{1,0:T(8,128)}, /*index=5*/f3...) custom-call(f32[4,128]{1,0:T(4,128)} %pad_maximum_fusion.2.totals_re, ...), custom_call_target="tpu_custom_call" | custom-call | tf_op jit(solution)/shard_map/adam_update/pallas_call | solution.py:833
  128.1 1.7 %copy.120 = f32[512,64]{0,1:T(8,128)} copy(f32[512,64]{1,0:T(8,128)} %get-tuple-element.185) | data formatting | bytes 262144
  129.9 1.7 %copy.121 = f32[512,64]{0,1:T(8,128)} copy(f32[512,64]{1,0:T(8,128)} %get-tuple-element.186) | data formatting | bytes 262144
  131.6 1.7 %copy.122 = f32[512,64]{0,1:T(8,128)} copy(f32[512,64]{1,0:T(8,128)} %get-tuple-element.187) | data formatting | bytes 262144
  133.3 1.6 %copy.124 = bf16[512,64]{0,1:T(8,128)(2,1)} copy(bf16[512,64]{1,0:T(8,128)(2,1)} %get-tuple-element.198) | data formatting | bytes 131072
  134.9 0.7 copy.117
  135.6 0.7 copy.118
  136.3 0.7 copy.119
  137.0 0.7 copy.123
  (119 shorter events, 9.5 us)
Async XLA Ops:
  5.7 10.7 %copy-start.15 = (s32[2,4]{1,0:T(2,128)S(1)}, s32[2,4]{1,0:T(2,128)}, u32[]{:S(2)}) copy-start(s32[2,4]{1,0:T(2,128)} %param.30) | copy-start | bytes 100
  5.7 10.8 %copy-start.20 = (f32[2,4]{1,0:T(2,128)S(1)}, f32[2,4]{1,0:T(2,128)}, u32[]{:S(2)}) copy-start(f32[2,4]{1,0:T(2,128)} %param.33) | copy-start | bytes 100
  5.7 19.3 %collective-permute-start = (f32[64,640]{1,0:T(8,128)}, f32[64,640]{1,0:T(8,128)S(1)}, u32[]{:S(2)}, u32[]{:S(2)}) collective-permute-start(f32[64,640]{1,0:T(8,128)} %pack_weights.1.pack_ref), channel_id=1, source_target_pairs={{0,2},{1,3},{2,0},{3,1},{4,6},{5,7},{6,4},{7,5},{8,10},{9,11},{10,... | collective-permute-start | bytes 491528 | tf_op jit(solution)/shard_map/ppermute | solution.py:744
  8.6 16.4 %collective-permute-start.1 = (f32[64,640]{1,0:T(8,128)}, f32[64,640]{1,0:T(8,128)S(1)}, u32[]{:S(2)}, u32[]{:S(2)}) collective-permute-start(f32[64,640]{1,0:T(8,128)} %pack_weights.1.pack_ref), channel_id=1, source_target_pairs={{0,4},{1,5},{2,6},{3,7},{4,0},{5,1},{6,2},{7,3},{8,12},{9,13},{10,... | collective-permute-start | bytes 491528 | tf_op jit(solution)/shard_map/ppermute | solution.py:744
  10.2 14.8 %collective-permute-start.2 = (f32[64,640]{1,0:T(8,128)}, f32[64,640]{1,0:T(8,128)S(1)}, u32[]{:S(2)}, u32[]{:S(2)}) collective-permute-start(f32[64,640]{1,0:T(8,128)} %pack_weights.1.pack_ref), channel_id=1, source_target_pairs={{0,6},{1,7},{2,4},{3,5},{4,2},{5,3},{6,0},{7,1},{8,14},{9,15},{10,... | collective-permute-start | bytes 491528 | tf_op jit(solution)/shard_map/ppermute | solution.py:744
  17.0 7.1 %copy-start.21 = (f32[3,3]{1,0:T(4,128)S(1)}, f32[3,3]{1,0:T(4,128)}, u32[]{:S(2)}) copy-start(f32[3,3]{1,0:T(4,128)} %small_ref.1) | copy-start | bytes 112
  17.0 8.0 %copy-start.1 = (f32[64,640]{1,0:T(8,128)S(1)}, f32[64,640]{1,0:T(8,128)}, u32[]{:S(2)}) copy-start(f32[64,640]{1,0:T(8,128)} %pack_weights.1.pack_ref) | copy-start | bytes 491524
  23.8 2.9 %copy-start.22 = (f32[3]{0:T(128)S(1)}, f32[3]{0:T(128)}, u32[]{:S(2)}) copy-start(f32[3]{0:T(128)} %param.41) | copy-start | bytes 40
  23.9 3.8 %copy-start.3 = (f32[3,8192]{1,0:T(4,128)S(1)}, f32[3,8192]{1,0:T(4,128)}, u32[]{:S(2)}) copy-start(f32[3,8192]{1,0:T(4,128)} %param.28) | copy-start | bytes 294916
  23.9 3.8 %copy-start.4 = (f32[3,8192]{1,0:T(4,128)S(1)}, f32[3,8192]{1,0:T(4,128)}, u32[]{:S(2)}) copy-start(f32[3,8192]{1,0:T(4,128)} %param.31) | copy-start | bytes 294916
  25.1 4.2 %copy-start = (f32[4,64,640]{2,1,0:T(8,128)}, f32[4,64,640]{2,1,0:T(8,128)S(1)}, u32[]{:S(2)}) copy-start(f32[4,64,640]{2,1,0:T(8,128)S(1)} %pad_maximum_fusion.x0_ref) | copy-start | bytes 1966084
  25.1 4.9 %collective-permute-start.3 = (f32[4,64,640]{2,1,0:T(8,128)S(1)}, f32[4,64,640]{2,1,0:T(8,128)S(1)}, u32[]{:S(2)}, u32[]{:S(2)}) collective-permute-start(f32[4,64,640]{2,1,0:T(8,128)S(1)} %pad_maximum_fusion.x0_ref), channel_id=1, source_target_pairs={{0,1},{1,0},{2,3},{3,2},{4,5},{5,4},{6,7},{7,6},{8,9},{9,8},{10,11... | collective-permute-start | bytes 1966088 | tf_op jit(solution)/shard_map/ppermute | solution.py:744
  27.6 1.7 %copy-start.16 = (f32[8,128]{1,0:T(8,128)}, f32[8,128]{1,0:T(8,128)S(1)}, u32[]{:S(2)}) copy-start(f32[8,128]{1,0:T(8,128)S(1)} %scatter.9.small_ref) | copy-start | bytes 12292
  30.0 0.9 copy-start.2
  87.1 2.4 %collective-permute-start.8 = (f32[4,64,640]{2,1,0:T(8,128)}, f32[4,64,640]{2,1,0:T(8,128)S(1)}, u32[]{:S(2)}, u32[]{:S(2)}) collective-permute-start(f32[4,64,640]{2,1,0:T(8,128)} %get-tuple-element.92), channel_id=1, source_target_pairs={{0,1},{1,0},{2,3},{3,2},{4,5},{5,4},{6,7},{7,6},{8,9},{9,8},{10,11... | collective-permute-start | bytes 1966088 | tf_op jit(solution)/shard_map/ppermute | solution.py:744
  89.6 4.9 %copy-start.14 = (f32[8,1024]{1,0:T(8,128)S(1)}, f32[8,1024]{1,0:T(8,128)}, u32[]{:S(2)}) copy-start(f32[8,1024]{1,0:T(8,128)} %get-tuple-element.87) | copy-start | bytes 98308
  90.7 27.5 %copy-start.7 = (f32[512,64]{0,1:T(8,128)S(1)}, f32[512,64]{0,1:T(8,128)}, u32[]{:S(2)}) copy-start(f32[512,64]{0,1:T(8,128)} %param.44) | copy-start | bytes 393220
  90.8 28.3 %copy-start.8 = (f32[512,64]{0,1:T(8,128)S(1)}, f32[512,64]{0,1:T(8,128)}, u32[]{:S(2)}) copy-start(f32[512,64]{0,1:T(8,128)} %param.45) | copy-start | bytes 393220
  90.8 29.2 %copy-start.17 = (f32[64,27]{0,1:T(8,128)S(1)}, f32[64,27]{0,1:T(8,128)}, u32[]{:S(2)}) copy-start(f32[64,27]{0,1:T(8,128)} %param.42) | copy-start | bytes 20740
  90.8 29.9 %copy-start.18 = (f32[64,27]{0,1:T(8,128)S(1)}, f32[64,27]{0,1:T(8,128)}, u32[]{:S(2)}) copy-start(f32[64,27]{0,1:T(8,128)} %param.43) | copy-start | bytes 20740
  90.8 7.0 %collective-permute-start.10 = (bf16[64,640]{1,0:T(8,128)(2,1)S(1)}, bf16[64,640]{1,0:T(8,128)(2,1)S(1)}, u32[]{:S(2)}, u32[]{:S(2)}) collective-permute-start(bf16[64,640]{1,0:T(8,128)(2,1)S(1)} %get-tuple-element.214), channel_id=1, source_target_pairs={{0,4},{1,5},{2,6},{3,7},{4,0},{5,1},{6,2},{7,3},{8,12},{9,13},{10,... | collective-permute-start | bytes 245768 | tf_op jit(solution)/shard_map/ppermute | solution.py:744
  92.9 7.4 %collective-permute-start.11 = (bf16[64,640]{1,0:T(8,128)(2,1)S(1)}, bf16[64,640]{1,0:T(8,128)(2,1)S(1)}, u32[]{:S(2)}, u32[]{:S(2)}) collective-permute-start(bf16[64,640]{1,0:T(8,128)(2,1)S(1)} %get-tuple-element.213), channel_id=1, source_target_pairs={{0,6},{1,7},{2,4},{3,5},{4,2},{5,3},{6,0},{7,1},{8,14},{9,15},{10,... | collective-permute-start | bytes 245768 | tf_op jit(solution)/shard_map/ppermute | solution.py:744
  94.3 5.9 %collective-permute-start.9 = (bf16[64,640]{1,0:T(8,128)(2,1)S(1)}, bf16[64,640]{1,0:T(8,128)(2,1)S(1)}, u32[]{:S(2)}, u32[]{:S(2)}) collective-permute-start(bf16[64,640]{1,0:T(8,128)(2,1)S(1)} %get-tuple-element.212), channel_id=1, source_target_pairs={{0,2},{1,3},{2,0},{3,1},{4,6},{5,7},{6,4},{7,5},{8,10},{9,11},{10,... | collective-permute-start | bytes 245768 | tf_op jit(solution)/shard_map/ppermute | solution.py:744
  94.4 7.5 %collective-permute-start.4 = (f32[8,1024]{1,0:T(8,128)S(1)}, f32[8,1024]{1,0:T(8,128)S(1)}, u32[]{:S(2)}, u32[]{:S(2)}) collective-permute-start(f32[8,1024]{1,0:T(8,128)S(1)} %copy-done.14), channel_id=1, source_target_pairs={{0,2},{1,3},{2,0},{3,1},{4,6},{5,7},{6,4},{7,5},{8,10},{9,11},{10,... | collective-permute-start | bytes 98312 | tf_op jit(solution)/shard_map/ppermute | solution.py:744
  96.3 5.6 %collective-permute-start.5 = (f32[8,1024]{1,0:T(8,128)S(1)}, f32[8,1024]{1,0:T(8,128)S(1)}, u32[]{:S(2)}, u32[]{:S(2)}) collective-permute-start(f32[8,1024]{1,0:T(8,128)S(1)} %copy-done.14), channel_id=1, source_target_pairs={{0,4},{1,5},{2,6},{3,7},{4,0},{5,1},{6,2},{7,3},{8,12},{9,13},{10,... | collective-permute-start | bytes 98312 | tf_op jit(solution)/shard_map/ppermute | solution.py:744
  97.9 4.8 %collective-permute-start.6 = (f32[8,1024]{1,0:T(8,128)S(1)}, f32[8,1024]{1,0:T(8,128)S(1)}, u32[]{:S(2)}, u32[]{:S(2)}) collective-permute-start(f32[8,1024]{1,0:T(8,128)S(1)} %copy-done.14), channel_id=1, source_target_pairs={{0,6},{1,7},{2,4},{3,5},{4,2},{5,3},{6,0},{7,1},{8,14},{9,15},{10,... | collective-permute-start | bytes 98312 | tf_op jit(solution)/shard_map/ppermute | solution.py:744
  100.3 4.5 %collective-permute-start.12 = (bf16[64,640]{1,0:T(8,128)(2,1)S(1)}, bf16[64,640]{1,0:T(8,128)(2,1)S(1)}, u32[]{:S(2)}, u32[]{:S(2)}) collective-permute-start(bf16[64,640]{1,0:T(8,128)(2,1)S(1)} %fusion.3), channel_id=1, source_target_pairs={{0,8},{8,0},{16,24},{24,16},{1,9},{9,1},{17,25},{25,17},{2,10},{10... | collective-permute-start | bytes 245768 | tf_op jit(solution)/shard_map/ppermute | solution.py:744
  102.7 18.7 %copy-start.5 = (f32[4,8,1024]{2,1,0:T(8,128)}, f32[4,8,1024]{2,1,0:T(8,128)S(1)}, u32[]{:S(2)}) copy-start(f32[4,8,1024]{2,1,0:T(8,128)S(1)} %pad_maximum_fusion.1.p0_ref) | copy-start | bytes 393220
  102.7 18.6 %collective-permute-start.7 = (f32[4,8,1024]{2,1,0:T(8,128)S(1)}, f32[4,8,1024]{2,1,0:T(8,128)S(1)}, u32[]{:S(2)}, u32[]{:S(2)}) collective-permute-start(f32[4,8,1024]{2,1,0:T(8,128)S(1)} %pad_maximum_fusion.1.p0_ref), channel_id=1, source_target_pairs={{0,1},{1,0},{2,3},{3,2},{4,5},{5,4},{6,7},{7,6},{8,9},{9,8},{10,11... | collective-permute-start | bytes 393224 | tf_op jit(solution)/shard_map/ppermute | solution.py:744
  104.8 5.4 %copy-start.6 = (bf16[64,640]{1,0:T(8,128)(2,1)}, bf16[64,640]{1,0:T(8,128)(2,1)S(1)}, u32[]{:S(2)}) copy-start(bf16[64,640]{1,0:T(8,128)(2,1)S(1)} %add_convert_fusion.a_ref) | copy-start | bytes 245764
  104.8 5.4 %collective-permute-start.13 = (bf16[64,640]{1,0:T(8,128)(2,1)S(1)}, bf16[64,640]{1,0:T(8,128)(2,1)S(1)}, u32[]{:S(2)}, u32[]{:S(2)}) collective-permute-start(bf16[64,640]{1,0:T(8,128)(2,1)S(1)} %add_convert_fusion.a_ref), channel_id=1, source_target_pairs={{0,16},{8,24},{16,0},{24,8},{1,17},{9,25},{17,1},{25,9},{2,18},{10... | collective-permute-start | bytes 245768 | tf_op jit(solution)/shard_map/ppermute | solution.py:744
  110.2 0.6 copy-start.10
  112.7 1.4 %collective-permute-start.14 = (f32[8,128]{1,0:T(8,128)}, f32[8,128]{1,0:T(8,128)S(1)}, u32[]{:S(2)}, u32[]{:S(2)}) collective-permute-start(f32[8,128]{1,0:T(8,128)} %get-tuple-element.95), channel_id=1, source_target_pairs={{0,1},{1,0},{2,3},{3,2},{4,5},{5,4},{6,7},{7,6},{8,9},{9,8},{10,11... | collective-permute-start | bytes 12296 | tf_op jit(solution)/shard_map/ppermute | solution.py:744
  114.8 9.7 %collective-permute-start.15 = (f32[8,128]{1,0:T(8,128)S(1)}, f32[8,128]{1,0:T(8,128)S(1)}, u32[]{:S(2)}, u32[]{:S(2)}) collective-permute-start(f32[8,128]{1,0:T(8,128)S(1)} %add.95), channel_id=1, source_target_pairs={{0,2},{1,3},{2,0},{3,1},{4,6},{5,7},{6,4},{7,5},{8,10},{9,11},{10,... | collective-permute-start | bytes 12296 | tf_op jit(solution)/shard_map/ppermute | solution.py:744
  115.5 9.0 %collective-permute-start.16 = (f32[8,128]{1,0:T(8,128)S(1)}, f32[8,128]{1,0:T(8,128)S(1)}, u32[]{:S(2)}, u32[]{:S(2)}) collective-permute-start(f32[8,128]{1,0:T(8,128)S(1)} %add.95), channel_id=1, source_target_pairs={{0,4},{1,5},{2,6},{3,7},{4,0},{5,1},{6,2},{7,3},{8,12},{9,13},{10,... | collective-permute-start | bytes 12296 | tf_op jit(solution)/shard_map/ppermute | solution.py:744
  117.2 7.3 %collective-permute-start.17 = (f32[8,128]{1,0:T(8,128)S(1)}, f32[8,128]{1,0:T(8,128)S(1)}, u32[]{:S(2)}, u32[]{:S(2)}) collective-permute-start(f32[8,128]{1,0:T(8,128)S(1)} %add.95), channel_id=1, source_target_pairs={{0,6},{1,7},{2,4},{3,5},{4,2},{5,3},{6,0},{7,1},{8,14},{9,15},{10,... | collective-permute-start | bytes 12296 | tf_op jit(solution)/shard_map/ppermute | solution.py:744
  121.3 0.7 copy-start.9
  128.1 6.9 %copy-start.13 = (f32[64,27]{1,0:T(8,128)S(1)}, f32[64,27]{1,0:T(8,128)}, u32[]{:S(2)}) copy-start(f32[64,27]{1,0:T(8,128)} %get-tuple-element.182) | copy-start | bytes 20740
  128.1 7.5 %copy-start.12 = (f32[64,27]{1,0:T(8,128)S(1)}, f32[64,27]{1,0:T(8,128)}, u32[]{:S(2)}) copy-start(f32[64,27]{1,0:T(8,128)} %get-tuple-element.183) | copy-start | bytes 20740
  128.1 8.2 %copy-start.11 = (f32[64,27]{1,0:T(8,128)S(1)}, f32[64,27]{1,0:T(8,128)}, u32[]{:S(2)}) copy-start(f32[64,27]{1,0:T(8,128)} %get-tuple-element.184) | copy-start | bytes 20740
  128.1 8.9 %copy-start.19 = (bf16[64,27]{1,0:T(8,128)(2,1)S(1)}, bf16[64,27]{1,0:T(8,128)(2,1)}, u32[]{:S(2)}) copy-start(bf16[64,27]{1,0:T(8,128)(2,1)} %get-tuple-element.197) | copy-start | bytes 10372

commit v2 on v1

--- a/solution.py
+++ b/solution.py
@@ -69,9 +69,9 @@
 
 
 def pack_kernel(w1_ref, w2_ref, w3_ref, bias_ref, u1_ref, out_ref):
-    channels = w2_ref.shape[0]
-    out_ref[:, 0:channels] = w2_ref[...].T
-    tile = dot_nn(w1_ref[...], spread_one(), HIGH) + dot_tn(w3_ref[...], spread_three(), HIGH)
+    channels = w2_ref.shape[1]
+    out_ref[:, 0:channels] = w2_ref[...]
+    tile = dot_tn(w1_ref[...], spread_one(), HIGH) + dot_tn(w3_ref[...], spread_three(), HIGH)
     lane = iota((1, LANES), 1)
     for index, row in enumerate((u1_ref[...], bias_ref[0:1, :], bias_ref[1:2, :])):
         column = jnp.broadcast_to(row, (8, row.shape[1])).T[:, 0:1]
@@ -119,7 +119,7 @@
 
 
 def main_kernel(
-    index_ref, x0_ref, x1_ref, u2_ref, u3_ref, planes_ref, small_ref,
+    index_ref, u3_ref, x0_ref, x1_ref, u2_ref, planes_ref, small_ref,
     keep_ref, send_ref, cols_ref, rows_ref, og_ref,
     w_s, w13_s, w2_s, w2t_s, wout_s, bias_s, taps_s, sl1_s, sl2_s, cv1_s, cv2_s,
     lin1_s, lin2_s, gt1_s, gt2_s, acc1_s, acc2_s, tan1_s, tan2_s, g1_s, g2_s, hid1_s, hid2_s,
@@ -143,7 +143,9 @@
     head = (lane % 8 == 4) & (lane < TAP_ROWS)
     u1 = tile[:, TAP_ROWS : TAP_ROWS + 1]
     u2 = u2_ref[...]
-    u3 = u3_ref[...]
+    u3 = jnp.zeros((1, LANES), F32)
+    for o in range(3):
+        u3 = jnp.where(is_three & (lane % 8 == 4 + o), u3_ref[o], u3)
     for _ in range(2):
         v1 = all_sum(taps_one * u1, axis=0)
         v2 = all_sum(w2t * u2, axis=1)
@@ -455,7 +457,7 @@
         send_ref[m] = w_s[block + 1 - core]
 
 
-def call_main(me, x0, x1, u2, u3, planes, small, own, channels, chips):
+def call_main(me, u3, x0, x1, u2, planes, small, own, channels, chips):
     rows_own = channels // (2 * chips)
     region = own + 2 * HALO
     wide = own + 2 * BLOCK
@@ -501,12 +503,12 @@
     return pl.pallas_call(
         functools.partial(main_kernel, own=own, channels=channels, chips=chips),
         out_shape=out_shape,
-        in_specs=[pl.BlockSpec(memory_space=pltpu.SMEM)] + [full] * 6,
+        in_specs=[pl.BlockSpec(memory_space=pltpu.SMEM)] * 2 + [full] * 5,
         out_specs=[full] * 5,
         scratch_shapes=scratch,
         compiler_params=pltpu.CompilerParams(vmem_limit_bytes=63 * 1024 * 1024),
         name="flow_block",
-    )(me, x0, x1, u2, u3, planes, small)
+    )(me, u3, x0, x1, u2, planes, small)
 
 
 def assemble_kernel(index_ref, kinds_ref, p0_ref, p1_ref, small_ref, z_ref, gin_ref, logdet_ref, dens_s, *, own, chips, frames):
@@ -519,7 +521,7 @@
             z_ref[:, lanes] = piece[0:3]
             gin_ref[:, lanes] = piece[4:7]
             dens_s[:, lanes] = piece[3:4]
-    scale_sum = small_ref[0, 0]
+    scale_sum = small_ref[1, 0] + small_ref[1, 1] + small_ref[1, 2]
     pixel = iota((1, FRAME), 1)
     bottom = (pixel // (WIDTH * 32)) % 2
     right = (pixel // 32) % 2
@@ -642,8 +644,8 @@
     fixed_one = jnp.where(is_one, scales[0][0] * (tile - scales[0][1] * outer_one) * clip, 0.0)
     fixed_two = scales[1][0] * (grad[:, 0:channels] - scales[1][1] * outer_two) * clip
     fixed_three = jnp.where(is_three, scales[2][0] * (tile - scales[2][1] * outer_three) * clip, 0.0)
-    grad_one = dot_nt(fixed_one, spread_one(), HIGH)
-    grad_two = fixed_two.T
+    grad_one = dot_nt(spread_one(), fixed_one, HIGH)
+    grad_two = fixed_two
     grad_three = dot_nt(spread_three(), fixed_three, HIGH)
 
     for grad_j, w_ref, m_ref, s_ref, nw, nm, ns, lw in (
@@ -689,36 +691,67 @@
     u3_out[...] = rows_ref[2:3, 4:7]
 
 
-def window_planes(images, frame_kinds, series_len, probes, cot_z, cot_logdet, first, region):
-    frames = frame_kinds.shape[0]
-    pixels = images.shape[1]
-    position = lax.iota(jnp.int32, pixels)
-    kind = jnp.broadcast_to(frame_kinds[:, None], (frames, FRAME)).reshape(pixels)
-    limit = jnp.where(kind == 1, 64, 32)
-    row = (position // WIDTH) % limit
-    col = position % limit
-
-    def spread(values):
-        quads = jnp.broadcast_to(values.reshape(-1, frames, 2, 1, 2, 1), (values.shape[0], frames, 2, 32, 2, 32))
-        single = values[:, :, 0].reshape(-1, frames, 1, 1, 1, 1)
-        picked = jnp.where(frame_kinds.reshape(1, frames, 1, 1, 1, 1) == 2, quads, single)
-        return picked.reshape(values.shape[0], pixels)
-
-    coefs = []
+def prepare_kernel(
+    index_ref, kinds_ref, len_ref, cot_ref, params_ref, images_ref, probes_ref, cot_z_ref,
+    planes_ref, small_ref, *, own, frames,
+):
+    region = planes_ref.shape[1]
+    pixels = images_ref.shape[1]
+    me = index_ref[0]
+    first = me * own - HALO
+    planes_ref[...] = jnp.zeros(planes_ref.shape, F32)
+    for chunk in range(region // LANES):
+        start = first + chunk * LANES
+        source = pl.ds(pl.multiple_of(jnp.clip(start, 0, pixels - LANES), LANES), LANES)
+        lanes = pl.ds(chunk * LANES, LANES)
+        inside = (start >= 0) & (start < pixels)
+        for row, ref in ((0, images_ref), (4, images_ref), (8, probes_ref), (12, probes_ref), (20, cot_z_ref)):
+            planes_ref[row : row + 3, lanes] = jnp.where(inside, ref[:, source], 0.0)
+
+    position = first + iota((1, region), 1)
+    frame = jnp.right_shift(position, 12)
+    pixel = jnp.bitwise_and(position, FRAME - 1)
+    row = jnp.right_shift(pixel, 6)
+    col = jnp.bitwise_and(pixel, WIDTH - 1)
+    half = WIDTH // 2
+    quad = 2 * jnp.right_shift(row, 5) + jnp.right_shift(col, 5)
+    split = jnp.zeros((1, region), jnp.int32)
+    for f in range(frames):
+        split = jnp.where(frame == f, jnp.where(kinds_ref[f] == 2, 1, 0), split)
+    slot = 4 * frame + jnp.where(split == 1, quad, 0)
+    length = jnp.zeros((1, region), jnp.int32)
+    weight = jnp.zeros((1, region), F32)
+    for f in range(frames):
+        for q in range(4):
+            here = slot == 4 * f + q
+            length = jnp.where(here, len_ref[f, q], length)
+            weight = jnp.where(here, cot_ref[f, q], weight)
     for k in range(NMAX):
-        term = (-1.0) ** k / (k + 1)
-        coefs.append(jnp.where(series_len >= k + 1, term, 0.0).astype(F32))
-    coefs = jnp.stack(coefs)
-    coefs = spread(jnp.concatenate([coefs, coefs * cot_logdet[None]], axis=0))
-    masks = jnp.stack([row > 0, row < limit - 1, col > 0, col < limit - 1]).astype(F32)
-    blank1 = jnp.zeros((1, pixels), F32)
-    blank4 = jnp.zeros((4, pixels), F32)
-    planes = jnp.concatenate(
-        [images, blank1, images, blank1, probes, blank1, probes, blank1, blank4, cot_z, blank1, coefs, masks, blank4],
-        axis=0,
-    )
-    planes = jnp.pad(planes, ((0, 0), (HALO, HALO)))
-    return lax.dynamic_slice_in_dim(planes, first, region, 1)
+        coef = jnp.where(length >= k + 1, (-1.0) ** k / (k + 1), 0.0)
+        planes_ref[24 + k : 25 + k] = coef
+        planes_ref[24 + NMAX + k : 25 + NMAX + k] = coef * weight
+    for index, line in enumerate((row, col)):
+        low = (line == 0) | ((split == 1) & (line == half))
+        high = (line == WIDTH - 1) | ((split == 1) & (line == half - 1))
+        planes_ref[32 + 2 * index : 33 + 2 * index] = jnp.where(low, 0.0, 1.0)
+        planes_ref[33 + 2 * index : 34 + 2 * index] = jnp.where(high, 0.0, 1.0)
+
+    extra = jnp.float32(0.0)
+    for f in range(frames):
+        whole = 4096.0 * cot_ref[f, 0]
+        quads = 1024.0 * (cot_ref[f, 0] + cot_ref[f, 1] + cot_ref[f, 2] + cot_ref[f, 3])
+        extra = extra + jnp.where(kinds_ref[f] == 2, quads, whole)
+    extra = jnp.where(me == 0, extra, 0.0)
+    row8 = iota((8, LANES), 0)
+    lane = iota((8, LANES), 1)
+    values = []
+    for a in range(3):
+        value = jnp.zeros((8, LANES), F32)
+        for i in range(3):
+            value = jnp.where(row8 % 4 == i, params_ref[a, i], value)
+        values.append(value)
+    result = jnp.where(lane == 0, values[0], jnp.where(lane == 1, jnp.exp(values[1]), values[2]))
+    small_ref[...] = jnp.where(row8 % 4 == 3, 0.0, jnp.where(lane == 3, extra, result))
 
 
 def local(
@@ -754,23 +787,22 @@
         in_specs=[full] * 5,
         out_specs=full,
         name="pack_weights",
-    )(weight1, weight2, weight3, biases, power_u1.reshape(1, rows_own))
+    )(weight1.T, weight2.T, weight3, biases, power_u1.reshape(1, rows_own))
     x0, x1 = gather_shards(pack)
 
-    u3_row = jnp.tile(jnp.concatenate([jnp.zeros((4,), F32), power_u3, jnp.zeros((1,), F32)]), LANES // 8)
-    planes = window_planes(
-        images, frame_kinds, series_len, probes, cot_z, cot_logdet, me * own, own + 2 * HALO
-    )
-    slots = lax.broadcasted_iota(jnp.int32, (frames, 4), 1)
-    counts = jnp.where(frame_kinds[:, None] == 2, 1024.0, jnp.where(slots == 0, 4096.0, 0.0))
-    extra = jnp.where(me == 0, jnp.sum(counts * cot_logdet), 0.0)
-    columns = jnp.stack(
-        [small_params[0], jnp.exp(small_params[1]), small_params[2], jnp.broadcast_to(extra, (3,))], axis=1
-    )
-    small = jnp.zeros((8, LANES), F32).at[0:3, 0:4].set(columns).at[4:7, 0:4].set(columns)
+    planes, small = pl.pallas_call(
+        functools.partial(prepare_kernel, own=own, frames=frames),
+        out_shape=(
+            jax.ShapeDtypeStruct((40, own + 2 * HALO), F32),
+            jax.ShapeDtypeStruct((8, LANES), F32),
+        ),
+        in_specs=[smem] * 5 + [full] * 3,
+        out_specs=[full] * 2,
+        name="prepare_planes",
+    )(index, frame_kinds, series_len, cot_logdet, small_params, images, probes, cot_z)
 
     keep, send, cols, rows, og = call_main(
-        index, x0, x1, power_u2.reshape(1, channels), u3_row.reshape(1, LANES), planes, small, own, channels, chips
+        index, power_u3, x0, x1, power_u2.reshape(1, channels), planes, small, own, channels, chips
     )
 
     got = swap(send, "chan", shards, 1)
@@ -779,7 +811,7 @@
     total = summed[0]
     for m in range(1, chips):
         total = total + swap(low[m], "chan", shards, 2 * m).astype(F32)
-    half = total.astype(BF16)
+    og, half = lax.optimization_barrier((og, total.astype(BF16)))
     bits = 1
     while 2 * bits < replicas:
         half = (half.astype(F32) + swap(half, "dp", replicas, bits).astype(F32)).astype(BF16)
@@ -798,7 +830,7 @@
         out_specs=[full] * 3,
         scratch_shapes=[pltpu.VMEM((1, pixels), F32)],
         name="assemble_outputs",
-    )(index, frame_kinds, p0, p1, jnp.sum(small_params[1]).reshape(1, 1))
+    )(index, frame_kinds, p0, p1, small_params)
 
     cols_own = lax.dynamic_index_in_dim(cols, me, 0, False)
     grad, parts = pl.pallas_call(
@@ -820,12 +852,12 @@
 
     out_shape = (
         [jax.ShapeDtypeStruct((1, 1), F32)]
-        + [like(weight1)] * 3
-        + [like(weight2)] * 3
+        + [like(weight1.T)] * 3
+        + [like(weight2.T)] * 3
         + [like(weight3)] * 3
         + [like(biases)] * 3
         + [like(small_params)] * 3
-        + [like(weight1, BF16), like(weight2, BF16), like(weight3, BF16)]
+        + [like(weight1.T, BF16), like(weight2.T, BF16), like(weight3, BF16)]
         + [jax.ShapeDtypeStruct((1, rows_own), F32), jax.ShapeDtypeStruct((1, 27), F32)]
         + [jax.ShapeDtypeStruct((1, channels), F32), jax.ShapeDtypeStruct((1, rows_own), F32)]
         + [jax.ShapeDtypeStruct((1, 3), F32), jax.ShapeDtypeStruct((9, rows_own), F32)]
@@ -838,10 +870,12 @@
         name="adam_update",
     )(
         totals, grad, cols_own, rows,
-        weight1, moment_w1, second_w1, weight2, moment_w2, second_w2, weight3, moment_w3, second_w3,
-        moment_bias, second_bias, small_params, moment_small, second_small,
-    )
-    norm, updates, vectors = done[0], done[1:19], done[19:]
+        weight1.T, moment_w1.T, second_w1.T, weight2.T, moment_w2.T, second_w2.T,
+        weight3, moment_w3, second_w3, moment_bias, second_bias, small_params, moment_small, second_small,
+    )
+    norm, updates, vectors = done[0], list(done[1:19]), done[19:]
+    for slot in (0, 1, 2, 3, 4, 5, 15, 16):
+        updates[slot] = updates[slot].T
     return (
         z_out,
         logdet,

time: 138 us -> 116 us (0.84)
  local copies, waits for them, and re-layouts: 28.7 us -> 4.29 us
  waiting for transfers between devices: 7.49 us -> 20.9 us
  other arithmetic: 12 us -> 3.5 us
  starting transfers between devices: 22.3 us -> 19.7 us
    unnamed x62 -> x14, local copies, waits for them, and re-layouts: 18.1 us -> 2.9 us
    ppermute x18, waiting for transfers between devices: 7.49 us -> 20.9 us  [swap(): return lax.ppermute(values, axis, [(j, j ^ bits) for j in range(size)])]
    gt x1 -> x0, other arithmetic: 5.02 us -> none  [window_planes(): row > 0]
    broadcast_in_dim x10 -> x0, local copies, waits for them, and re-layouts: 3.84 us -> none  [the longest x5 2 us: spread(): jnp.where(frame_kinds.reshape(1, frames, 1, 1, 1, 1) == 2, quads, single)]
    ppermute x18, starting transfers between devices: 22.3 us -> 19.7 us  [swap(): return lax.ppermute(values, axis, [(j, j ^ bits) for j in range(size)])]
    concatenate x10 -> x0, local copies, waits for them, and re-layouts: 2.47 us -> none  [the longest x1 1.6 us: window_planes(): jnp.concatenate([images, blank1, images, blank1, probes, blank1, probes,...]
    pallas_call x0 -> x1, Pallas kernels: none -> 2.22 us  [local(): pl.pallas_call(functools.partial(prepare_kernel, own=own, frames=frames),...]
  transfers between devices with their start and end apart: 18 -> 18, of which waited for: 5 -> 11; matrix products, arithmetic and copies ran while one was open for 17% -> 2% of each run, Pallas kernels for 3% -> 5%
where the time goes in v2:
time: 116 us
  Pallas kernels  66.4 us (57%)
  waiting for transfers between devices  20.9 us (18%)
  starting transfers between devices  19.7 us (17%)
  local copies, waits for them, and re-layouts  4.29 us (4%)
  other arithmetic  3.5 us (3%)
    pallas_call x1, Pallas kernels, call_main(): pl.pallas_call(functools.partial(main_kernel, own=own, channels=channels,...  56.1 us
    ppermute x18, waiting for transfers between devices, swap(): return lax.ppermute(values, axis, [(j, j ^ bits) for j in range(size)])  20.9 us
    ppermute x18, starting transfers between devices, swap(): return lax.ppermute(values, axis, [(j, j ^ bits) for j in range(size)])  19.7 us
    unnamed x14, local copies, waits for them, and re-layouts  2.9 us
    pallas_call x1, Pallas kernels, local(): pl.pallas_call(functools.partial(update_kernel, channels=channels), out_s...  2.57 us
  transfers between devices with their start and end apart: 18, of which 11 were waited for; matrix products, arithmetic and copies ran while one was open for 2% of the time, Pallas kernels for 5%

profile of v2, /device:TPU:0, one launch (start us, length us, event | category | flops | bytes accessed | tf_op | source)
XLA Modules:
  0.0 115.8 jit_solution(5607182250270884756)
XLA Ops:
  0.7 1.8 %pack_weights.1.pack_ref = f32[64,640]{1,0:T(8,128)} custom-call(f32[27,64]{1,0:T(8,128)} %bitcast.57, f32[64,512]{1,0:T(8,128)} %bitcast.50, f32[27,64]{1,0:T(8,128)} %w3_ref.3, f32[2,64]{1,0:T(2,128)} %bias_ref.1, f32[1,64]{1,0:T(1,128)} %bitcast.66), custom_call_target="tpu_custom_call" | custom-call | tf_op jit(solution)/shard_map/pack_weights/pallas_call | solution.py:784
  2.5 2.9 %collective-permute-start = (f32[64,640]{1,0:T(8,128)}, f32[64,640]{1,0:T(8,128)S(1)}, u32[]{:S(2)}, u32[]{:S(2)}) collective-permute-start(f32[64,640]{1,0:T(8,128)} %pack_weights.1.pack_ref), channel_id=1, source_target_pairs={{0,2},{1,3},{2,0},{3,1},{4,6},{5,7},{6,4},{7,5},{8,10},{9,11},{10,... | collective-permute-start | bytes 491528 | tf_op jit(solution)/shard_map/ppermute | solution.py:777
  5.4 1.5 %collective-permute-start.1 = (f32[64,640]{1,0:T(8,128)}, f32[64,640]{1,0:T(8,128)S(1)}, u32[]{:S(2)}, u32[]{:S(2)}) collective-permute-start(f32[64,640]{1,0:T(8,128)} %pack_weights.1.pack_ref), channel_id=1, source_target_pairs={{0,4},{1,5},{2,6},{3,7},{4,0},{5,1},{6,2},{7,3},{8,12},{9,13},{10,... | collective-permute-start | bytes 491528 | tf_op jit(solution)/shard_map/ppermute | solution.py:777
  7.0 3.7 %collective-permute-done = f32[64,640]{1,0:T(8,128)S(1)} collective-permute-done((f32[64,640]{1,0:T(8,128)}, f32[64,640]{1,0:T(8,128)S(1)}, u32[]{:S(2)}, u32[]{:S(2)}) %collective-permute-start) | collective-permute-done | bytes 163872 | tf_op jit(solution)/shard_map/ppermute | solution.py:777
  10.7 4.1 %collective-permute-done.1 = f32[64,640]{1,0:T(8,128)S(1)} collective-permute-done((f32[64,640]{1,0:T(8,128)}, f32[64,640]{1,0:T(8,128)S(1)}, u32[]{:S(2)}, u32[]{:S(2)}) %collective-permute-start.1) | collective-permute-done | bytes 163872 | tf_op jit(solution)/shard_map/ppermute | solution.py:777
  14.8 0.0 collective-permute-done.2
  14.8 1.0 pad_maximum_fusion.x0_ref
  15.8 0.1 collective-permute-start.3
  15.9 2.2 %prepare_planes.1 = (f32[40,2048]{1,0:T(8,128)}, f32[8,128]{1,0:T(8,128)}) custom-call(s32[1]{0:T(128)} %bitcast.index_ref, s32[2]{0:T(128)} %kinds_ref.3, s32[2,4]{1,0:T(2,128)} %len_ref.1, f32[2,4]{1,0:T(2,128)} %cot_ref.1, f32[3,3]{1,0:T(4,128)} %small_ref.3, f32[3,8192]{1,0:T(4,128)} %images_ref.1, f32[3,8192]{1,0:T(4,128)} %probes_ref.1, ...), custom_call_target="tpu_custom_call" | custom-call | tf_op jit(solution)/shard_map/prepare_planes/pallas_call | solution.py:793
  18.1 0.9 copy-done.1
  19.0 56.1 %flow_block.1 = (f32[4,64,640]{2,1,0:T(8,128)}, f32[4,64,640]{2,1,0:T(8,128)}, f32[8,64,128]{2,1,0:T(8,128)}, f32[8,512]{1,0:T(8,128)}, f32[8,1024]{1,0:T(8,128)}) custom-call(s32[1]{0:T(128)} %bitcast.index_ref, f32[3]{0:T(128)} %u3_ref.1, f32[4,64,640]{2,1,0:T(8,128)} %copy-done, f32[4,64,640]{2,1,0:T(8,128)} %copy-done.1, f32[1,512]{1,0:T(1,128)} %bitcast.65, ...), custom_call_target="tpu_custom_call" | custom-call | tf_op jit(solution)/shard_map/flow_block/pallas_call | solution.py:503
  75.1 0.4 collective-permute-start.4
  75.5 1.9 %collective-permute-done.4 = f32[4,64,640]{2,1,0:T(8,128)S(1)} collective-permute-done((f32[4,64,640]{2,1,0:T(8,128)}, f32[4,64,640]{2,1,0:T(8,128)S(1)}, u32[]{:S(2)}, u32[]{:S(2)}) %collective-permute-start.4) | collective-permute-done | bytes 655392 | tf_op jit(solution)/shard_map/ppermute | solution.py:777
  77.4 1.2 %fusion.4 = (bf16[4,64,640]{2,1,0:T(8,128)(2,1)S(1)}, f32[4,64,640]{2,1,0:T(8,128)S(1)}) fusion(f32[4,64,640]{2,1,0:T(8,128)} %get-tuple-element.70, f32[4,64,640]{2,1,0:T(8,128)S(1)} %collective-permute-done.4), kind=kLoop, calls=%fused_computation.13 | loop fusion | flops 327680 | bytes 2293760 | tf_op jit(solution)/shard_map/convert_element_type | solution.py:810
  78.6 1.3 %collective-permute-start.5 = (bf16[64,640]{1,0:T(8,128)(2,1)S(1)}, bf16[64,640]{1,0:T(8,128)(2,1)S(1)}, u32[]{:S(2)}, u32[]{:S(2)}) collective-permute-start(bf16[64,640]{1,0:T(8,128)(2,1)S(1)} %get-tuple-element.108), channel_id=1, source_target_pairs={{0,2},{1,3},{2,0},{3,1},{4,6},{5,7},{6,4},{7,5},{8,10},{9,11},{10,... | collective-permute-start | bytes 245768 | tf_op jit(solution)/shard_map/ppermute | solution.py:777
  79.9 0.8 collective-permute-start.6
  80.8 1.4 %collective-permute-start.7 = (bf16[64,640]{1,0:T(8,128)(2,1)S(1)}, bf16[64,640]{1,0:T(8,128)(2,1)S(1)}, u32[]{:S(2)}, u32[]{:S(2)}) collective-permute-start(bf16[64,640]{1,0:T(8,128)(2,1)S(1)} %get-tuple-element.109), channel_id=1, source_target_pairs={{0,6},{1,7},{2,4},{3,5},{4,2},{5,3},{6,0},{7,1},{8,14},{9,15},{10,... | collective-permute-start | bytes 245768 | tf_op jit(solution)/shard_map/ppermute | solution.py:777
  82.2 1.2 %collective-permute-done.5 = bf16[64,640]{1,0:T(8,128)(2,1)S(1)} collective-permute-done((bf16[64,640]{1,0:T(8,128)(2,1)S(1)}, bf16[64,640]{1,0:T(8,128)(2,1)S(1)}, u32[]{:S(2)}, u32[]{:S(2)}) %collective-permute-start.5) | collective-permute-done | bytes 81952 | tf_op jit(solution)/shard_map/ppermute | solution.py:777
  83.4 1.4 %collective-permute-done.6 = bf16[64,640]{1,0:T(8,128)(2,1)S(1)} collective-permute-done((bf16[64,640]{1,0:T(8,128)(2,1)S(1)}, bf16[64,640]{1,0:T(8,128)(2,1)S(1)}, u32[]{:S(2)}, u32[]{:S(2)}) %collective-permute-start.6) | collective-permute-done | bytes 81952 | tf_op jit(solution)/shard_map/ppermute | solution.py:777
  84.8 1.3 %collective-permute-done.7 = bf16[64,640]{1,0:T(8,128)(2,1)S(1)} collective-permute-done((bf16[64,640]{1,0:T(8,128)(2,1)S(1)}, bf16[64,640]{1,0:T(8,128)(2,1)S(1)}, u32[]{:S(2)}, u32[]{:S(2)}) %collective-permute-start.7) | collective-permute-done | bytes 81952 | tf_op jit(solution)/shard_map/ppermute | solution.py:777
  86.2 0.7 copy-done.6
  86.9 1.5 %collective-permute-start.8 = (f32[8,1024]{1,0:T(8,128)S(1)}, f32[8,1024]{1,0:T(8,128)S(1)}, u32[]{:S(2)}, u32[]{:S(2)}) collective-permute-start(f32[8,1024]{1,0:T(8,128)S(1)} %copy-done.6), channel_id=1, source_target_pairs={{0,2},{1,3},{2,0},{3,1},{4,6},{5,7},{6,4},{7,5},{8,10},{9,11},{10,... | collective-permute-start | bytes 98312 | tf_op jit(solution)/shard_map/ppermute | solution.py:777
  88.4 0.9 collective-permute-start.9
  89.2 1.2 %collective-permute-start.10 = (f32[8,1024]{1,0:T(8,128)S(1)}, f32[8,1024]{1,0:T(8,128)S(1)}, u32[]{:S(2)}, u32[]{:S(2)}) collective-permute-start(f32[8,1024]{1,0:T(8,128)S(1)} %copy-done.6), channel_id=1, source_target_pairs={{0,6},{1,7},{2,4},{3,5},{4,2},{5,3},{6,0},{7,1},{8,14},{9,15},{10,... | collective-permute-start | bytes 98312 | tf_op jit(solution)/shard_map/ppermute | solution.py:777
  90.4 1.6 %collective-permute-start.12 = (bf16[64,640]{1,0:T(8,128)(2,1)S(1)}, bf16[64,640]{1,0:T(8,128)(2,1)S(1)}, u32[]{:S(2)}, u32[]{:S(2)}) collective-permute-start(bf16[64,640]{1,0:T(8,128)(2,1)S(1)} %fusion.3), channel_id=1, source_target_pairs={{0,8},{8,0},{16,24},{24,16},{1,9},{9,1},{17,25},{25,17},{2,10},{10... | collective-permute-start | bytes 245768 | tf_op jit(solution)/shard_map/ppermute | solution.py:777
  92.0 0.3 collective-permute-done.9
  92.3 1.8 %collective-permute-done.10 = f32[8,1024]{1,0:T(8,128)S(1)} collective-permute-done((f32[8,1024]{1,0:T(8,128)S(1)}, f32[8,1024]{1,0:T(8,128)S(1)}, u32[]{:S(2)}, u32[]{:S(2)}) %collective-permute-start.10) | collective-permute-done | bytes 32800 | tf_op jit(solution)/shard_map/ppermute | solution.py:777
  94.1 0.0 copy-start.2
  94.1 0.1 collective-permute-start.11
  94.1 0.7 collective-permute-done.12
  94.9 0.0 copy-start.3
  94.9 2.6 %collective-permute-start.13 = (bf16[64,640]{1,0:T(8,128)(2,1)S(1)}, bf16[64,640]{1,0:T(8,128)(2,1)S(1)}, u32[]{:S(2)}, u32[]{:S(2)}) collective-permute-start(bf16[64,640]{1,0:T(8,128)(2,1)S(1)} %add_convert_fusion.a_ref), channel_id=1, source_target_pairs={{0,16},{8,24},{16,0},{24,8},{1,17},{9,25},{17,1},{25,9},{2,18},{10... | collective-permute-start | bytes 245768 | tf_op jit(solution)/shard_map/ppermute | solution.py:777
  97.5 1.4 %dynamic-slice_bitcast_fusion.cols_ref = f32[64,128]{1,0:T(8,128)} fusion(f32[8,64,128]{2,1,0:T(8,128)} %get-tuple-element.77, s32[]{:T(128)S(6)} %select_n.4), kind=kLoop, calls=%fused_computation.11 | loop fusion | bytes 65540 | tf_op jit(solution)/shard_map/jit(dynamic_index_in_dim)/squeeze | solution.py:835
  98.9 3.0 %collective-permute-done.13.b_ref = bf16[64,640]{1,0:T(8,128)(2,1)S(1)} collective-permute-done((bf16[64,640]{1,0:T(8,128)(2,1)S(1)}, bf16[64,640]{1,0:T(8,128)(2,1)S(1)}, u32[]{:S(2)}, u32[]{:S(2)}) %collective-permute-start.13) | collective-permute-done | bytes 81952 | tf_op jit(solution)/shard_map/ppermute | solution.py:777
  101.9 0.6 copy-done.5
  102.5 1.8 %norm_parts.1 = (f32[64,640]{1,0:T(8,128)}, f32[8,128]{1,0:T(8,128)}) custom-call(s32[1]{0:T(128)} %bitcast.index_ref, bf16[64,640]{1,0:T(8,128)(2,1)} %copy-done.3, bf16[64,640]{1,0:T(8,128)(2,1)} %copy-done.5, f32[64,640]{1,0:T(8,128)} %pack_weights.1.pack_ref, f32[64,128]{1,0:T(8,128)} %dynamic-slice_bitcast_fusion.cols_ref, ...), custom_call_target="tpu_custom_call" | custom-call | tf_op jit(solution)/shard_map/norm_parts/pallas_call | solution.py:836
  104.3 0.0 collective-permute-start.14
  104.3 1.4 %collective-permute-done.14 = f32[8,128]{1,0:T(8,128)S(1)} collective-permute-done((f32[8,128]{1,0:T(8,128)}, f32[8,128]{1,0:T(8,128)S(1)}, u32[]{:S(2)}, u32[]{:S(2)}) %collective-permute-start.14) | collective-permute-done | bytes 4128 | tf_op jit(solution)/shard_map/ppermute | solution.py:777
  105.7 0.7 add.28
  106.4 1.2 %collective-permute-start.16 = (f32[8,128]{1,0:T(8,128)S(1)}, f32[8,128]{1,0:T(8,128)S(1)}, u32[]{:S(2)}, u32[]{:S(2)}) collective-permute-start(f32[8,128]{1,0:T(8,128)S(1)} %add.28), channel_id=1, source_target_pairs={{0,4},{1,5},{2,6},{3,7},{4,0},{5,1},{6,2},{7,3},{8,12},{9,13},{10,... | collective-permute-start | bytes 12296 | tf_op jit(solution)/shard_map/ppermute | solution.py:777
  107.6 2.3 %collective-permute-start.17 = (f32[8,128]{1,0:T(8,128)S(1)}, f32[8,128]{1,0:T(8,128)S(1)}, u32[]{:S(2)}, u32[]{:S(2)}) collective-permute-start(f32[8,128]{1,0:T(8,128)S(1)} %add.28), channel_id=1, source_target_pairs={{0,6},{1,7},{2,4},{3,5},{4,2},{5,3},{6,0},{7,1},{8,14},{9,15},{10,... | collective-permute-start | bytes 12296 | tf_op jit(solution)/shard_map/ppermute | solution.py:777
  109.9 0.0 collective-permute-done.11.p1_ref
  109.9 0.7 copy-done.4
  110.6 1.9 %assemble_outputs.1 = (f32[3,8192]{1,0:T(4,128)}, f32[3,8192]{1,0:T(4,128)}, f32[2,4]{1,0:T(2,128)}) custom-call(s32[1]{0:T(128)} %bitcast.index_ref, s32[2]{0:T(128)} %kinds_ref.3, f32[4,8,1024]{2,1,0:T(8,128)} %copy-done.2, f32[4,8,1024]{2,1,0:T(8,128)} %copy-done.4, f32[3,3]{1,0:T(4,128)} %small_ref.3), custom_call_target="tpu_custom_call" | custom-call | tf_op jit(solution)/shard_map/assemble_outputs/pallas_call | solution.py:822
  112.4 0.0 collective-permute-done.16
  112.5 0.0 collective-permute-done.17
  112.5 0.6 pad_maximum_fusion.2.totals_ref
  113.1 2.6 %adam_update.1 = (f32[1,1]{1,0:T(1,128)}, f32[27,64]{1,0:T(8,128)}, f32[27,64]{1,0:T(8,128)}, f32[27,64]{1,0:T(8,128)}, f32[64,512]{1,0:T(8,128)}, /*index=5*/f3...) custom-call(f32[4,128]{1,0:T(4,128)} %pad_maximum_fusion.2.totals_re, ...), custom_call_target="tpu_custom_call" | custom-call | tf_op jit(solution)/shard_map/adam_update/pallas_call | solution.py:865
  (21 shorter events, 0.1 us)
Async XLA Ops:
  2.5 8.2 %collective-permute-start = (f32[64,640]{1,0:T(8,128)}, f32[64,640]{1,0:T(8,128)S(1)}, u32[]{:S(2)}, u32[]{:S(2)}) collective-permute-start(f32[64,640]{1,0:T(8,128)} %pack_weights.1.pack_ref), channel_id=1, source_target_pairs={{0,2},{1,3},{2,0},{3,1},{4,6},{5,7},{6,4},{7,5},{8,10},{9,11},{10,... | collective-permute-start | bytes 491528 | tf_op jit(solution)/shard_map/ppermute | solution.py:777
  5.4 9.4 %collective-permute-start.1 = (f32[64,640]{1,0:T(8,128)}, f32[64,640]{1,0:T(8,128)S(1)}, u32[]{:S(2)}, u32[]{:S(2)}) collective-permute-start(f32[64,640]{1,0:T(8,128)} %pack_weights.1.pack_ref), channel_id=1, source_target_pairs={{0,4},{1,5},{2,6},{3,7},{4,0},{5,1},{6,2},{7,3},{8,12},{9,13},{10,... | collective-permute-start | bytes 491528 | tf_op jit(solution)/shard_map/ppermute | solution.py:777
  7.0 7.9 %collective-permute-start.2 = (f32[64,640]{1,0:T(8,128)}, f32[64,640]{1,0:T(8,128)S(1)}, u32[]{:S(2)}, u32[]{:S(2)}) collective-permute-start(f32[64,640]{1,0:T(8,128)} %pack_weights.1.pack_ref), channel_id=1, source_target_pairs={{0,6},{1,7},{2,4},{3,5},{4,2},{5,3},{6,0},{7,1},{8,14},{9,15},{10,... | collective-permute-start | bytes 491528 | tf_op jit(solution)/shard_map/ppermute | solution.py:777
  15.8 3.2 %copy-start = (f32[4,64,640]{2,1,0:T(8,128)}, f32[4,64,640]{2,1,0:T(8,128)S(1)}, u32[]{:S(2)}) copy-start(f32[4,64,640]{2,1,0:T(8,128)S(1)} %pad_maximum_fusion.x0_ref) | copy-start | bytes 1966084
  15.8 2.3 %collective-permute-start.3 = (f32[4,64,640]{2,1,0:T(8,128)S(1)}, f32[4,64,640]{2,1,0:T(8,128)S(1)}, u32[]{:S(2)}, u32[]{:S(2)}) collective-permute-start(f32[4,64,640]{2,1,0:T(8,128)S(1)} %pad_maximum_fusion.x0_ref), channel_id=1, source_target_pairs={{0,1},{1,0},{2,3},{3,2},{4,5},{5,4},{6,7},{7,6},{8,9},{9,8},{10,11... | collective-permute-start | bytes 1966088 | tf_op jit(solution)/shard_map/ppermute | solution.py:777
  18.1 0.9 copy-start.1
  75.1 2.3 %collective-permute-start.4 = (f32[4,64,640]{2,1,0:T(8,128)}, f32[4,64,640]{2,1,0:T(8,128)S(1)}, u32[]{:S(2)}, u32[]{:S(2)}) collective-permute-start(f32[4,64,640]{2,1,0:T(8,128)} %get-tuple-element.71), channel_id=1, source_target_pairs={{0,1},{1,0},{2,3},{3,2},{4,5},{5,4},{6,7},{7,6},{8,9},{9,8},{10,11... | collective-permute-start | bytes 1966088 | tf_op jit(solution)/shard_map/ppermute | solution.py:777
  78.6 4.8 %collective-permute-start.5 = (bf16[64,640]{1,0:T(8,128)(2,1)S(1)}, bf16[64,640]{1,0:T(8,128)(2,1)S(1)}, u32[]{:S(2)}, u32[]{:S(2)}) collective-permute-start(bf16[64,640]{1,0:T(8,128)(2,1)S(1)} %get-tuple-element.108), channel_id=1, source_target_pairs={{0,2},{1,3},{2,0},{3,1},{4,6},{5,7},{6,4},{7,5},{8,10},{9,11},{10,... | collective-permute-start | bytes 245768 | tf_op jit(solution)/shard_map/ppermute | solution.py:777
  79.9 4.9 %collective-permute-start.6 = (bf16[64,640]{1,0:T(8,128)(2,1)S(1)}, bf16[64,640]{1,0:T(8,128)(2,1)S(1)}, u32[]{:S(2)}, u32[]{:S(2)}) collective-permute-start(bf16[64,640]{1,0:T(8,128)(2,1)S(1)} %get-tuple-element.110), channel_id=1, source_target_pairs={{0,4},{1,5},{2,6},{3,7},{4,0},{5,1},{6,2},{7,3},{8,12},{9,13},{10,... | collective-permute-start | bytes 245768 | tf_op jit(solution)/shard_map/ppermute | solution.py:777
  80.8 5.4 %collective-permute-start.7 = (bf16[64,640]{1,0:T(8,128)(2,1)S(1)}, bf16[64,640]{1,0:T(8,128)(2,1)S(1)}, u32[]{:S(2)}, u32[]{:S(2)}) collective-permute-start(bf16[64,640]{1,0:T(8,128)(2,1)S(1)} %get-tuple-element.109), channel_id=1, source_target_pairs={{0,6},{1,7},{2,4},{3,5},{4,2},{5,3},{6,0},{7,1},{8,14},{9,15},{10,... | collective-permute-start | bytes 245768 | tf_op jit(solution)/shard_map/ppermute | solution.py:777
  86.1 0.8 copy-start.6
  86.9 5.1 %collective-permute-start.8 = (f32[8,1024]{1,0:T(8,128)S(1)}, f32[8,1024]{1,0:T(8,128)S(1)}, u32[]{:S(2)}, u32[]{:S(2)}) collective-permute-start(f32[8,1024]{1,0:T(8,128)S(1)} %copy-done.6), channel_id=1, source_target_pairs={{0,2},{1,3},{2,0},{3,1},{4,6},{5,7},{6,4},{7,5},{8,10},{9,11},{10,... | collective-permute-start | bytes 98312 | tf_op jit(solution)/shard_map/ppermute | solution.py:777
  88.4 3.9 %collective-permute-start.9 = (f32[8,1024]{1,0:T(8,128)S(1)}, f32[8,1024]{1,0:T(8,128)S(1)}, u32[]{:S(2)}, u32[]{:S(2)}) collective-permute-start(f32[8,1024]{1,0:T(8,128)S(1)} %copy-done.6), channel_id=1, source_target_pairs={{0,4},{1,5},{2,6},{3,7},{4,0},{5,1},{6,2},{7,3},{8,12},{9,13},{10,... | collective-permute-start | bytes 98312 | tf_op jit(solution)/shard_map/ppermute | solution.py:777
  89.2 4.8 %collective-permute-start.10 = (f32[8,1024]{1,0:T(8,128)S(1)}, f32[8,1024]{1,0:T(8,128)S(1)}, u32[]{:S(2)}, u32[]{:S(2)}) collective-permute-start(f32[8,1024]{1,0:T(8,128)S(1)} %copy-done.6), channel_id=1, source_target_pairs={{0,6},{1,7},{2,4},{3,5},{4,2},{5,3},{6,0},{7,1},{8,14},{9,15},{10,... | collective-permute-start | bytes 98312 | tf_op jit(solution)/shard_map/ppermute | solution.py:777
  90.4 4.4 %collective-permute-start.12 = (bf16[64,640]{1,0:T(8,128)(2,1)S(1)}, bf16[64,640]{1,0:T(8,128)(2,1)S(1)}, u32[]{:S(2)}, u32[]{:S(2)}) collective-permute-start(bf16[64,640]{1,0:T(8,128)(2,1)S(1)} %fusion.3), channel_id=1, source_target_pairs={{0,8},{8,0},{16,24},{24,16},{1,9},{9,1},{17,25},{25,17},{2,10},{10... | collective-permute-start | bytes 245768 | tf_op jit(solution)/shard_map/ppermute | solution.py:777
  94.1 4.8 %copy-start.2 = (f32[4,8,1024]{2,1,0:T(8,128)}, f32[4,8,1024]{2,1,0:T(8,128)S(1)}, u32[]{:S(2)}) copy-start(f32[4,8,1024]{2,1,0:T(8,128)S(1)} %pad_maximum_fusion.1.p0_ref) | copy-start | bytes 393220
  94.1 15.8 %collective-permute-start.11 = (f32[4,8,1024]{2,1,0:T(8,128)S(1)}, f32[4,8,1024]{2,1,0:T(8,128)S(1)}, u32[]{:S(2)}, u32[]{:S(2)}) collective-permute-start(f32[4,8,1024]{2,1,0:T(8,128)S(1)} %pad_maximum_fusion.1.p0_ref), channel_id=1, source_target_pairs={{0,1},{1,0},{2,3},{3,2},{4,5},{5,4},{6,7},{7,6},{8,9},{9,8},{10,11... | collective-permute-start | bytes 393224 | tf_op jit(solution)/shard_map/ppermute | solution.py:777
  94.9 7.0 %copy-start.3 = (bf16[64,640]{1,0:T(8,128)(2,1)}, bf16[64,640]{1,0:T(8,128)(2,1)S(1)}, u32[]{:S(2)}) copy-start(bf16[64,640]{1,0:T(8,128)(2,1)S(1)} %add_convert_fusion.a_ref) | copy-start | bytes 245764
  94.9 7.0 %collective-permute-start.13 = (bf16[64,640]{1,0:T(8,128)(2,1)S(1)}, bf16[64,640]{1,0:T(8,128)(2,1)S(1)}, u32[]{:S(2)}, u32[]{:S(2)}) collective-permute-start(bf16[64,640]{1,0:T(8,128)(2,1)S(1)} %add_convert_fusion.a_ref), channel_id=1, source_target_pairs={{0,16},{8,24},{16,0},{24,8},{1,17},{9,25},{17,1},{25,9},{2,18},{10... | collective-permute-start | bytes 245768 | tf_op jit(solution)/shard_map/ppermute | solution.py:777
  101.9 0.6 copy-start.5
  104.3 1.4 %collective-permute-start.14 = (f32[8,128]{1,0:T(8,128)}, f32[8,128]{1,0:T(8,128)S(1)}, u32[]{:S(2)}, u32[]{:S(2)}) collective-permute-start(f32[8,128]{1,0:T(8,128)} %get-tuple-element.79), channel_id=1, source_target_pairs={{0,1},{1,0},{2,3},{3,2},{4,5},{5,4},{6,7},{7,6},{8,9},{9,8},{10,11... | collective-permute-start | bytes 12296 | tf_op jit(solution)/shard_map/ppermute | solution.py:777
  106.4 6.0 %collective-permute-start.15 = (f32[8,128]{1,0:T(8,128)S(1)}, f32[8,128]{1,0:T(8,128)S(1)}, u32[]{:S(2)}, u32[]{:S(2)}) collective-permute-start(f32[8,128]{1,0:T(8,128)S(1)} %add.28), channel_id=1, source_target_pairs={{0,2},{1,3},{2,0},{3,1},{4,6},{5,7},{6,4},{7,5},{8,10},{9,11},{10,... | collective-permute-start | bytes 12296 | tf_op jit(solution)/shard_map/ppermute | solution.py:777
  106.4 6.0 %collective-permute-start.16 = (f32[8,128]{1,0:T(8,128)S(1)}, f32[8,128]{1,0:T(8,128)S(1)}, u32[]{:S(2)}, u32[]{:S(2)}) collective-permute-start(f32[8,128]{1,0:T(8,128)S(1)} %add.28), channel_id=1, source_target_pairs={{0,4},{1,5},{2,6},{3,7},{4,0},{5,1},{6,2},{7,3},{8,12},{9,13},{10,... | collective-permute-start | bytes 12296 | tf_op jit(solution)/shard_map/ppermute | solution.py:777
  107.6 4.9 %collective-permute-start.17 = (f32[8,128]{1,0:T(8,128)S(1)}, f32[8,128]{1,0:T(8,128)S(1)}, u32[]{:S(2)}, u32[]{:S(2)}) collective-permute-start(f32[8,128]{1,0:T(8,128)S(1)} %add.28), channel_id=1, source_target_pairs={{0,6},{1,7},{2,4},{3,5},{4,2},{5,3},{6,0},{7,1},{8,14},{9,15},{10,... | collective-permute-start | bytes 12296 | tf_op jit(solution)/shard_map/ppermute | solution.py:777
  109.9 0.7 copy-start.4

commit v3 on v2

--- a/solution.py
+++ b/solution.py
@@ -206,10 +206,11 @@
         return [planes_ref[32 + i : 33 + i, lanes] for i in range(4)]
 
     def put_taps(slot, pieces, lanes):
-        taps_s[slot, 0 : TAP_ROWS + 8, lanes] = jnp.concatenate(
-            pieces + [jnp.zeros((8, lanes.size), F32)], axis=0
-        ).astype(BF16)
-        taps_s[slot, TAP_ROWS + 8 :, lanes] = jnp.zeros((LANES - TAP_ROWS - 8, lanes.size), BF16)
+        full = jnp.concatenate(pieces + [jnp.zeros((8, lanes.size), F32)], axis=0).astype(BF16)
+        for c in range(lanes.size // LANES):
+            chunk = lanes.start // LANES + c
+            taps_s[slot, chunk, 0 : TAP_ROWS + 8] = full[:, c * LANES : (c + 1) * LANES]
+            taps_s[slot, chunk, TAP_ROWS + 8 :] = jnp.zeros((LANES - TAP_ROWS - 8, LANES), BF16)
 
     whole = pl.ds(0, region)
     h8 = (planes_ref[0:8] + shift8) * scale8
@@ -222,107 +223,108 @@
     state = probes8 * jnp.where(upper, planes_ref[24 + 7 : 24 + 8], slope0)
     put_taps(1, col_taps(state, masks_at(whole)), whole)
 
-    def activation(act, slope_ref, curve_ref, lanes, curve_lanes, in_curve):
-        half = 0.5 * jnp.tanh(0.5 * act)
-        sig = 0.5 + half
+    own_blocks = own // BLOCK
+    ring = own + BLOCK
+
+    def over_blocks(count, body, carry=0):
+        pairs = count // 2
+        if pairs:
+            carry = lax.fori_loop(0, pairs, lambda j, kept: body(2 * j * BLOCK, 2 * BLOCK, kept), carry)
+        if count % 2:
+            carry = body((count - 1) * BLOCK, BLOCK, carry)
+        return carry
+
+    def halves(start, size, base, width):
+        places = []
+        for h in range(size // LANES):
+            chunk = start // LANES + h - base // LANES
+            chunks = width // LANES
+            places.append(jnp.where((chunk >= 0) & (chunk < chunks), chunk, chunks))
+        return places
+
+    def put(ref, places, value):
+        for h, place in enumerate(places):
+            ref[place] = value[:, h * LANES : (h + 1) * LANES]
+
+    def join(ref, first, count):
+        return jnp.concatenate([ref[first + i] for i in range(count)], axis=1)
+
+    def activation(act, slope_ref, curve_ref, lanes, ring_places):
+        tanh = jnp.tanh(0.5 * act)
+        half = 0.5 * tanh
         rest = 0.5 - half
-        hidden = act * sig * (1.0 / 1.1)
-        slope_ref[:, lanes] = sig * (1.0 / 1.1) + hidden * rest
-        sig2 = sig * (2.0 / 1.1)
-
-        @pl.when(in_curve)
-        def _():
-            curve_ref[:, curve_lanes] = (rest * (sig2 - 2.0 * half * hidden)).astype(BF16)
-
+        sig = (1.0 / 1.1) * (0.5 + half)
+        hidden = act * sig
+        slope_ref[:, lanes] = sig + hidden * rest
+        put(curve_ref, ring_places, (rest * ((sig + sig) - tanh * hidden)).astype(BF16))
         return hidden.astype(BF16)
 
-    own_blocks = own // BLOCK
-
-    def start_body(j, carry):
-        lanes = pl.ds(pl.multiple_of(j * BLOCK, LANES), BLOCK)
-        in_curve = (j >= 1) & (j < own_blocks + 3)
-        curve_lanes = pl.ds(pl.multiple_of(jnp.clip(j - 1, 0, own_blocks + 1) * BLOCK, LANES), BLOCK)
-        taps = taps_s[0, :, lanes]
-        act1 = dot_nn(w13_s[0:channels], taps)
+    def start_body(at, size, carry):
+        start = pl.multiple_of(at, LANES)
+        lanes = pl.ds(start, size)
+        count = size // LANES
+        ring_places = halves(start, size, HALO - LANES, ring)
+        own_places = halves(start, size, HALO, own)
+        act1 = dot_nn(w13_s[0:channels], join(taps_s.at[0], start // LANES, count))
         bias1 = bias_s[0]
         hidden1 = activation(
-            act1 + jnp.concatenate([bias1, bias1], axis=1), sl1_s, cv1_s, lanes, curve_lanes, in_curve
+            act1 + jnp.concatenate([bias1] * count, axis=1), sl1_s, cv1_s, lanes, ring_places
         )
+        put(hid1_s, own_places, hidden1)
         act2 = dot_nn(w2_s[...], hidden1)
         bias2 = bias_s[1]
         hidden2 = activation(
-            act2 + jnp.concatenate([bias2, bias2], axis=1), sl2_s, cv2_s, lanes, curve_lanes, in_curve
+            act2 + jnp.concatenate([bias2] * count, axis=1), sl2_s, cv2_s, lanes, ring_places
         )
+        put(hid2_s, own_places, hidden2)
         q0_s[:, lanes] = dot_nn(wout_s[:, 0:channels], hidden2)[0:TAP_ROWS]
-
-        @pl.when((j >= 2) & (j < own_blocks + 2))
-        def _():
-            own_lanes = pl.ds(pl.multiple_of((j - 2) * BLOCK, LANES), BLOCK)
-            hid1_s[:, own_lanes] = hidden1
-            hid2_s[:, own_lanes] = hidden2
-
         return carry
 
-    lax.fori_loop(0, own_blocks + 4, start_body, 0)
-
-    own_in_slot = pl.ds(LANES, own)
+    over_blocks(own_blocks + 4, start_body)
+
 
     def series_stage(stage):
         offset = LANES * (stage - 1)
         count = own_blocks + 5 - stage
         tan_slot = min(stage, 3) - 1
-        aligned = stage % 2 == 1
-        store_from = (HALO - offset) // BLOCK if aligned else (HALO - LANES - offset) // BLOCK
-        store_count = own_blocks if aligned else own_blocks + 1
-
-        def body(j, carry):
-            start = pl.multiple_of(offset + j * BLOCK, LANES)
-            lanes = pl.ds(start, BLOCK)
-            both = dot_nn(w13_s[...], taps_s[stage, :, lanes])
-            lin1 = both[0:channels]
-            gt2 = both[channels:]
-            slope1 = sl1_s[:, lanes]
-            slope2 = sl2_s[:, lanes]
-            tan1 = (slope1 * lin1).astype(BF16)
-            g2 = (slope2 * gt2).astype(BF16)
+
+        def body(at, size, carry):
+            start = pl.multiple_of(offset + at, LANES)
+            lanes = pl.ds(start, size)
+            ring_places = halves(start, size, HALO - LANES, ring)
+            own_places = halves(start, size, HALO, own)
+
+            def pair_up(acc_ref, mine_ref, other_ref, value, slot):
+                for h, place in enumerate(ring_places):
+                    part = value[:, h * LANES : (h + 1) * LANES]
+                    if stage <= 2:
+                        mine_ref[stage - 1, place] = part.astype(BF16)
+                    else:
+                        acc_ref[place] += part * other_ref[slot, place].astype(F32)
+
+            slot = 4 - stage
+            taps = join(taps_s.at[stage], start // LANES, size // LANES)
+            lin1 = dot_nn(w13_s[0:channels], taps)
+            tan1 = (sl1_s[:, lanes] * lin1).astype(BF16)
+            put(tan1_s.at[tan_slot], own_places, tan1)
+            pair_up(acc1_s, lin1_s, gt1_s, lin1, slot)
+            gt2 = dot_nn(w13_s[channels:], taps)
+            g2 = (sl2_s[:, lanes] * gt2).astype(BF16)
+            put(g2_s.at[tan_slot], own_places, g2)
+            pair_up(acc2_s, gt2_s, lin2_s, gt2, slot)
             lin2 = dot_nn(w2_s[...], tan1)
+            tan2 = (sl2_s[:, lanes] * lin2).astype(BF16)
+            put(tan2_s.at[tan_slot], own_places, tan2)
+            pair_up(acc2_s, lin2_s, gt2_s, lin2, slot)
             gt1 = dot_nn(w2t_s[...], g2)
-            tan2 = (slope2 * lin2).astype(BF16)
-            g1 = (slope1 * gt1).astype(BF16)
-            q_s[:, lanes] = dot_nn(wout_s[...], jnp.concatenate([tan2, g1], axis=0))[0:TAP_ROWS]
-
-            @pl.when((j >= store_from) & (j < store_from + store_count))
-            def _():
-                slot_lanes = pl.ds(pl.multiple_of(start - (HALO - LANES), LANES), BLOCK)
-                tan1_s[tan_slot, :, slot_lanes] = tan1
-                tan2_s[tan_slot, :, slot_lanes] = tan2
-                g1_s[tan_slot, :, slot_lanes] = g1
-                g2_s[tan_slot, :, slot_lanes] = g2
-
-            wide_lanes = pl.ds(pl.multiple_of(jnp.maximum(start - BLOCK, 0), LANES), BLOCK)
-            if stage <= 2:
-                wide_count = own_blocks + 3 - stage
-
-                @pl.when((j >= 1) & (j < 1 + wide_count))
-                def _():
-                    lin1_s[stage - 1, :, wide_lanes] = lin1.astype(BF16)
-                    lin2_s[stage - 1, :, wide_lanes] = lin2.astype(BF16)
-                    gt1_s[stage - 1, :, wide_lanes] = gt1.astype(BF16)
-                    gt2_s[stage - 1, :, wide_lanes] = gt2.astype(BF16)
-            else:
-                slot = 4 - stage
-                for acc_ref, lin_ref, gt_ref, lin, gt in (
-                    (acc1_s, lin1_s, gt1_s, lin1, gt1),
-                    (acc2_s, lin2_s, gt2_s, lin2, gt2),
-                ):
-                    total = lin * gt_ref[slot, :, wide_lanes].astype(F32)
-                    total = total + gt * lin_ref[slot, :, wide_lanes].astype(F32)
-                    if stage == 4:
-                        total = total + acc_ref[:, wide_lanes]
-                    acc_ref[:, wide_lanes] = total
+            g1 = (sl1_s[:, lanes] * gt1).astype(BF16)
+            put(g1_s.at[tan_slot], own_places, g1)
+            pair_up(acc1_s, gt1_s, lin1_s, gt1, slot)
+            q_fwd = dot_nn(wout_s[:, 0:channels], tan2)[0:TAP_ROWS]
+            q_s[:, lanes] = q_fwd + dot_nn(wout_s[:, channels:], g1)[0:TAP_ROWS]
             return carry
 
-        lax.fori_loop(0, count, body, 0)
+        over_blocks(count, body)
 
         inside = pl.ds(offset, count * BLOCK)
         result = comb_taps(q_s, inside, masks_at(inside))
@@ -338,7 +340,7 @@
             put_taps(stage + 1, col_taps(following, masks_at(lanes)), lanes)
 
     def own_taps(slot):
-        return taps_s[slot, :, pl.ds(HALO, own)]
+        return join(taps_s.at[slot], HALO // LANES, own // LANES)
 
     def add_weight_grads(slot_pairs, tap_pairs, first):
         total = None
@@ -363,8 +365,10 @@
             w_s[:, :, channels:] = w_s[:, :, channels:] + tile_part
 
     def slot_of(ref, slot):
-        return ref[slot, :, own_in_slot]
-
+        return join(ref.at[slot], 0, own // LANES)
+
+    acc1_s[...] = jnp.zeros(acc1_s.shape, F32)
+    acc2_s[...] = jnp.zeros(acc2_s.shape, F32)
     series_stage(1)
     series_stage(2)
     series_stage(3)
@@ -386,31 +390,32 @@
         False,
     )
 
-    def final_body(j, carry):
+    def final_body(at, size, carry):
         bias_one, bias_two = carry
-        start = pl.multiple_of(HALO - LANES + j * BLOCK, LANES)
-        lanes = pl.ds(start, BLOCK)
-        wide_lanes = pl.ds(pl.multiple_of(LANES + j * BLOCK, LANES), BLOCK)
-        slot_lanes = pl.ds(pl.multiple_of(j * BLOCK, LANES), BLOCK)
-        low_lanes = (j > 0).astype(F32)
-        high_lanes = (j < own_blocks).astype(F32)
-        gs2 = dot_nn(w13_s[channels:], taps_s[0, :, lanes])
-        ga2 = cv2_s[:, wide_lanes].astype(F32) * acc2_s[:, wide_lanes] + sl2_s[:, lanes] * gs2
+        start = pl.multiple_of(HALO - LANES + at, LANES)
+        lanes = pl.ds(start, size)
+        count = size // LANES
+        ring_from = at // LANES
+        own_places = halves(start, size, HALO, own)
+        gs2 = dot_nn(w13_s[channels:], join(taps_s.at[0], start // LANES, count))
+        ga2 = join(cv2_s, ring_from, count).astype(F32) * join(acc2_s, ring_from, count) + sl2_s[:, lanes] * gs2
         low2 = ga2.astype(BF16)
         gs1 = dot_nn(w2t_s[...], low2)
-        ga1 = cv1_s[:, wide_lanes].astype(F32) * acc1_s[:, wide_lanes] + sl1_s[:, lanes] * gs1
+        ga1 = join(cv1_s, ring_from, count).astype(F32) * join(acc1_s, ring_from, count) + sl1_s[:, lanes] * gs1
         low1 = ga1.astype(BF16)
         q_s[:, lanes] = q0_s[:, lanes] + dot_nn(wout_s[:, channels:], low1)[0:TAP_ROWS]
-        g2_s[0, :, slot_lanes] = low2
-        g1_s[0, :, slot_lanes] = low1
-        bias_one = bias_one + low_lanes * ga1[:, 0:LANES] + high_lanes * ga1[:, LANES:]
-        bias_two = bias_two + low_lanes * ga2[:, 0:LANES] + high_lanes * ga2[:, LANES:]
+        put(g2_s.at[0], own_places, low2)
+        put(g1_s.at[0], own_places, low1)
+        for c in range(count):
+            here = jnp.where(own_places[c] < own // LANES, 1.0, 0.0)
+            bias_one = bias_one + here * ga1[:, c * LANES : (c + 1) * LANES]
+            bias_two = bias_two + here * ga2[:, c * LANES : (c + 1) * LANES]
         return bias_one, bias_two
 
     zero = jnp.zeros((channels, LANES), F32)
-    bias_one, bias_two = lax.fori_loop(0, own_blocks + 1, final_body, (zero, zero))
+    bias_one, bias_two = over_blocks(own_blocks + 1, final_body, (zero, zero))
     add_weight_grads(
-        ((hid1_s[...], slot_of(g2_s, 0)),), ((slot_of(g1_s, 0), hid2_s[...], 0),), False
+        ((join(hid1_s, 0, own // LANES), slot_of(g2_s, 0)),), ((slot_of(g1_s, 0), join(hid2_s, 0, own // LANES), 0),), False
     )
 
     inside = pl.ds(HALO - LANES, own + BLOCK)
@@ -460,8 +465,8 @@
 def call_main(me, u3, x0, x1, u2, planes, small, own, channels, chips):
     rows_own = channels // (2 * chips)
     region = own + 2 * HALO
-    wide = own + 2 * BLOCK
-    slot = own + BLOCK
+    wide = (own + BLOCK) // LANES + 1
+    slot = own // LANES + 1
     width = channels + LANES
     out_shape = (
         jax.ShapeDtypeStruct((chips, rows_own, width), F32),
@@ -478,23 +483,23 @@
         vmem((channels, channels), BF16),
         vmem((TAP_ROWS + 8, 2 * channels), BF16),
         vmem((2, channels, LANES), F32),
-        vmem((NMAX + 1, LANES, region), BF16),
+        vmem((NMAX + 1, region // LANES, LANES, LANES), BF16),
         vmem((channels, region), F32),
         vmem((channels, region), F32),
-        vmem((channels, wide), BF16),
-        vmem((channels, wide), BF16),
-        vmem((2, channels, wide), BF16),
-        vmem((2, channels, wide), BF16),
-        vmem((2, channels, wide), BF16),
-        vmem((2, channels, wide), BF16),
-        vmem((channels, wide), F32),
-        vmem((channels, wide), F32),
-        vmem((3, channels, slot), BF16),
-        vmem((3, channels, slot), BF16),
-        vmem((3, channels, slot), BF16),
-        vmem((3, channels, slot), BF16),
-        vmem((channels, own), BF16),
-        vmem((channels, own), BF16),
+        vmem((wide, channels, LANES), BF16),
+        vmem((wide, channels, LANES), BF16),
+        vmem((2, wide, channels, LANES), BF16),
+        vmem((2, wide, channels, LANES), BF16),
+        vmem((2, wide, channels, LANES), BF16),
+        vmem((2, wide, channels, LANES), BF16),
+        vmem((wide, channels, LANES), F32),
+        vmem((wide, channels, LANES), F32),
+        vmem((3, slot, channels, LANES), BF16),
+        vmem((3, slot, channels, LANES), BF16),
+        vmem((3, slot, channels, LANES), BF16),
+        vmem((3, slot, channels, LANES), BF16),
+        vmem((slot, channels, LANES), BF16),
+        vmem((slot, channels, LANES), BF16),
         vmem((TAP_ROWS, region), F32),
         vmem((TAP_ROWS, region), F32),
         vmem((NMAX, 8, own), F32),

time: 116 us -> 103 us (0.89)
  Pallas kernels: 66.4 us -> 52.7 us
    pallas_call x1, Pallas kernels: 56.1 us -> 42.4 us  [call_main(): pl.pallas_call(functools.partial(main_kernel, own=own, channels=channels,...]
  transfers between devices with their start and end apart: 18 -> 18, of which waited for: 11 -> 11; matrix products, arithmetic and copies ran while one was open for 2% -> 2% of each run, Pallas kernels for 5% -> 6%
where the time goes in v3:
time: 103 us; the launch traced here: 102 us
  Pallas kernels  52.7 us (51%)
  waiting for transfers between devices  20.9 us (20%)
  starting transfers between devices  19.7 us (19%)
  local copies, waits for them, and re-layouts  4.29 us (4%)
  other arithmetic  3.5 us (3%)
    pallas_call x1, Pallas kernels, call_main(): pl.pallas_call(functools.partial(main_kernel, own=own, channels=channels,...  42.4 us
    ppermute x18, waiting for transfers between devices, swap(): return lax.ppermute(values, axis, [(j, j ^ bits) for j in range(size)])  20.9 us
    ppermute x18, starting transfers between devices, swap(): return lax.ppermute(values, axis, [(j, j ^ bits) for j in range(size)])  19.7 us
    unnamed x14, local copies, waits for them, and re-layouts  2.9 us
    pallas_call x1, Pallas kernels, local(): pl.pallas_call(functools.partial(update_kernel, channels=channels), out_s...  2.57 us
    pallas_call x1, Pallas kernels, local(): pl.pallas_call(functools.partial(prepare_kernel, own=own, frames=frames),...  2.22 us
  transfers between devices with their start and end apart: 18, of which 11 were waited for; matrix products, arithmetic and copies ran while one was open for 2% of the time, Pallas kernels for 6%

profile of v3, /device:TPU:0, one launch (start us, length us, event | category | flops | bytes accessed | tf_op | source)
XLA Modules:
  0.0 102.1 jit_solution(9418832423751755379)
XLA Ops:
  0.7 1.8 %pack_weights.1.pack_ref = f32[64,640]{1,0:T(8,128)} custom-call(f32[27,64]{1,0:T(8,128)} %bitcast.57, f32[64,512]{1,0:T(8,128)} %bitcast.50, f32[27,64]{1,0:T(8,128)} %w3_ref.3, f32[2,64]{1,0:T(2,128)} %bias_ref.1, f32[1,64]{1,0:T(1,128)} %bitcast.66), custom_call_target="tpu_custom_call" | custom-call | tf_op jit(solution)/shard_map/pack_weights/pallas_call | solution.py:789
  2.5 2.9 %collective-permute-start = (f32[64,640]{1,0:T(8,128)}, f32[64,640]{1,0:T(8,128)S(1)}, u32[]{:S(2)}, u32[]{:S(2)}) collective-permute-start(f32[64,640]{1,0:T(8,128)} %pack_weights.1.pack_ref), channel_id=1, source_target_pairs={{0,2},{1,3},{2,0},{3,1},{4,6},{5,7},{6,4},{7,5},{8,10},{9,11},{10,... | collective-permute-start | bytes 491528 | tf_op jit(solution)/shard_map/ppermute | solution.py:782
  5.4 1.5 %collective-permute-start.1 = (f32[64,640]{1,0:T(8,128)}, f32[64,640]{1,0:T(8,128)S(1)}, u32[]{:S(2)}, u32[]{:S(2)}) collective-permute-start(f32[64,640]{1,0:T(8,128)} %pack_weights.1.pack_ref), channel_id=1, source_target_pairs={{0,4},{1,5},{2,6},{3,7},{4,0},{5,1},{6,2},{7,3},{8,12},{9,13},{10,... | collective-permute-start | bytes 491528 | tf_op jit(solution)/shard_map/ppermute | solution.py:782
  7.0 0.0 collective-permute-start.2
  7.0 3.7 %collective-permute-done = f32[64,640]{1,0:T(8,128)S(1)} collective-permute-done((f32[64,640]{1,0:T(8,128)}, f32[64,640]{1,0:T(8,128)S(1)}, u32[]{:S(2)}, u32[]{:S(2)}) %collective-permute-start) | collective-permute-done | bytes 163872 | tf_op jit(solution)/shard_map/ppermute | solution.py:782
  10.7 4.1 %collective-permute-done.1 = f32[64,640]{1,0:T(8,128)S(1)} collective-permute-done((f32[64,640]{1,0:T(8,128)}, f32[64,640]{1,0:T(8,128)S(1)}, u32[]{:S(2)}, u32[]{:S(2)}) %collective-permute-start.1) | collective-permute-done | bytes 163872 | tf_op jit(solution)/shard_map/ppermute | solution.py:782
  14.8 0.0 collective-permute-done.2
  14.8 1.0 pad_maximum_fusion.x0_ref
  15.8 0.1 collective-permute-start.3
  15.9 2.2 %prepare_planes.1 = (f32[40,2048]{1,0:T(8,128)}, f32[8,128]{1,0:T(8,128)}) custom-call(s32[1]{0:T(128)} %bitcast.index_ref, s32[2]{0:T(128)} %kinds_ref.3, s32[2,4]{1,0:T(2,128)} %len_ref.1, f32[2,4]{1,0:T(2,128)} %cot_ref.1, f32[3,3]{1,0:T(4,128)} %small_ref.3, f32[3,8192]{1,0:T(4,128)} %images_ref.1, f32[3,8192]{1,0:T(4,128)} %probes_ref.1, ...), custom_call_target="tpu_custom_call" | custom-call | tf_op jit(solution)/shard_map/prepare_planes/pallas_call | solution.py:798
  18.1 0.9 copy-done.1
  19.0 42.4 %flow_block.1 = (f32[4,64,640]{2,1,0:T(8,128)}, f32[4,64,640]{2,1,0:T(8,128)}, f32[8,64,128]{2,1,0:T(8,128)}, f32[8,512]{1,0:T(8,128)}, f32[8,1024]{1,0:T(8,128)}) custom-call(s32[1]{0:T(128)} %bitcast.index_ref, f32[3]{0:T(128)} %u3_ref.1, f32[4,64,640]{2,1,0:T(8,128)} %copy-done, f32[4,64,640]{2,1,0:T(8,128)} %copy-done.1, f32[1,512]{1,0:T(1,128)} %bitcast.65, ...), custom_call_target="tpu_custom_call" | custom-call | tf_op jit(solution)/shard_map/flow_block/pallas_call | solution.py:508
  61.4 0.3 collective-permute-start.4
  61.8 2.0 %collective-permute-done.4 = f32[4,64,640]{2,1,0:T(8,128)S(1)} collective-permute-done((f32[4,64,640]{2,1,0:T(8,128)}, f32[4,64,640]{2,1,0:T(8,128)S(1)}, u32[]{:S(2)}, u32[]{:S(2)}) %collective-permute-start.4) | collective-permute-done | bytes 655392 | tf_op jit(solution)/shard_map/ppermute | solution.py:782
  63.7 1.2 %fusion.4 = (bf16[4,64,640]{2,1,0:T(8,128)(2,1)S(1)}, f32[4,64,640]{2,1,0:T(8,128)S(1)}) fusion(f32[4,64,640]{2,1,0:T(8,128)} %get-tuple-element.70, f32[4,64,640]{2,1,0:T(8,128)S(1)} %collective-permute-done.4), kind=kLoop, calls=%fused_computation.13 | loop fusion | flops 327680 | bytes 2293760 | tf_op jit(solution)/shard_map/convert_element_type | solution.py:815
  64.9 1.3 %collective-permute-start.5 = (bf16[64,640]{1,0:T(8,128)(2,1)S(1)}, bf16[64,640]{1,0:T(8,128)(2,1)S(1)}, u32[]{:S(2)}, u32[]{:S(2)}) collective-permute-start(bf16[64,640]{1,0:T(8,128)(2,1)S(1)} %get-tuple-element.108), channel_id=1, source_target_pairs={{0,2},{1,3},{2,0},{3,1},{4,6},{5,7},{6,4},{7,5},{8,10},{9,11},{10,... | collective-permute-start | bytes 245768 | tf_op jit(solution)/shard_map/ppermute | solution.py:782
  66.2 0.8 collective-permute-start.6
  67.1 1.4 %collective-permute-start.7 = (bf16[64,640]{1,0:T(8,128)(2,1)S(1)}, bf16[64,640]{1,0:T(8,128)(2,1)S(1)}, u32[]{:S(2)}, u32[]{:S(2)}) collective-permute-start(bf16[64,640]{1,0:T(8,128)(2,1)S(1)} %get-tuple-element.109), channel_id=1, source_target_pairs={{0,6},{1,7},{2,4},{3,5},{4,2},{5,3},{6,0},{7,1},{8,14},{9,15},{10,... | collective-permute-start | bytes 245768 | tf_op jit(solution)/shard_map/ppermute | solution.py:782
  68.5 1.2 %collective-permute-done.5 = bf16[64,640]{1,0:T(8,128)(2,1)S(1)} collective-permute-done((bf16[64,640]{1,0:T(8,128)(2,1)S(1)}, bf16[64,640]{1,0:T(8,128)(2,1)S(1)}, u32[]{:S(2)}, u32[]{:S(2)}) %collective-permute-start.5) | collective-permute-done | bytes 81952 | tf_op jit(solution)/shard_map/ppermute | solution.py:782
  69.7 1.5 %collective-permute-done.6 = bf16[64,640]{1,0:T(8,128)(2,1)S(1)} collective-permute-done((bf16[64,640]{1,0:T(8,128)(2,1)S(1)}, bf16[64,640]{1,0:T(8,128)(2,1)S(1)}, u32[]{:S(2)}, u32[]{:S(2)}) %collective-permute-start.6) | collective-permute-done | bytes 81952 | tf_op jit(solution)/shard_map/ppermute | solution.py:782
  71.2 1.2 %collective-permute-done.7 = bf16[64,640]{1,0:T(8,128)(2,1)S(1)} collective-permute-done((bf16[64,640]{1,0:T(8,128)(2,1)S(1)}, bf16[64,640]{1,0:T(8,128)(2,1)S(1)}, u32[]{:S(2)}, u32[]{:S(2)}) %collective-permute-start.7) | collective-permute-done | bytes 81952 | tf_op jit(solution)/shard_map/ppermute | solution.py:782
  72.5 0.7 copy-done.6
  73.2 1.5 %collective-permute-start.8 = (f32[8,1024]{1,0:T(8,128)S(1)}, f32[8,1024]{1,0:T(8,128)S(1)}, u32[]{:S(2)}, u32[]{:S(2)}) collective-permute-start(f32[8,1024]{1,0:T(8,128)S(1)} %copy-done.6), channel_id=1, source_target_pairs={{0,2},{1,3},{2,0},{3,1},{4,6},{5,7},{6,4},{7,5},{8,10},{9,11},{10,... | collective-permute-start | bytes 98312 | tf_op jit(solution)/shard_map/ppermute | solution.py:782
  74.6 0.9 collective-permute-start.9
  75.5 1.2 %collective-permute-start.10 = (f32[8,1024]{1,0:T(8,128)S(1)}, f32[8,1024]{1,0:T(8,128)S(1)}, u32[]{:S(2)}, u32[]{:S(2)}) collective-permute-start(f32[8,1024]{1,0:T(8,128)S(1)} %copy-done.6), channel_id=1, source_target_pairs={{0,6},{1,7},{2,4},{3,5},{4,2},{5,3},{6,0},{7,1},{8,14},{9,15},{10,... | collective-permute-start | bytes 98312 | tf_op jit(solution)/shard_map/ppermute | solution.py:782
  76.7 1.6 %collective-permute-start.12 = (bf16[64,640]{1,0:T(8,128)(2,1)S(1)}, bf16[64,640]{1,0:T(8,128)(2,1)S(1)}, u32[]{:S(2)}, u32[]{:S(2)}) collective-permute-start(bf16[64,640]{1,0:T(8,128)(2,1)S(1)} %fusion.3), channel_id=1, source_target_pairs={{0,8},{8,0},{16,24},{24,16},{1,9},{9,1},{17,25},{25,17},{2,10},{10... | collective-permute-start | bytes 245768 | tf_op jit(solution)/shard_map/ppermute | solution.py:782
  78.3 0.0 collective-permute-done.8
  78.3 0.3 collective-permute-done.9
  78.6 1.8 %collective-permute-done.10 = f32[8,1024]{1,0:T(8,128)S(1)} collective-permute-done((f32[8,1024]{1,0:T(8,128)S(1)}, f32[8,1024]{1,0:T(8,128)S(1)}, u32[]{:S(2)}, u32[]{:S(2)}) %collective-permute-start.10) | collective-permute-done | bytes 32800 | tf_op jit(solution)/shard_map/ppermute | solution.py:782
  80.3 0.0 copy-start.2
  80.3 0.1 collective-permute-start.11
  80.4 0.7 collective-permute-done.12
  81.1 0.0 copy-start.3
  81.2 2.7 %collective-permute-start.13 = (bf16[64,640]{1,0:T(8,128)(2,1)S(1)}, bf16[64,640]{1,0:T(8,128)(2,1)S(1)}, u32[]{:S(2)}, u32[]{:S(2)}) collective-permute-start(bf16[64,640]{1,0:T(8,128)(2,1)S(1)} %add_convert_fusion.a_ref), channel_id=1, source_target_pairs={{0,16},{8,24},{16,0},{24,8},{1,17},{9,25},{17,1},{25,9},{2,18},{10... | collective-permute-start | bytes 245768 | tf_op jit(solution)/shard_map/ppermute | solution.py:782
  83.8 1.4 %dynamic-slice_bitcast_fusion.cols_ref = f32[64,128]{1,0:T(8,128)} fusion(f32[8,64,128]{2,1,0:T(8,128)} %get-tuple-element.77, s32[]{:T(128)S(6)} %select_n.4), kind=kLoop, calls=%fused_computation.11 | loop fusion | bytes 65540 | tf_op jit(solution)/shard_map/jit(dynamic_index_in_dim)/squeeze | solution.py:840
  85.2 3.0 %collective-permute-done.13.b_ref = bf16[64,640]{1,0:T(8,128)(2,1)S(1)} collective-permute-done((bf16[64,640]{1,0:T(8,128)(2,1)S(1)}, bf16[64,640]{1,0:T(8,128)(2,1)S(1)}, u32[]{:S(2)}, u32[]{:S(2)}) %collective-permute-start.13) | collective-permute-done | bytes 81952 | tf_op jit(solution)/shard_map/ppermute | solution.py:782
  88.2 0.6 copy-done.5
  88.8 1.8 %norm_parts.1 = (f32[64,640]{1,0:T(8,128)}, f32[8,128]{1,0:T(8,128)}) custom-call(s32[1]{0:T(128)} %bitcast.index_ref, bf16[64,640]{1,0:T(8,128)(2,1)} %copy-done.3, bf16[64,640]{1,0:T(8,128)(2,1)} %copy-done.5, f32[64,640]{1,0:T(8,128)} %pack_weights.1.pack_ref, f32[64,128]{1,0:T(8,128)} %dynamic-slice_bitcast_fusion.cols_ref, ...), custom_call_target="tpu_custom_call" | custom-call | tf_op jit(solution)/shard_map/norm_parts/pallas_call | solution.py:841
  90.6 1.4 %collective-permute-done.14 = f32[8,128]{1,0:T(8,128)S(1)} collective-permute-done((f32[8,128]{1,0:T(8,128)}, f32[8,128]{1,0:T(8,128)S(1)}, u32[]{:S(2)}, u32[]{:S(2)}) %collective-permute-start.14) | collective-permute-done | bytes 4128 | tf_op jit(solution)/shard_map/ppermute | solution.py:782
  92.0 0.7 add.28
  92.7 0.0 collective-permute-start.15
  92.7 1.2 %collective-permute-start.16 = (f32[8,128]{1,0:T(8,128)S(1)}, f32[8,128]{1,0:T(8,128)S(1)}, u32[]{:S(2)}, u32[]{:S(2)}) collective-permute-start(f32[8,128]{1,0:T(8,128)S(1)} %add.28), channel_id=1, source_target_pairs={{0,4},{1,5},{2,6},{3,7},{4,0},{5,1},{6,2},{7,3},{8,12},{9,13},{10,... | collective-permute-start | bytes 12296 | tf_op jit(solution)/shard_map/ppermute | solution.py:782
  93.9 2.3 %collective-permute-start.17 = (f32[8,128]{1,0:T(8,128)S(1)}, f32[8,128]{1,0:T(8,128)S(1)}, u32[]{:S(2)}, u32[]{:S(2)}) collective-permute-start(f32[8,128]{1,0:T(8,128)S(1)} %add.28), channel_id=1, source_target_pairs={{0,6},{1,7},{2,4},{3,5},{4,2},{5,3},{6,0},{7,1},{8,14},{9,15},{10,... | collective-permute-start | bytes 12296 | tf_op jit(solution)/shard_map/ppermute | solution.py:782
  96.2 0.7 copy-done.4
  96.8 1.9 %assemble_outputs.1 = (f32[3,8192]{1,0:T(4,128)}, f32[3,8192]{1,0:T(4,128)}, f32[2,4]{1,0:T(2,128)}) custom-call(s32[1]{0:T(128)} %bitcast.index_ref, s32[2]{0:T(128)} %kinds_ref.3, f32[4,8,1024]{2,1,0:T(8,128)} %copy-done.2, f32[4,8,1024]{2,1,0:T(8,128)} %copy-done.4, f32[3,3]{1,0:T(4,128)} %small_ref.3), custom_call_target="tpu_custom_call" | custom-call | tf_op jit(solution)/shard_map/assemble_outputs/pallas_call | solution.py:827
  98.7 0.0 collective-permute-done.15
  98.8 0.6 pad_maximum_fusion.2.totals_ref
  99.4 2.6 %adam_update.1 = (f32[1,1]{1,0:T(1,128)}, f32[27,64]{1,0:T(8,128)}, f32[27,64]{1,0:T(8,128)}, f32[27,64]{1,0:T(8,128)}, f32[64,512]{1,0:T(8,128)}, /*index=5*/f3...) custom-call(f32[4,128]{1,0:T(4,128)} %pad_maximum_fusion.2.totals_re, ...), custom_call_target="tpu_custom_call" | custom-call | tf_op jit(solution)/shard_map/adam_update/pallas_call | solution.py:870
  (21 shorter events, 0.1 us)
Async XLA Ops:
  2.5 8.2 %collective-permute-start = (f32[64,640]{1,0:T(8,128)}, f32[64,640]{1,0:T(8,128)S(1)}, u32[]{:S(2)}, u32[]{:S(2)}) collective-permute-start(f32[64,640]{1,0:T(8,128)} %pack_weights.1.pack_ref), channel_id=1, source_target_pairs={{0,2},{1,3},{2,0},{3,1},{4,6},{5,7},{6,4},{7,5},{8,10},{9,11},{10,... | collective-permute-start | bytes 491528 | tf_op jit(solution)/shard_map/ppermute | solution.py:782
  5.4 9.4 %collective-permute-start.1 = (f32[64,640]{1,0:T(8,128)}, f32[64,640]{1,0:T(8,128)S(1)}, u32[]{:S(2)}, u32[]{:S(2)}) collective-permute-start(f32[64,640]{1,0:T(8,128)} %pack_weights.1.pack_ref), channel_id=1, source_target_pairs={{0,4},{1,5},{2,6},{3,7},{4,0},{5,1},{6,2},{7,3},{8,12},{9,13},{10,... | collective-permute-start | bytes 491528 | tf_op jit(solution)/shard_map/ppermute | solution.py:782
  7.0 7.9 %collective-permute-start.2 = (f32[64,640]{1,0:T(8,128)}, f32[64,640]{1,0:T(8,128)S(1)}, u32[]{:S(2)}, u32[]{:S(2)}) collective-permute-start(f32[64,640]{1,0:T(8,128)} %pack_weights.1.pack_ref), channel_id=1, source_target_pairs={{0,6},{1,7},{2,4},{3,5},{4,2},{5,3},{6,0},{7,1},{8,14},{9,15},{10,... | collective-permute-start | bytes 491528 | tf_op jit(solution)/shard_map/ppermute | solution.py:782
  15.8 3.2 %copy-start = (f32[4,64,640]{2,1,0:T(8,128)}, f32[4,64,640]{2,1,0:T(8,128)S(1)}, u32[]{:S(2)}) copy-start(f32[4,64,640]{2,1,0:T(8,128)S(1)} %pad_maximum_fusion.x0_ref) | copy-start | bytes 1966084
  15.8 2.3 %collective-permute-start.3 = (f32[4,64,640]{2,1,0:T(8,128)S(1)}, f32[4,64,640]{2,1,0:T(8,128)S(1)}, u32[]{:S(2)}, u32[]{:S(2)}) collective-permute-start(f32[4,64,640]{2,1,0:T(8,128)S(1)} %pad_maximum_fusion.x0_ref), channel_id=1, source_target_pairs={{0,1},{1,0},{2,3},{3,2},{4,5},{5,4},{6,7},{7,6},{8,9},{9,8},{10,11... | collective-permute-start | bytes 1966088 | tf_op jit(solution)/shard_map/ppermute | solution.py:782
  18.1 0.9 copy-start.1
  61.4 2.3 %collective-permute-start.4 = (f32[4,64,640]{2,1,0:T(8,128)}, f32[4,64,640]{2,1,0:T(8,128)S(1)}, u32[]{:S(2)}, u32[]{:S(2)}) collective-permute-start(f32[4,64,640]{2,1,0:T(8,128)} %get-tuple-element.71), channel_id=1, source_target_pairs={{0,1},{1,0},{2,3},{3,2},{4,5},{5,4},{6,7},{7,6},{8,9},{9,8},{10,11... | collective-permute-start | bytes 1966088 | tf_op jit(solution)/shard_map/ppermute | solution.py:782
  64.9 4.8 %collective-permute-start.5 = (bf16[64,640]{1,0:T(8,128)(2,1)S(1)}, bf16[64,640]{1,0:T(8,128)(2,1)S(1)}, u32[]{:S(2)}, u32[]{:S(2)}) collective-permute-start(bf16[64,640]{1,0:T(8,128)(2,1)S(1)} %get-tuple-element.108), channel_id=1, source_target_pairs={{0,2},{1,3},{2,0},{3,1},{4,6},{5,7},{6,4},{7,5},{8,10},{9,11},{10,... | collective-permute-start | bytes 245768 | tf_op jit(solution)/shard_map/ppermute | solution.py:782
  66.2 5.0 %collective-permute-start.6 = (bf16[64,640]{1,0:T(8,128)(2,1)S(1)}, bf16[64,640]{1,0:T(8,128)(2,1)S(1)}, u32[]{:S(2)}, u32[]{:S(2)}) collective-permute-start(bf16[64,640]{1,0:T(8,128)(2,1)S(1)} %get-tuple-element.110), channel_id=1, source_target_pairs={{0,4},{1,5},{2,6},{3,7},{4,0},{5,1},{6,2},{7,3},{8,12},{9,13},{10,... | collective-permute-start | bytes 245768 | tf_op jit(solution)/shard_map/ppermute | solution.py:782
  67.1 5.4 %collective-permute-start.7 = (bf16[64,640]{1,0:T(8,128)(2,1)S(1)}, bf16[64,640]{1,0:T(8,128)(2,1)S(1)}, u32[]{:S(2)}, u32[]{:S(2)}) collective-permute-start(bf16[64,640]{1,0:T(8,128)(2,1)S(1)} %get-tuple-element.109), channel_id=1, source_target_pairs={{0,6},{1,7},{2,4},{3,5},{4,2},{5,3},{6,0},{7,1},{8,14},{9,15},{10,... | collective-permute-start | bytes 245768 | tf_op jit(solution)/shard_map/ppermute | solution.py:782
  72.4 0.8 copy-start.6
  73.2 5.1 %collective-permute-start.8 = (f32[8,1024]{1,0:T(8,128)S(1)}, f32[8,1024]{1,0:T(8,128)S(1)}, u32[]{:S(2)}, u32[]{:S(2)}) collective-permute-start(f32[8,1024]{1,0:T(8,128)S(1)} %copy-done.6), channel_id=1, source_target_pairs={{0,2},{1,3},{2,0},{3,1},{4,6},{5,7},{6,4},{7,5},{8,10},{9,11},{10,... | collective-permute-start | bytes 98312 | tf_op jit(solution)/shard_map/ppermute | solution.py:782
  74.6 3.9 %collective-permute-start.9 = (f32[8,1024]{1,0:T(8,128)S(1)}, f32[8,1024]{1,0:T(8,128)S(1)}, u32[]{:S(2)}, u32[]{:S(2)}) collective-permute-start(f32[8,1024]{1,0:T(8,128)S(1)} %copy-done.6), channel_id=1, source_target_pairs={{0,4},{1,5},{2,6},{3,7},{4,0},{5,1},{6,2},{7,3},{8,12},{9,13},{10,... | collective-permute-start | bytes 98312 | tf_op jit(solution)/shard_map/ppermute | solution.py:782
  75.5 4.8 %collective-permute-start.10 = (f32[8,1024]{1,0:T(8,128)S(1)}, f32[8,1024]{1,0:T(8,128)S(1)}, u32[]{:S(2)}, u32[]{:S(2)}) collective-permute-start(f32[8,1024]{1,0:T(8,128)S(1)} %copy-done.6), channel_id=1, source_target_pairs={{0,6},{1,7},{2,4},{3,5},{4,2},{5,3},{6,0},{7,1},{8,14},{9,15},{10,... | collective-permute-start | bytes 98312 | tf_op jit(solution)/shard_map/ppermute | solution.py:782
  76.7 4.4 %collective-permute-start.12 = (bf16[64,640]{1,0:T(8,128)(2,1)S(1)}, bf16[64,640]{1,0:T(8,128)(2,1)S(1)}, u32[]{:S(2)}, u32[]{:S(2)}) collective-permute-start(bf16[64,640]{1,0:T(8,128)(2,1)S(1)} %fusion.3), channel_id=1, source_target_pairs={{0,8},{8,0},{16,24},{24,16},{1,9},{9,1},{17,25},{25,17},{2,10},{10... | collective-permute-start | bytes 245768 | tf_op jit(solution)/shard_map/ppermute | solution.py:782
  80.3 4.8 %copy-start.2 = (f32[4,8,1024]{2,1,0:T(8,128)}, f32[4,8,1024]{2,1,0:T(8,128)S(1)}, u32[]{:S(2)}) copy-start(f32[4,8,1024]{2,1,0:T(8,128)S(1)} %pad_maximum_fusion.1.p0_ref) | copy-start | bytes 393220
  80.3 15.8 %collective-permute-start.11 = (f32[4,8,1024]{2,1,0:T(8,128)S(1)}, f32[4,8,1024]{2,1,0:T(8,128)S(1)}, u32[]{:S(2)}, u32[]{:S(2)}) collective-permute-start(f32[4,8,1024]{2,1,0:T(8,128)S(1)} %pad_maximum_fusion.1.p0_ref), channel_id=1, source_target_pairs={{0,1},{1,0},{2,3},{3,2},{4,5},{5,4},{6,7},{7,6},{8,9},{9,8},{10,11... | collective-permute-start | bytes 393224 | tf_op jit(solution)/shard_map/ppermute | solution.py:782
  81.1 7.0 %copy-start.3 = (bf16[64,640]{1,0:T(8,128)(2,1)}, bf16[64,640]{1,0:T(8,128)(2,1)S(1)}, u32[]{:S(2)}) copy-start(bf16[64,640]{1,0:T(8,128)(2,1)S(1)} %add_convert_fusion.a_ref) | copy-start | bytes 245764
  81.2 7.0 %collective-permute-start.13 = (bf16[64,640]{1,0:T(8,128)(2,1)S(1)}, bf16[64,640]{1,0:T(8,128)(2,1)S(1)}, u32[]{:S(2)}, u32[]{:S(2)}) collective-permute-start(bf16[64,640]{1,0:T(8,128)(2,1)S(1)} %add_convert_fusion.a_ref), channel_id=1, source_target_pairs={{0,16},{8,24},{16,0},{24,8},{1,17},{9,25},{17,1},{25,9},{2,18},{10... | collective-permute-start | bytes 245768 | tf_op jit(solution)/shard_map/ppermute | solution.py:782
  88.2 0.6 copy-start.5
  90.6 1.4 %collective-permute-start.14 = (f32[8,128]{1,0:T(8,128)}, f32[8,128]{1,0:T(8,128)S(1)}, u32[]{:S(2)}, u32[]{:S(2)}) collective-permute-start(f32[8,128]{1,0:T(8,128)} %get-tuple-element.79), channel_id=1, source_target_pairs={{0,1},{1,0},{2,3},{3,2},{4,5},{5,4},{6,7},{7,6},{8,9},{9,8},{10,11... | collective-permute-start | bytes 12296 | tf_op jit(solution)/shard_map/ppermute | solution.py:782
  92.7 6.0 %collective-permute-start.15 = (f32[8,128]{1,0:T(8,128)S(1)}, f32[8,128]{1,0:T(8,128)S(1)}, u32[]{:S(2)}, u32[]{:S(2)}) collective-permute-start(f32[8,128]{1,0:T(8,128)S(1)} %add.28), channel_id=1, source_target_pairs={{0,2},{1,3},{2,0},{3,1},{4,6},{5,7},{6,4},{7,5},{8,10},{9,11},{10,... | collective-permute-start | bytes 12296 | tf_op jit(solution)/shard_map/ppermute | solution.py:782
  92.7 6.0 %collective-permute-start.16 = (f32[8,128]{1,0:T(8,128)S(1)}, f32[8,128]{1,0:T(8,128)S(1)}, u32[]{:S(2)}, u32[]{:S(2)}) collective-permute-start(f32[8,128]{1,0:T(8,128)S(1)} %add.28), channel_id=1, source_target_pairs={{0,4},{1,5},{2,6},{3,7},{4,0},{5,1},{6,2},{7,3},{8,12},{9,13},{10,... | collective-permute-start | bytes 12296 | tf_op jit(solution)/shard_map/ppermute | solution.py:782
  93.9 4.9 %collective-permute-start.17 = (f32[8,128]{1,0:T(8,128)S(1)}, f32[8,128]{1,0:T(8,128)S(1)}, u32[]{:S(2)}, u32[]{:S(2)}) collective-permute-start(f32[8,128]{1,0:T(8,128)S(1)} %add.28), channel_id=1, source_target_pairs={{0,6},{1,7},{2,4},{3,5},{4,2},{5,3},{6,0},{7,1},{8,14},{9,15},{10,... | collective-permute-start | bytes 12296 | tf_op jit(solution)/shard_map/ppermute | solution.py:782
  96.2 0.7 copy-start.4

commit v4 on v3

--- a/solution.py
+++ b/solution.py
@@ -118,21 +118,58 @@
     return values / jnp.sqrt(square + 1e-12)
 
 
-def main_kernel(
-    index_ref, u3_ref, x0_ref, x1_ref, u2_ref, planes_ref, small_ref,
-    keep_ref, send_ref, cols_ref, rows_ref, og_ref,
-    w_s, w13_s, w2_s, w2t_s, wout_s, bias_s, taps_s, sl1_s, sl2_s, cv1_s, cv2_s,
-    lin1_s, lin2_s, gt1_s, gt2_s, acc1_s, acc2_s, tan1_s, tan2_s, g1_s, g2_s, hid1_s, hid2_s,
-    q_s, q0_s, comb_s, *, own, channels, chips,
-):
+def visits(blocks):
+    pairs = blocks // 2
+    listed = [(2 * (blocks - 1), 2)] if blocks % 2 else []
+    return listed + [(4 * j, 4) for j in [pairs - 1] + list(range(pairs - 1)) if pairs]
+
+
+def margins(uses, valid):
+    for extra in range(64):
+        for before in range(extra + 1):
+            size = extra + valid
+            wrong = size < 4
+            for first, blocks in uses:
+                held = {}
+                for at, n in visits(blocks):
+                    place = min(max(first + at + before, 0), size - n)
+                    for h in range(n):
+                        held[place + h] = first + at + h
+                wrong = wrong or any(held.get(before + c, c) != c for c in range(valid))
+            if not wrong:
+                return before, extra - before
+    raise ValueError("no margins")
+
+
+def buffer_plan(own):
+    chunks = own // LANES
+    blocks = own // BLOCK
+    ring = chunks + 2
+    return {
+        "early": margins([(-4, blocks + 4)], chunks),
+        "second": margins([(-3, blocks + 3)], chunks),
+        "late": margins([(-2, blocks + 2), (-1, blocks + 1)], chunks),
+        "kept": margins([(-2, blocks + 3), (0, blocks + 1), (-1, blocks + 2)], ring),
+    }
+
+
+def main_kernel(index_ref, u3_ref, u2_ref, planes_ref, small_ref, *refs, own, channels, chips):
+    packs = refs[: 2 * chips]
+    keep_ref, send_ref, og_ref, cols_ref, rows_ref = refs[2 * chips : 2 * chips + 5]
+    (
+        w_s, w13_s, w2_s, w2t_s, wout_s, bias_s, taps_s, sl1_s, sl2_s, cv1_s, cv2_s,
+        lin1a_s, lin2a_s, gt1a_s, gt2a_s, lin1b_s, lin2b_s, gt1b_s, gt2b_s,
+        part1_s, part2_s, mid1_s, mid2_s, tan1a_s, tan2a_s, g1a_s, g2a_s, tan1b_s, tan2b_s, g1b_s, g2b_s,
+        tan1c_s, tan2c_s, g1c_s, g2c_s, hid1_s, hid2_s,
+        q_s, q0_s, comb_s, tile_s, cols_s,
+    ) = refs[2 * chips + 5 :]
     me = index_ref[0]
     rows_own = channels // (2 * chips)
     region = own + 2 * HALO
     all_sum = functools.partial(jnp.sum, keepdims=True)
 
-    for m in range(chips):
-        for b, ref in ((0, x0_ref), (1, x1_ref)):
-            w_s[jnp.bitwise_xor(me, 2 * m + b)] = ref[m]
+    for shard, ref in enumerate(packs):
+        w_s[jnp.bitwise_xor(me, shard)] = ref[...]
     tile = w_s[:, :, channels:].reshape(channels, LANES)
     w2t = w_s[:, :, 0:channels].reshape(channels, channels)
     lane = iota((1, LANES), 1)
@@ -170,7 +207,8 @@
     sigma1 = jnp.sqrt(square1)
     sigma2 = jnp.sqrt(square2)
     sigma3 = jnp.sqrt(square3)
-    cols_ref[...] = jnp.where(lane == 0, u1, jnp.where(lane == 1, v2, v3)).reshape(cols_ref.shape)
+    cols_s[...] = jnp.where(lane == 0, u1, jnp.where(lane == 1, v2, v3)).reshape(cols_s.shape)
+    cols_ref[...] = cols_s[me]
     sigma_row = jnp.where(lane == 0, sigma1, jnp.where(lane == 1, sigma2, sigma3))
     rows_ref[...] = jnp.zeros(rows_ref.shape, F32)
     rows_ref[0:1, :] = u2
@@ -179,20 +217,24 @@
     rows_ref[3:4, 0:LANES] = sigma_row
 
     scaled = taps_one * (SHRINK / sigma1) + taps_three * (SHRINK / sigma3)
-    w13_s[0:channels] = jnp.where(is_one, scaled, 0.0).astype(BF16)
-    w13_s[channels:] = jnp.where(is_three, scaled, 0.0).astype(BF16)
+    halved = jnp.where(is_one, 0.5 * scaled, 0.0)
+    rest1 = 0.5 * tile[:, TAP_ROWS + 1 : TAP_ROWS + 2]
+    for i in range(3):
+        part = rest1.astype(BF16).astype(F32)
+        halved = jnp.where(lane == TAP_ROWS + i, part, halved)
+        rest1 = rest1 - part
+    w13_s[0:channels] = halved.astype(BF16)
+    w13_s[channels:] = jnp.where(is_three, 0.5 * scaled, 0.0).astype(BF16)
     flipped = scaled.T
     blocks = [pltpu.roll(flipped[(8 - t) * 8 : (9 - t) * 8], 4, 0) for t in range(9)]
     flipped = jnp.concatenate(blocks + [jnp.zeros((8, channels), F32)], axis=0)
     first_rows = iota((TAP_ROWS + 8, 1), 0) % 8 < 4
     wout_s[:, 0:channels] = jnp.where(first_rows, flipped, 0.0).astype(BF16)
     wout_s[:, channels:] = jnp.where(first_rows, 0.0, flipped).astype(BF16)
-    w2t_scaled = w2t * (SHRINK / sigma2)
+    w2t_scaled = w2t * (0.5 * SHRINK / sigma2)
     w2t_s[...] = w2t_scaled.astype(BF16)
     w2_s[...] = w2t_scaled.T.astype(BF16)
-    for layer in range(2):
-        column = tile[:, TAP_ROWS + 1 + layer : TAP_ROWS + 2 + layer]
-        bias_s[layer] = jnp.broadcast_to(column, (channels, LANES))
+    bias_s[...] = jnp.broadcast_to(0.5 * tile[:, TAP_ROWS + 2 : TAP_ROWS + 3], (channels, LANES))
 
     shift8 = small_ref[:, 0:1]
     scale8 = small_ref[:, 1:2]
@@ -206,11 +248,11 @@
         return [planes_ref[32 + i : 33 + i, lanes] for i in range(4)]
 
     def put_taps(slot, pieces, lanes):
-        full = jnp.concatenate(pieces + [jnp.zeros((8, lanes.size), F32)], axis=0).astype(BF16)
+        ones = jnp.where(iota((8, lanes.size), 0) < 3, 1.0 if slot == 0 else 0.0, 0.0)
+        full = jnp.concatenate(pieces + [ones], axis=0).astype(BF16)
         for c in range(lanes.size // LANES):
             chunk = lanes.start // LANES + c
-            taps_s[slot, chunk, 0 : TAP_ROWS + 8] = full[:, c * LANES : (c + 1) * LANES]
-            taps_s[slot, chunk, TAP_ROWS + 8 :] = jnp.zeros((LANES - TAP_ROWS - 8, LANES), BF16)
+            taps_s[slot, chunk] = full[:, c * LANES : (c + 1) * LANES]
 
     whole = pl.ds(0, region)
     h8 = (planes_ref[0:8] + shift8) * scale8
@@ -225,14 +267,25 @@
 
     own_blocks = own // BLOCK
     ring = own + BLOCK
+    plan = buffer_plan(own)
+    own_before = [plan[name][0] for name in ("early", "second", "late")]
+    kept_before = plan["kept"][0]
+    tan_s = (
+        (tan1a_s, tan2a_s, g1a_s, g2a_s),
+        (tan1b_s, tan2b_s, g1b_s, g2b_s),
+        (tan1c_s, tan2c_s, g1c_s, g2c_s),
+    )
+    kept_s = ((lin1a_s, lin2a_s, gt1a_s, gt2a_s), (lin1b_s, lin2b_s, gt1b_s, gt2b_s))
 
     def over_blocks(count, body, carry=0):
         pairs = count // 2
-        if pairs:
-            carry = lax.fori_loop(0, pairs, lambda j, kept: body(2 * j * BLOCK, 2 * BLOCK, kept), carry)
         if count % 2:
             carry = body((count - 1) * BLOCK, BLOCK, carry)
-        return carry
+
+        def turn(j, kept):
+            return body(jnp.where(j == 0, pairs - 1, j - 1) * (2 * BLOCK), 2 * BLOCK, kept)
+
+        return lax.fori_loop(0, pairs, turn, carry)
 
     def halves(start, size, base, width):
         places = []
@@ -242,6 +295,11 @@
             places.append(jnp.where((chunk >= 0) & (chunk < chunks), chunk, chunks))
         return places
 
+    def run_of(ref, start, size, base, before):
+        first = start // LANES - base // LANES + before
+        first = jnp.clip(first, 0, ref.shape[0] - size // LANES)
+        return [first + h for h in range(size // LANES)]
+
     def put(ref, places, value):
         for h, place in enumerate(places):
             ref[place] = value[:, h * LANES : (h + 1) * LANES]
@@ -249,14 +307,13 @@
     def join(ref, first, count):
         return jnp.concatenate([ref[first + i] for i in range(count)], axis=1)
 
-    def activation(act, slope_ref, curve_ref, lanes, ring_places):
-        tanh = jnp.tanh(0.5 * act)
-        half = 0.5 * tanh
-        rest = 0.5 - half
-        sig = (1.0 / 1.1) * (0.5 + half)
-        hidden = act * sig
-        slope_ref[:, lanes] = sig + hidden * rest
-        put(curve_ref, ring_places, (rest * ((sig + sig) - tanh * hidden)).astype(BF16))
+    def activation(half_act, slope_ref, curve_ref, lanes, ring_places):
+        tanh = jnp.tanh(half_act)
+        sig = (1.0 / 1.1) + (1.0 / 1.1) * tanh
+        hidden = half_act * sig
+        bent = tanh * hidden
+        slope_ref[:, lanes] = (sig + hidden) - bent
+        put(curve_ref, ring_places, ((1.0 - tanh) * (sig - bent)).astype(BF16))
         return hidden.astype(BF16)
 
     def start_body(at, size, carry):
@@ -264,15 +321,12 @@
         lanes = pl.ds(start, size)
         count = size // LANES
         ring_places = halves(start, size, HALO - LANES, ring)
-        own_places = halves(start, size, HALO, own)
-        act1 = dot_nn(w13_s[0:channels], join(taps_s.at[0], start // LANES, count))
-        bias1 = bias_s[0]
-        hidden1 = activation(
-            act1 + jnp.concatenate([bias1] * count, axis=1), sl1_s, cv1_s, lanes, ring_places
-        )
+        own_places = run_of(hid1_s, start, size, HALO, own_before[0])
+        act1 = dot_nn(w13_s[0:channels, 0 : TAP_ROWS + 8], join(taps_s.at[0], start // LANES, count))
+        hidden1 = activation(act1, sl1_s, cv1_s, lanes, ring_places)
         put(hid1_s, own_places, hidden1)
         act2 = dot_nn(w2_s[...], hidden1)
-        bias2 = bias_s[1]
+        bias2 = bias_s[...]
         hidden2 = activation(
             act2 + jnp.concatenate([bias2] * count, axis=1), sl2_s, cv2_s, lanes, ring_places
         )
@@ -287,39 +341,60 @@
         offset = LANES * (stage - 1)
         count = own_blocks + 5 - stage
         tan_slot = min(stage, 3) - 1
+        tan_refs = tan_s[tan_slot]
 
         def body(at, size, carry):
             start = pl.multiple_of(offset + at, LANES)
             lanes = pl.ds(start, size)
-            ring_places = halves(start, size, HALO - LANES, ring)
-            own_places = halves(start, size, HALO, own)
-
-            def pair_up(acc_ref, mine_ref, other_ref, value, slot):
+            own_places = run_of(tan_refs[0], start, size, HALO, own_before[tan_slot])
+            if stage == 1:
+                ring_places = halves(start, size, HALO - LANES, ring)
+            else:
+                ring_places = run_of(mid1_s, start, size, HALO - LANES, kept_before)
+            shift = -kept_before if stage == 4 else 0
+
+            def pair_up(value, save_to, partner, add_from, mix_to):
                 for h, place in enumerate(ring_places):
                     part = value[:, h * LANES : (h + 1) * LANES]
-                    if stage <= 2:
-                        mine_ref[stage - 1, place] = part.astype(BF16)
-                    else:
-                        acc_ref[place] += part * other_ref[slot, place].astype(F32)
-
-            slot = 4 - stage
+                    if save_to is not None:
+                        save_to[place] = part.astype(BF16)
+                        continue
+                    part = (part.astype(BF16) * partner[place + shift]).astype(F32)
+                    if add_from is not None:
+                        part = part + add_from[place].astype(F32)
+                    mix_to[place] = part.astype(BF16)
+
+            if stage <= 2:
+                lin1_to, lin2_to, gt1_to, gt2_to = kept_s[stage - 1]
+                moves = ((lin1_to,), (gt2_to,), (lin2_to,), (gt1_to,))
+                moves = [(place, None, None, None) for (place,) in moves]
+            else:
+                lin1_of, lin2_of, gt1_of, gt2_of = kept_s[4 - stage]
+                sum1, sum2 = (None, None) if stage == 3 else (mid1_s, mid2_s)
+                end1, end2 = (mid1_s, mid2_s) if stage == 3 else (lin1b_s, lin2b_s)
+                moves = (
+                    (None, gt1_of, sum1, part1_s),
+                    (None, lin2_of, sum2, part2_s),
+                    (None, gt2_of, part2_s, end2),
+                    (None, lin1_of, part1_s, end1),
+                )
             taps = join(taps_s.at[stage], start // LANES, size // LANES)
-            lin1 = dot_nn(w13_s[0:channels], taps)
+            lin1 = dot_nn(w13_s[0:channels, 0 : TAP_ROWS + 8], taps)
             tan1 = (sl1_s[:, lanes] * lin1).astype(BF16)
-            put(tan1_s.at[tan_slot], own_places, tan1)
-            pair_up(acc1_s, lin1_s, gt1_s, lin1, slot)
-            gt2 = dot_nn(w13_s[channels:], taps)
+            put(tan_refs[0], own_places, tan1)
+            pair_up(lin1, *moves[0])
+            gt2 = dot_nn(w13_s[channels:, 0 : TAP_ROWS + 8], taps)
             g2 = (sl2_s[:, lanes] * gt2).astype(BF16)
-            put(g2_s.at[tan_slot], own_places, g2)
-            pair_up(acc2_s, gt2_s, lin2_s, gt2, slot)
+            put(tan_refs[3], own_places, g2)
+            pair_up(gt2, *moves[1])
             lin2 = dot_nn(w2_s[...], tan1)
             tan2 = (sl2_s[:, lanes] * lin2).astype(BF16)
-            put(tan2_s.at[tan_slot], own_places, tan2)
-            pair_up(acc2_s, lin2_s, gt2_s, lin2, slot)
+            put(tan_refs[1], own_places, tan2)
+            pair_up(lin2, *moves[2])
             gt1 = dot_nn(w2t_s[...], g2)
             g1 = (sl1_s[:, lanes] * gt1).astype(BF16)
-            put(g1_s.at[tan_slot], own_places, g1)
-            pair_up(acc1_s, gt1_s, lin1_s, gt1, slot)
+            put(tan_refs[2], own_places, g1)
+            pair_up(gt1, *moves[3])
             q_fwd = dot_nn(wout_s[:, 0:channels], tan2)[0:TAP_ROWS]
             q_s[:, lanes] = q_fwd + dot_nn(wout_s[:, channels:], g1)[0:TAP_ROWS]
             return carry
@@ -350,42 +425,40 @@
         one = None
         three = None
         for left_one, left_three, slot in tap_pairs:
-            part_one = dot_nt(left_one, own_taps(slot))
-            part_three = dot_nt(left_three, own_taps(slot))
+            taps = own_taps(slot)
+            part_one = dot_nt(taps, left_one)
+            part_three = dot_nt(taps, left_three)
             one = part_one if one is None else one + part_one
             three = part_three if three is None else three + part_three
-        tile_part = jnp.where(is_one, one, jnp.where(is_three, three, 0.0))
         w2_part = total.reshape(2 * chips, rows_own, channels)
-        tile_part = tile_part.reshape(2 * chips, rows_own, LANES)
+        tile_part = jnp.where(first_rows, one, three)
         if first:
             w_s[:, :, 0:channels] = w2_part
-            w_s[:, :, channels:] = tile_part
+            tile_s[...] = tile_part
         else:
             w_s[:, :, 0:channels] = w_s[:, :, 0:channels] + w2_part
-            w_s[:, :, channels:] = w_s[:, :, channels:] + tile_part
-
-    def slot_of(ref, slot):
-        return join(ref.at[slot], 0, own // LANES)
-
-    acc1_s[...] = jnp.zeros(acc1_s.shape, F32)
-    acc2_s[...] = jnp.zeros(acc2_s.shape, F32)
+            tile_s[...] = tile_s[...] + tile_part
+
+    def slot_of(kind, slot):
+        return join(tan_s[slot][kind], own_before[slot], own // LANES)
+
     series_stage(1)
     series_stage(2)
     series_stage(3)
     add_weight_grads(
-        ((slot_of(tan1_s, 1), slot_of(g2_s, 2)), (slot_of(tan1_s, 2), slot_of(g2_s, 1))),
+        ((slot_of(0, 1), slot_of(3, 2)), (slot_of(0, 2), slot_of(3, 1))),
         (
-            (slot_of(g1_s, 2), slot_of(tan2_s, 2), 2),
-            (slot_of(g1_s, 1), slot_of(tan2_s, 1), 3),
+            (slot_of(2, 2), slot_of(1, 2), 2),
+            (slot_of(2, 1), slot_of(1, 1), 3),
         ),
         True,
     )
     series_stage(4)
     add_weight_grads(
-        ((slot_of(tan1_s, 0), slot_of(g2_s, 2)), (slot_of(tan1_s, 2), slot_of(g2_s, 0))),
+        ((slot_of(0, 0), slot_of(3, 2)), (slot_of(0, 2), slot_of(3, 0))),
         (
-            (slot_of(g1_s, 2), slot_of(tan2_s, 2), 1),
-            (slot_of(g1_s, 0), slot_of(tan2_s, 0), 4),
+            (slot_of(2, 2), slot_of(1, 2), 1),
+            (slot_of(2, 0), slot_of(1, 0), 4),
         ),
         False,
     )
@@ -396,18 +469,21 @@
         lanes = pl.ds(start, size)
         count = size // LANES
         ring_from = at // LANES
-        own_places = halves(start, size, HALO, own)
-        gs2 = dot_nn(w13_s[channels:], join(taps_s.at[0], start // LANES, count))
-        ga2 = join(cv2_s, ring_from, count).astype(F32) * join(acc2_s, ring_from, count) + sl2_s[:, lanes] * gs2
+        own_places = run_of(g1c_s, start, size, HALO, own_before[2])
+        gs2 = dot_nn(w13_s[channels:, 0 : TAP_ROWS + 8], join(taps_s.at[0], start // LANES, count))
+        acc2 = join(cv2_s, ring_from, count).astype(F32) * join(lin2b_s, ring_from + kept_before, count).astype(F32)
+        ga2 = (acc2 + acc2) + sl2_s[:, lanes] * gs2
         low2 = ga2.astype(BF16)
         gs1 = dot_nn(w2t_s[...], low2)
-        ga1 = join(cv1_s, ring_from, count).astype(F32) * join(acc1_s, ring_from, count) + sl1_s[:, lanes] * gs1
+        acc1 = join(cv1_s, ring_from, count).astype(F32) * join(lin1b_s, ring_from + kept_before, count).astype(F32)
+        ga1 = (acc1 + acc1) + sl1_s[:, lanes] * gs1
         low1 = ga1.astype(BF16)
         q_s[:, lanes] = q0_s[:, lanes] + dot_nn(wout_s[:, channels:], low1)[0:TAP_ROWS]
-        put(g2_s.at[0], own_places, low2)
-        put(g1_s.at[0], own_places, low1)
+        put(g2c_s, own_places, low2)
+        put(g1c_s, own_places, low1)
         for c in range(count):
-            here = jnp.where(own_places[c] < own // LANES, 1.0, 0.0)
+            chunk = (start - HALO) // LANES + c
+            here = jnp.where((chunk >= 0) & (chunk < own // LANES), 1.0, 0.0)
             bias_one = bias_one + here * ga1[:, c * LANES : (c + 1) * LANES]
             bias_two = bias_two + here * ga2[:, c * LANES : (c + 1) * LANES]
         return bias_one, bias_two
@@ -415,7 +491,7 @@
     zero = jnp.zeros((channels, LANES), F32)
     bias_one, bias_two = over_blocks(own_blocks + 1, final_body, (zero, zero))
     add_weight_grads(
-        ((join(hid1_s, 0, own // LANES), slot_of(g2_s, 0)),), ((slot_of(g1_s, 0), join(hid2_s, 0, own // LANES), 0),), False
+        ((join(hid1_s, own_before[0], own // LANES), slot_of(3, 2)),), ((slot_of(2, 2), join(hid2_s, own_before[0], own // LANES), 0),), False
     )
 
     inside = pl.ds(HALO - LANES, own + BLOCK)
@@ -436,8 +512,19 @@
     density = density * probes_own
     density = density[0:1] + density[1:2] + density[2:3]
     row8 = iota((8, 1), 0)
-    out = jnp.where(row8 < 3, h_own + result + bias8, jnp.where(row8 == 3, density, grad_in))
-    og_ref[...] = jnp.where(row8 < 7, out, 0.0)
+    high = density.astype(BF16).astype(F32)
+    out = jnp.where(row8 < 3, h_own + result + bias8, jnp.where(row8 == 3, high, grad_in))
+    out = jnp.where(row8 == 7, density - high, out)
+    if own < channels:
+        out = jnp.concatenate([out, jnp.zeros((8, channels - own), F32)], axis=1)
+    lines = [out[:, c * channels : (c + 1) * channels] for c in range(out.shape[1] // channels)]
+    if len(lines) == 1:
+        lines.append(jnp.zeros((8, channels), F32))
+    out = jnp.concatenate(lines, axis=0).astype(BF16)
+    og_ref[...] = jnp.zeros(og_ref.shape, BF16)
+    og_ref[:, 0:channels] = out
+    send_ref[chips * rows_own :, 0:channels] = out
+    send_ref[chips * rows_own :, channels:] = jnp.zeros((out.shape[0], LANES), BF16)
 
     sums = (
         all_sum(grad_in, axis=1),
@@ -451,81 +538,98 @@
     bias_one = all_sum(bias_one, axis=1)
     bias_two = all_sum(bias_two, axis=1)
     extras = jnp.where(lane == TAP_ROWS, bias_one, jnp.where(lane == TAP_ROWS + 1, bias_two, small_row))
-    extras = extras.reshape(2 * chips, rows_own, LANES)
-    w_s[:, :, channels:] = w_s[:, :, channels:] + extras
+    blank = jnp.zeros((LANES - TAP_ROWS - 8, channels), F32)
+    flat = jnp.concatenate([tile_s[...], blank], axis=0).T
+    extras = jnp.where(lane < TAP_ROWS, flat, extras)
+    w_s[:, :, channels:] = extras.reshape(2 * chips, rows_own, LANES)
 
     core = jnp.bitwise_and(me, 1)
     chip = jnp.right_shift(me, 1)
     for m in range(chips):
         block = 2 * jnp.bitwise_xor(chip, m)
         keep_ref[m] = w_s[block + core]
-        send_ref[m] = w_s[block + 1 - core]
-
-
-def call_main(me, u3, x0, x1, u2, planes, small, own, channels, chips):
+        send_ref[m * rows_own : (m + 1) * rows_own] = w_s[block + 1 - core].astype(BF16)
+
+
+def output_rows(own, channels):
+    return max(8 * (own // channels), 16)
+
+
+def call_main(me, u3, u2, planes, small, packs, own, channels, chips):
     rows_own = channels // (2 * chips)
     region = own + 2 * HALO
     wide = (own + BLOCK) // LANES + 1
-    slot = own // LANES + 1
     width = channels + LANES
     out_shape = (
         jax.ShapeDtypeStruct((chips, rows_own, width), F32),
-        jax.ShapeDtypeStruct((chips, rows_own, width), F32),
-        jax.ShapeDtypeStruct((2 * chips, rows_own, LANES), F32),
+        jax.ShapeDtypeStruct((chips * rows_own + output_rows(own, channels), width), BF16),
+        jax.ShapeDtypeStruct((output_rows(own, channels), width), BF16),
+        jax.ShapeDtypeStruct((rows_own, LANES), F32),
         jax.ShapeDtypeStruct((8, channels), F32),
-        jax.ShapeDtypeStruct((8, own), F32),
     )
     vmem = pltpu.VMEM
+    plan = buffer_plan(own)
+
+    def buffer(name, lanes):
+        return vmem((lanes // LANES + sum(plan[name]), channels, LANES), BF16)
+
     scratch = [
         vmem((2 * chips, rows_own, width), F32),
         vmem((2 * channels, LANES), BF16),
         vmem((channels, channels), BF16),
         vmem((channels, channels), BF16),
         vmem((TAP_ROWS + 8, 2 * channels), BF16),
-        vmem((2, channels, LANES), F32),
-        vmem((NMAX + 1, region // LANES, LANES, LANES), BF16),
+        vmem((channels, LANES), F32),
+        vmem((NMAX + 1, region // LANES, TAP_ROWS + 8, LANES), BF16),
         vmem((channels, region), F32),
         vmem((channels, region), F32),
-        vmem((wide, channels, LANES), BF16),
-        vmem((wide, channels, LANES), BF16),
-        vmem((2, wide, channels, LANES), BF16),
-        vmem((2, wide, channels, LANES), BF16),
-        vmem((2, wide, channels, LANES), BF16),
-        vmem((2, wide, channels, LANES), BF16),
-        vmem((wide, channels, LANES), F32),
-        vmem((wide, channels, LANES), F32),
-        vmem((3, slot, channels, LANES), BF16),
-        vmem((3, slot, channels, LANES), BF16),
-        vmem((3, slot, channels, LANES), BF16),
-        vmem((3, slot, channels, LANES), BF16),
-        vmem((slot, channels, LANES), BF16),
-        vmem((slot, channels, LANES), BF16),
+        *[vmem((wide, channels, LANES), BF16)] * 6,
+        *[buffer("kept", own + BLOCK)] * 8,
+        *[buffer("early", own)] * 4,
+        *[buffer("second", own)] * 4,
+        *[buffer("late", own)] * 4,
+        *[buffer("early", own)] * 2,
         vmem((TAP_ROWS, region), F32),
         vmem((TAP_ROWS, region), F32),
         vmem((NMAX, 8, own), F32),
+        vmem((TAP_ROWS + 8, channels), F32),
+        vmem((2 * chips, rows_own, LANES), F32),
     ]
     full = pl.BlockSpec(memory_space=pltpu.VMEM)
     return pl.pallas_call(
         functools.partial(main_kernel, own=own, channels=channels, chips=chips),
         out_shape=out_shape,
-        in_specs=[pl.BlockSpec(memory_space=pltpu.SMEM)] * 2 + [full] * 5,
+        in_specs=[pl.BlockSpec(memory_space=pltpu.SMEM)] * 2 + [full] * (3 + 2 * chips),
         out_specs=[full] * 5,
         scratch_shapes=scratch,
         compiler_params=pltpu.CompilerParams(vmem_limit_bytes=63 * 1024 * 1024),
         name="flow_block",
-    )(me, u3, x0, x1, u2, planes, small)
-
-
-def assemble_kernel(index_ref, kinds_ref, p0_ref, p1_ref, small_ref, z_ref, gin_ref, logdet_ref, dens_s, *, own, chips, frames):
+    )(me, u3, u2, planes, small, *packs)
+
+
+def assemble_kernel(index_ref, kinds_ref, small_ref, *refs, own, channels, chips, frames):
+    pieces = refs[: chips + 1]
+    z_ref, gin_ref, logdet_ref, dens_s = refs[chips + 1 :]
     me = index_ref[0]
+    lines = max(own // channels, 1)
+    size = min(own, channels)
+    rows = output_rows(own, channels)
     for m in range(chips):
-        for b, ref in ((0, p0_ref), (1, p1_ref)):
+        for b in range(2):
             shard = jnp.bitwise_xor(me, 2 * m + b)
-            lanes = pl.ds(pl.multiple_of(shard * own, LANES), own)
-            piece = ref[m]
-            z_ref[:, lanes] = piece[0:3]
-            gin_ref[:, lanes] = piece[4:7]
-            dens_s[:, lanes] = piece[3:4]
+            if m == 0:
+                block = pieces[b][...]
+            else:
+                message = pieces[m + 1]
+                first = message.shape[0] - (2 - b) * rows
+                block = message[first : first + rows]
+            block = block.astype(F32)
+            for c in range(lines):
+                lanes = pl.ds(pl.multiple_of(shard * own + c * size, LANES), size)
+                piece = block[8 * c : 8 * c + 8, 0:size]
+                z_ref[:, lanes] = piece[0:3]
+                gin_ref[:, lanes] = piece[4:7]
+                dens_s[:, lanes] = piece[3:4] + piece[7:8]
     scale_sum = small_ref[1, 0] + small_ref[1, 1] + small_ref[1, 2]
     pixel = iota((1, FRAME), 1)
     bottom = (pixel // (WIDTH * 32)) % 2
@@ -605,12 +709,41 @@
     return (param - LR_RATE * update, new_moment, new_second)
 
 
+def arrange_kernel(
+    grad_ref, cols_ref, rows_ref,
+    g1_out, o1_out, o2_out, g3_out, o3_out, bias_out, u1_out, v1_out, u2_out, v2_out, u3_out, v3_out, *, channels,
+):
+    lane = iota((1, LANES), 1)
+    cols = cols_ref[...]
+    tile = grad_ref[:, channels:]
+    is_one = lane_is_one(lane)
+    is_three = lane_is_three(lane)
+    spread = jnp.where((lane % 8 == 4) & (lane < TAP_ROWS), cols, 0.0)
+    spread = spread + pltpu.roll(spread, 1, 1) + pltpu.roll(spread, 2, 1)
+    outer_one = jnp.where(is_one, cols[:, 0:1] * rows_ref[1:2, 0:LANES], 0.0)
+    outer_three = jnp.where(is_three, spread * rows_ref[2:3, 0:LANES], 0.0)
+    o2_out[...] = cols[:, 1:2] * rows_ref[0:1, :]
+    g1_out[...] = dot_nt(spread_one(), jnp.where(is_one, tile, 0.0), HIGH)
+    o1_out[...] = dot_nt(spread_one(), outer_one, HIGH)
+    g3_out[...] = dot_nt(spread_three(), jnp.where(is_three, tile, 0.0), HIGH)
+    o3_out[...] = dot_nt(spread_three(), outer_three, HIGH)
+    bias_out[...] = tile.T[TAP_ROWS : TAP_ROWS + 2, :]
+    flipped = cols.T
+    u1_out[...] = flipped[0:1]
+    v2_out[...] = flipped[1:2]
+    tap = iota((9, LANES), 0)
+    select = (iota((9, LANES), 1) == (8 - tap) * 8 + 4).astype(F32)
+    v3_out[...] = dot_nn(select, flipped, HIGH)
+    v1_out[...] = dot_nt(rows_ref[1:2, 0:LANES], spread_one(), HIGH)
+    u2_out[...] = rows_ref[0:1, :]
+    u3_out[...] = rows_ref[2:3, 4:7]
+
+
 def update_kernel(
-    totals_ref, grad_ref, cols_ref, rows_ref,
+    totals_ref, rows_ref, grad_ref, g1_ref, o1_ref, o2_ref, g3_ref, o3_ref, bias_ref,
     w1_ref, m1_ref, s1_ref, w2_ref, m2_ref, s2_ref, w3_ref, m3_ref, s3_ref,
     mb_ref, sb_ref, small_ref, msmall_ref, ssmall_ref,
-    norm_out, nw1, nm1, ns1, nw2, nm2, ns2, nw3, nm3, ns3, cb, nmb, nsb, nsm, nmsm, nssm, lw1, lw2, lw3,
-    u1_out, v1_out, u2_out, v2_out, u3_out, v3_out, *, channels,
+    norm_out, nw1, nm1, ns1, nw2, nm2, ns2, nw3, nm3, ns3, cb, nmb, nsb, nsm, nmsm, nssm, lw1, lw2, lw3, *, channels,
 ):
     lane = iota((1, LANES), 1)
     lines = [totals_ref[m : m + 1] for m in range(totals_ref.shape[0])]
@@ -619,14 +752,13 @@
     row = lines[0]
 
     def pick(index):
-        return jnp.sum(jnp.where(lane == index, row, 0.0), axis=1, keepdims=True)
-
-    sigmas = rows_ref[3:4, 0:LANES]
+        return row[:, index : index + 1]
+
     small_row = jnp.where((lane >= TAP_ROWS + 2) & (lane < TAP_ROWS + 11), row, 0.0)
     square = pick(12) + jnp.sum(small_row * small_row, axis=1, keepdims=True)
     scales = []
     for j in range(3):
-        sigma = sigmas[:, j : j + 1]
+        sigma = rows_ref[3:4, j : j + 1]
         ratio = SHRINK / sigma
         factor = pick(3 + j) / sigma
         fixed = pick(j) - 2.0 * factor * pick(6 + j) + factor * factor * pick(9 + j)
@@ -636,35 +768,20 @@
     norm_out[...] = norm
     clip = jnp.minimum(1.0, CLIP_LIMIT / (norm + 1e-06))
 
-    cols = cols_ref[...]
-    grad = grad_ref[...]
-    tile = grad[:, channels:]
-    is_one = lane_is_one(lane)
-    is_three = lane_is_three(lane)
-    spread = jnp.where((lane % 8 == 4) & (lane < TAP_ROWS), cols, 0.0)
-    spread = spread + pltpu.roll(spread, 1, 1) + pltpu.roll(spread, 2, 1)
-    outer_one = cols[:, 0:1] * rows_ref[1:2, 0:LANES]
-    outer_three = spread * rows_ref[2:3, 0:LANES]
-    outer_two = cols[:, 1:2] * rows_ref[0:1, :]
-    fixed_one = jnp.where(is_one, scales[0][0] * (tile - scales[0][1] * outer_one) * clip, 0.0)
-    fixed_two = scales[1][0] * (grad[:, 0:channels] - scales[1][1] * outer_two) * clip
-    fixed_three = jnp.where(is_three, scales[2][0] * (tile - scales[2][1] * outer_three) * clip, 0.0)
-    grad_one = dot_nt(spread_one(), fixed_one, HIGH)
-    grad_two = fixed_two
-    grad_three = dot_nt(spread_three(), fixed_three, HIGH)
-
-    for grad_j, w_ref, m_ref, s_ref, nw, nm, ns, lw in (
-        (grad_one, w1_ref, m1_ref, s1_ref, nw1, nm1, ns1, lw1),
-        (grad_two, w2_ref, m2_ref, s2_ref, nw2, nm2, ns2, lw2),
-        (grad_three, w3_ref, m3_ref, s3_ref, nw3, nm3, ns3, lw3),
+    for index, grad, outer, w_ref, m_ref, s_ref, nw, nm, ns, lw in (
+        (0, g1_ref[...], o1_ref, w1_ref, m1_ref, s1_ref, nw1, nm1, ns1, lw1),
+        (1, grad_ref[:, 0:channels], o2_ref, w2_ref, m2_ref, s2_ref, nw2, nm2, ns2, lw2),
+        (2, g3_ref[...], o3_ref, w3_ref, m3_ref, s3_ref, nw3, nm3, ns3, lw3),
     ):
-        new, moment, second = adam_step(w_ref[...], grad_j, m_ref[...], s_ref[...])
+        ratio, factor = scales[index]
+        fixed = (clip * ratio) * (grad - factor * outer[...])
+        new, moment, second = adam_step(w_ref[...], fixed, m_ref[...], s_ref[...])
         nw[...] = new
         nm[...] = moment
         ns[...] = second
         lw[...] = new.astype(BF16)
 
-    bias = (tile * clip).T[TAP_ROWS : TAP_ROWS + 2, :]
+    bias = bias_ref[...] * clip
     cb[...] = bias
     moment, second = moment_step(bias, mb_ref[...], sb_ref[...])
     nmb[...] = moment
@@ -684,16 +801,6 @@
     nsm[...] = new
     nmsm[...] = moment
     nssm[...] = second
-
-    flipped = cols.T
-    u1_out[...] = flipped[0:1]
-    v2_out[...] = flipped[1:2]
-    tap = iota((9, LANES), 0)
-    select = (iota((9, LANES), 1) == (8 - tap) * 8 + 4).astype(F32)
-    v3_out[...] = dot_nn(select, flipped, HIGH)
-    v1_out[...] = dot_nt(rows_ref[1:2, 0:LANES], spread_one(), HIGH)
-    u2_out[...] = rows_ref[0:1, :]
-    u3_out[...] = rows_ref[2:3, 4:7]
 
 
 def prepare_kernel(
@@ -781,11 +888,6 @@
     def swap(values, axis, size, bits):
         return lax.ppermute(values, axis, [(j, j ^ bits) for j in range(size)])
 
-    def gather_shards(values):
-        pieces = [values] + [swap(values, "chan", shards, 2 * m) for m in range(1, chips)]
-        first = jnp.stack(pieces)
-        return first, swap(first, "chan", shards, 1)
-
     pack = pl.pallas_call(
         pack_kernel,
         out_shape=jax.ShapeDtypeStruct((rows_own, width), F32),
@@ -793,8 +895,7 @@
         out_specs=full,
         name="pack_weights",
     )(weight1.T, weight2.T, weight3, biases, power_u1.reshape(1, rows_own))
-    x0, x1 = gather_shards(pack)
-
+    near = [pack] + [swap(pack, "chan", shards, 2 * m) for m in range(1, chips)]
     planes, small = pl.pallas_call(
         functools.partial(prepare_kernel, own=own, frames=frames),
         out_shape=(
@@ -806,38 +907,47 @@
         name="prepare_planes",
     )(index, frame_kinds, series_len, cot_logdet, small_params, images, probes, cot_z)
 
-    keep, send, cols, rows, og = call_main(
-        index, power_u3, x0, x1, power_u2.reshape(1, channels), planes, small, own, channels, chips
+    near[-1], planes = lax.optimization_barrier((near[-1], planes))
+    packs = []
+    for values in near:
+        packs += [values, swap(values, "chan", shards, 1)]
+
+    keep, send, og, cols_own, rows = call_main(
+        index, power_u3, power_u2.reshape(1, channels), planes, small, packs, own, channels, chips
     )
 
     got = swap(send, "chan", shards, 1)
-    summed = keep + got
-    low = summed.astype(BF16)
+    og_other = got[chips * rows_own :]
+    summed = keep + got[: chips * rows_own].reshape(keep.shape).astype(F32)
     total = summed[0]
+    pieces = [og, og_other]
     for m in range(1, chips):
-        total = total + swap(low[m], "chan", shards, 2 * m).astype(F32)
-    og, half = lax.optimization_barrier((og, total.astype(BF16)))
+        message = jnp.concatenate([summed[m].astype(BF16), og, og_other], axis=0)
+        message = swap(message, "chan", shards, 2 * m)
+        total = total + message[:rows_own].astype(F32)
+        pieces.append(message)
+    half = total.astype(BF16)
+    assembled = pl.pallas_call(
+        functools.partial(assemble_kernel, own=own, channels=channels, chips=chips, frames=frames),
+        out_shape=(
+            jax.ShapeDtypeStruct((3, pixels), F32),
+            jax.ShapeDtypeStruct((3, pixels), F32),
+            jax.ShapeDtypeStruct((frames, 4), F32),
+        ),
+        in_specs=[smem] * 3 + [full] * (chips + 1),
+        out_specs=[full] * 3,
+        scratch_shapes=[pltpu.VMEM((1, pixels), F32)],
+        name="assemble_outputs",
+    )(index, frame_kinds, small_params, *pieces)
     bits = 1
     while 2 * bits < replicas:
         half = (half.astype(F32) + swap(half, "dp", replicas, bits).astype(F32)).astype(BF16)
         bits *= 2
     other = swap(half, "dp", replicas, bits) if replicas > 1 else jnp.zeros_like(half)
-
-    p0, p1 = gather_shards(og)
-    z_out, grad_input, logdet = pl.pallas_call(
-        functools.partial(assemble_kernel, own=own, chips=chips, frames=frames),
-        out_shape=(
-            jax.ShapeDtypeStruct((3, pixels), F32),
-            jax.ShapeDtypeStruct((3, pixels), F32),
-            jax.ShapeDtypeStruct((frames, 4), F32),
-        ),
-        in_specs=[smem, smem, full, full, smem],
-        out_specs=[full] * 3,
-        scratch_shapes=[pltpu.VMEM((1, pixels), F32)],
-        name="assemble_outputs",
-    )(index, frame_kinds, p0, p1, small_params)
-
-    cols_own = lax.dynamic_index_in_dim(cols, me, 0, False)
+    other, assembled = lax.optimization_barrier((other, assembled))
+    z_out, grad_input, logdet = assembled
+
+
     grad, parts = pl.pallas_call(
         functools.partial(norm_kernel, channels=channels),
         out_shape=(
@@ -855,6 +965,23 @@
     def like(value, dtype=F32):
         return jax.ShapeDtypeStruct(value.shape, dtype)
 
+    arranged_shape = (
+        [like(weight1.T)] * 2
+        + [jax.ShapeDtypeStruct((rows_own, channels), F32)]
+        + [like(weight3)] * 2
+        + [like(biases)]
+        + [jax.ShapeDtypeStruct((1, rows_own), F32), jax.ShapeDtypeStruct((1, 27), F32)]
+        + [jax.ShapeDtypeStruct((1, channels), F32), jax.ShapeDtypeStruct((1, rows_own), F32)]
+        + [jax.ShapeDtypeStruct((1, 3), F32), jax.ShapeDtypeStruct((9, rows_own), F32)]
+    )
+    arranged = pl.pallas_call(
+        functools.partial(arrange_kernel, channels=channels),
+        out_shape=arranged_shape,
+        in_specs=[full] * 3,
+        out_specs=[full] * len(arranged_shape),
+        name="arrange_gradients",
+    )(grad, cols_own, rows)
+    vectors = arranged[6:]
     out_shape = (
         [jax.ShapeDtypeStruct((1, 1), F32)]
         + [like(weight1.T)] * 3
@@ -863,22 +990,19 @@
         + [like(biases)] * 3
         + [like(small_params)] * 3
         + [like(weight1.T, BF16), like(weight2.T, BF16), like(weight3, BF16)]
-        + [jax.ShapeDtypeStruct((1, rows_own), F32), jax.ShapeDtypeStruct((1, 27), F32)]
-        + [jax.ShapeDtypeStruct((1, channels), F32), jax.ShapeDtypeStruct((1, rows_own), F32)]
-        + [jax.ShapeDtypeStruct((1, 3), F32), jax.ShapeDtypeStruct((9, rows_own), F32)]
     )
     done = pl.pallas_call(
         functools.partial(update_kernel, channels=channels),
         out_shape=out_shape,
-        in_specs=[full] * 18,
+        in_specs=[full] * 23,
         out_specs=[full] * len(out_shape),
         name="adam_update",
     )(
-        totals, grad, cols_own, rows,
+        totals, rows, grad, *arranged[:6],
         weight1.T, moment_w1.T, second_w1.T, weight2.T, moment_w2.T, second_w2.T,
         weight3, moment_w3, second_w3, moment_bias, second_bias, small_params, moment_small, second_small,
     )
-    norm, updates, vectors = done[0], list(done[1:19]), done[19:]
+    norm, updates = done[0], list(done[1:])
     for slot in (0, 1, 2, 3, 4, 5, 15, 16):
         updates[slot] = updates[slot].T
     return (

time: 103 us -> 92.6 us (0.90)
  starting transfers between devices: 19.7 us -> 16.6 us
  other arithmetic: 3.5 us -> 1.48 us
  Pallas kernels: 52.7 us -> 51.1 us
  waiting for transfers between devices: 20.9 us -> 19.3 us
  local copies, waits for them, and re-layouts: 4.29 us -> 2.72 us
    pallas_call x1, Pallas kernels: 42.4 us -> 38.9 us  [call_main(): pl.pallas_call(functools.partial(main_kernel, own=own, channels=channels,...]
    ppermute x18 -> x17, starting transfers between devices: 19.7 us -> 16.6 us  [swap(): return lax.ppermute(values, axis, [(j, j ^ bits) for j in range(size)])]
    pallas_call x1 -> x2, Pallas kernels: 1.86 us -> 3.96 us  [the longest x1 1.98 us: local(): pl.pallas_call(functools.partial(assemble_kernel, own=own, channels=chann...]
    ppermute x18 -> x17, waiting for transfers between devices: 20.9 us -> 19.3 us  [swap(): return lax.ppermute(values, axis, [(j, j ^ bits) for j in range(size)])]
    squeeze x2 -> x0, local copies, waits for them, and re-layouts: 1.39 us -> none  [the longest x1 1.37 us: local(): cols_own = lax.dynamic_index_in_dim(cols, me, 0, False)]
    convert_element_type x2 -> x1, other arithmetic: 1.21 us -> 0.05 us  [local(): half = total.astype(BF16)]
    unnamed x14 -> x30, local copies, waits for them, and re-layouts: 2.9 us -> 2.65 us
  transfers between devices with their start and end apart: 18 -> 17, of which waited for: 11 -> 12; matrix products, arithmetic and copies ran while one was open for 2% -> 0% of each run, Pallas kernels for 6% -> 7%
where the time goes in v4:
time: 92.6 us; the launch traced here: 92.2 us
  Pallas kernels  51.1 us (55%)
  waiting for transfers between devices  19.3 us (21%)
  starting transfers between devices  16.6 us (18%)
  local copies, waits for them, and re-layouts  2.72 us (3%)
  other arithmetic  1.48 us (2%)
  between operations  1.04 us (1%)
    pallas_call x1, Pallas kernels, call_main(): pl.pallas_call(functools.partial(main_kernel, own=own, channels=channels,...  38.9 us
    ppermute x17, waiting for transfers between devices, swap(): return lax.ppermute(values, axis, [(j, j ^ bits) for j in range(size)])  19.3 us
    ppermute x17, starting transfers between devices, swap(): return lax.ppermute(values, axis, [(j, j ^ bits) for j in range(size)])  16.6 us
    unnamed x30, local copies, waits for them, and re-layouts  2.65 us
    pallas_call x1, Pallas kernels, local(): pl.pallas_call(functools.partial(update_kernel, channels=channels), out_s...  2.54 us
    pallas_call x1, Pallas kernels, local(): pl.pallas_call(functools.partial(prepare_kernel, own=own, frames=frames),...  2.07 us
    pallas_call x1, Pallas kernels, local(): pl.pallas_call(functools.partial(assemble_kernel, own=own, channels=chann...  1.98 us
    pallas_call x1, Pallas kernels, local(): pl.pallas_call(functools.partial(arrange_kernel, channels=channels), out_...  1.98 us
  transfers between devices with their start and end apart: 17, of which 12 were waited for; matrix products, arithmetic and copies ran while one was open for 0% of the time, Pallas kernels for 7%

profile of v4, /device:TPU:0, one launch (start us, length us, event | category | flops | bytes accessed | tf_op | source)
XLA Modules:
  0.0 92.2 jit_solution(9836414674826490159)
XLA Ops:
  0.7 1.8 %pack_weights.1.refs_0_.pack_ref = f32[64,640]{1,0:T(8,128)} custom-call(f32[27,64]{1,0:T(8,128)} %bitcast.46, f32[64,512]{1,0:T(8,128)} %bitcast.42, f32[27,64]{1,0:T(8,128)} %w3_ref.3, f32[2,64]{1,0:T(2,128)} %bias_ref.1, f32[1,64]{1,0:T(1,128)} %bitcast.51), custom_call_target="tpu_custom_call" | custom-call | tf_op jit(solution)/shard_map/pack_weights/pallas_call | solution.py:891
  2.5 3.9 %collective-permute-start = (f32[64,640]{1,0:T(8,128)}, f32[64,640]{1,0:T(8,128)S(1)}, u32[]{:S(2)}, u32[]{:S(2)}) collective-permute-start(f32[64,640]{1,0:T(8,128)} %pack_weights.1.refs_0_.pack_ref), channel_id=1, source_target_pairs={{0,6},{1,7},{2,4},{3,5},{4,2},{5,3},{6,0},{7,1},{8,14},{9,15},{10,... | collective-permute-start | bytes 491528 | tf_op jit(solution)/shard_map/ppermute | solution.py:889
  6.4 0.5 collective-permute-start.4
  6.9 0.1 collective-permute-start.2
  7.0 0.0 collective-permute-start.1
  7.0 2.1 %prepare_planes.1 = (f32[40,2048]{1,0:T(8,128)}, f32[8,128]{1,0:T(8,128)}) custom-call(s32[1]{0:T(128)} %bitcast.index_ref, s32[2]{0:T(128)} %kinds_ref.3, s32[2,4]{1,0:T(2,128)} %len_ref.1, f32[2,4]{1,0:T(2,128)} %cot_ref.1, f32[3,3]{1,0:T(4,128)} %small_ref.3, f32[3,8192]{1,0:T(4,128)} %images_ref.1, f32[3,8192]{1,0:T(4,128)} %probes_ref.1, ...), custom_call_target="tpu_custom_call" | custom-call | tf_op jit(solution)/shard_map/prepare_planes/pallas_call | solution.py:899
  9.0 2.6 %collective-permute-done.refs_6_ = f32[64,640]{1,0:T(8,128)S(1)} collective-permute-done((f32[64,640]{1,0:T(8,128)}, f32[64,640]{1,0:T(8,128)S(1)}, u32[]{:S(2)}, u32[]{:S(2)}) %collective-permute-start) | collective-permute-done | bytes 163872 | tf_op jit(solution)/shard_map/ppermute | solution.py:889
  11.6 2.7 %collective-permute-done.4.refs_4_ = f32[64,640]{1,0:T(8,128)S(1)} collective-permute-done((f32[64,640]{1,0:T(8,128)}, f32[64,640]{1,0:T(8,128)S(1)}, u32[]{:S(2)}, u32[]{:S(2)}) %collective-permute-start.4) | collective-permute-done | bytes 163872 | tf_op jit(solution)/shard_map/ppermute | solution.py:889
  14.3 0.0 collective-permute-start.5
  14.3 0.3 collective-permute-done.2.refs_2_
  14.6 0.2 collective-permute-start.3
  14.8 0.3 collective-permute-start.6
  15.1 0.0 collective-permute-done.1.refs_1_
  15.1 0.6 collective-permute-done.5.refs_5_
  15.7 0.3 collective-permute-done.3.refs_3_
  16.0 0.2 collective-permute-done.6.refs_7_
  16.2 0.7 copy-done.12
  16.9 38.9 %flow_block.1 = (f32[4,64,640]{2,1,0:T(8,128)}, bf16[272,640]{1,0:T(8,128)(2,1)}, bf16[16,640]{1,0:T(8,128)(2,1)}, f32[64,128]{1,0:T(8,128)}, f32[8,512]{1,0:T(8,128)}) custom-call(s32[1]{0:T(128)} %bitcast.index_ref, f32[3]{0:T(128)} %u3_ref.1, f32[1,512]{1,0:T(1,128)} %bitcast.50, f32[40,2048]{1,0:T(8,128)} %get-tuple-element.78.planes_ref, ...), custom_call_target="tpu_custom_call" | custom-call | tf_op jit(solution)/shard_map/flow_block/pallas_call | solution.py:599
  55.8 0.3 collective-permute-start.7
  56.2 1.6 %collective-permute-done.7 = bf16[272,640]{1,0:T(8,128)(2,1)S(1)} collective-permute-done((bf16[272,640]{1,0:T(8,128)(2,1)}, bf16[272,640]{1,0:T(8,128)(2,1)S(1)}, u32[]{:S(2)}, u32[]{:S(2)}) %collective-permute-start.7) | collective-permute-done | bytes 348192 | tf_op jit(solution)/shard_map/ppermute | solution.py:889
  57.8 0.1 fusion.4
  57.9 0.7 copy-done.13
  58.7 1.7 %collective-permute-start.8 = (bf16[96,640]{1,0:T(8,128)(2,1)S(1)}, bf16[96,640]{1,0:T(8,128)(2,1)S(1)}, u32[]{:S(2)}, u32[]{:S(2)}) collective-permute-start(bf16[96,640]{1,0:T(8,128)(2,1)S(1)} %get-tuple-element.131), channel_id=1, source_target_pairs={{0,2},{1,3},{2,0},{3,1},{4,6},{5,7},{6,4},{7,5},{8,10},{9,11},{10,... | collective-permute-start | bytes 368648 | tf_op jit(solution)/shard_map/ppermute | solution.py:889
  60.4 0.6 collective-permute-start.9
  61.1 1.2 %collective-permute-start.10 = (bf16[96,640]{1,0:T(8,128)(2,1)S(1)}, bf16[96,640]{1,0:T(8,128)(2,1)S(1)}, u32[]{:S(2)}, u32[]{:S(2)}) collective-permute-start(bf16[96,640]{1,0:T(8,128)(2,1)S(1)} %get-tuple-element.133), channel_id=1, source_target_pairs={{0,6},{1,7},{2,4},{3,5},{4,2},{5,3},{6,0},{7,1},{8,14},{9,15},{10,... | collective-permute-start | bytes 368648 | tf_op jit(solution)/shard_map/ppermute | solution.py:889
  62.2 2.0 %collective-permute-done.8.refs_2_ = bf16[96,640]{1,0:T(8,128)(2,1)S(1)} collective-permute-done((bf16[96,640]{1,0:T(8,128)(2,1)S(1)}, bf16[96,640]{1,0:T(8,128)(2,1)S(1)}, u32[]{:S(2)}, u32[]{:S(2)}) %collective-permute-start.8) | collective-permute-done | bytes 122912 | tf_op jit(solution)/shard_map/ppermute | solution.py:889
  64.3 4.0 %collective-permute-done.9.refs_3_ = bf16[96,640]{1,0:T(8,128)(2,1)S(1)} collective-permute-done((bf16[96,640]{1,0:T(8,128)(2,1)S(1)}, bf16[96,640]{1,0:T(8,128)(2,1)S(1)}, u32[]{:S(2)}, u32[]{:S(2)}) %collective-permute-start.9) | collective-permute-done | bytes 122912 | tf_op jit(solution)/shard_map/ppermute | solution.py:889
  68.3 0.0 collective-permute-done.10.refs_4_
  68.3 0.6 copy-done.2
  68.9 0.0 copy-done.3
  68.9 1.6 %collective-permute-start.11 = (bf16[64,640]{1,0:T(8,128)(2,1)S(1)}, bf16[64,640]{1,0:T(8,128)(2,1)S(1)}, u32[]{:S(2)}, u32[]{:S(2)}) collective-permute-start(bf16[64,640]{1,0:T(8,128)(2,1)S(1)} %fusion.3), channel_id=1, source_target_pairs={{0,8},{8,0},{16,24},{24,16},{1,9},{9,1},{17,25},{25,17},{2,10},{10... | collective-permute-start | bytes 245768 | tf_op jit(solution)/shard_map/ppermute | solution.py:889
  70.5 2.9 %collective-permute-done.11 = bf16[64,640]{1,0:T(8,128)(2,1)S(1)} collective-permute-done((bf16[64,640]{1,0:T(8,128)(2,1)S(1)}, bf16[64,640]{1,0:T(8,128)(2,1)S(1)}, u32[]{:S(2)}, u32[]{:S(2)}) %collective-permute-start.11) | collective-permute-done | bytes 81952 | tf_op jit(solution)/shard_map/ppermute | solution.py:889
  73.4 2.7 %collective-permute-start.12 = (bf16[64,640]{1,0:T(8,128)(2,1)S(1)}, bf16[64,640]{1,0:T(8,128)(2,1)S(1)}, u32[]{:S(2)}, u32[]{:S(2)}) collective-permute-start(bf16[64,640]{1,0:T(8,128)(2,1)S(1)} %add_convert_fusion.a_ref), channel_id=1, source_target_pairs={{0,16},{8,24},{16,0},{24,8},{1,17},{9,25},{17,1},{25,9},{2,18},{10... | collective-permute-start | bytes 245768 | tf_op jit(solution)/shard_map/ppermute | solution.py:889
  76.1 2.0 %assemble_outputs.1 = (f32[3,8192]{1,0:T(4,128)}, f32[3,8192]{1,0:T(4,128)}, f32[2,4]{1,0:T(2,128)}) custom-call(s32[1]{0:T(128)} %bitcast.index_ref, s32[2]{0:T(128)} %kinds_ref.3, f32[3,3]{1,0:T(4,128)} %small_ref.3, bf16[16,640]{1,0:T(8,128)(2,1)} %get-tuple-element.83.refs_0_, bf16[16,640]{1,0:T(8,128)(2,1)} %copy-done.5, bf16[96,640]{1,0:T(8,128)(2,1)} %copy-done.1, ...), custom_call_target="tpu_custom_call" | custom-call | tf_op jit(solution)/shard_map/assemble_outputs/pallas_call | solution.py:930
  78.1 0.8 collective-permute-done.12.b_ref
  78.8 0.6 copy-done.14
  79.5 1.8 %norm_parts.1 = (f32[64,640]{1,0:T(8,128)}, f32[8,128]{1,0:T(8,128)}) custom-call(s32[1]{0:T(128)} %bitcast.index_ref, bf16[64,640]{1,0:T(8,128)(2,1)} %copy-done.4, bf16[64,640]{1,0:T(8,128)(2,1)} %copy-done.14, f32[64,640]{1,0:T(8,128)} %pack_weights.1.refs_0_.pack_ref, f32[64,128]{1,0:T(8,128)} %get-tuple-element.91.cols_ref, ...), custom_call_target="tpu_custom_call" | custom-call | tf_op jit(solution)/shard_map/norm_parts/pallas_call | solution.py:951
  81.3 0.0 collective-permute-start.13
  81.3 1.4 %collective-permute-done.13 = f32[8,128]{1,0:T(8,128)S(1)} collective-permute-done((f32[8,128]{1,0:T(8,128)}, f32[8,128]{1,0:T(8,128)S(1)}, u32[]{:S(2)}, u32[]{:S(2)}) %collective-permute-start.13) | collective-permute-done | bytes 4128 | tf_op jit(solution)/shard_map/ppermute | solution.py:889
  82.7 0.7 add.23
  83.4 1.5 %collective-permute-start.16 = (f32[8,128]{1,0:T(8,128)S(1)}, f32[8,128]{1,0:T(8,128)S(1)}, u32[]{:S(2)}, u32[]{:S(2)}) collective-permute-start(f32[8,128]{1,0:T(8,128)S(1)} %add.23), channel_id=1, source_target_pairs={{0,6},{1,7},{2,4},{3,5},{4,2},{5,3},{6,0},{7,1},{8,14},{9,15},{10,... | collective-permute-start | bytes 12296 | tf_op jit(solution)/shard_map/ppermute | solution.py:889
  84.8 0.3 collective-permute-start.15
  85.2 1.7 %collective-permute-start.14 = (f32[8,128]{1,0:T(8,128)S(1)}, f32[8,128]{1,0:T(8,128)S(1)}, u32[]{:S(2)}, u32[]{:S(2)}) collective-permute-start(f32[8,128]{1,0:T(8,128)S(1)} %add.23), channel_id=1, source_target_pairs={{0,2},{1,3},{2,0},{3,1},{4,6},{5,7},{6,4},{7,5},{8,10},{9,11},{10,... | collective-permute-start | bytes 12296 | tf_op jit(solution)/shard_map/ppermute | solution.py:889
  86.8 2.0 %arrange_gradients.1 = (f32[27,64]{1,0:T(8,128)}, f32[27,64]{1,0:T(8,128)}, f32[64,512]{1,0:T(8,128)}, f32[27,64]{1,0:T(8,128)}, f32[27,64]{1,0:T(8,128)}, /*ind...) custom-call(f32[64,640]{1,0:T(8,128)} %get-tuple-element.94.grad_ref, ...), custom_call_target="tpu_custom_call" | custom-call | tf_op jit(solution)/shard_map/arrange_gradients/pallas_call | solution.py:977
  88.9 0.0 collective-permute-done.15
  88.9 0.0 collective-permute-done.14
  88.9 0.6 pad_maximum_fusion.6.totals_ref
  89.5 2.5 %adam_update.1 = (f32[1,1]{1,0:T(1,128)}, f32[27,64]{1,0:T(8,128)}, f32[27,64]{1,0:T(8,128)}, f32[27,64]{1,0:T(8,128)}, f32[64,512]{1,0:T(8,128)}, /*index=5*/f3...) custom-call(f32[4,128]{1,0:T(4,128)} %pad_maximum_fusion.6.totals_re, ...), custom_call_target="tpu_custom_call" | custom-call | tf_op jit(solution)/shard_map/adam_update/pallas_call | solution.py:994
  (36 shorter events, 0.2 us)
Async XLA Ops:
  2.5 9.1 %collective-permute-start = (f32[64,640]{1,0:T(8,128)}, f32[64,640]{1,0:T(8,128)S(1)}, u32[]{:S(2)}, u32[]{:S(2)}) collective-permute-start(f32[64,640]{1,0:T(8,128)} %pack_weights.1.refs_0_.pack_ref), channel_id=1, source_target_pairs={{0,6},{1,7},{2,4},{3,5},{4,2},{5,3},{6,0},{7,1},{8,14},{9,15},{10,... | collective-permute-start | bytes 491528 | tf_op jit(solution)/shard_map/ppermute | solution.py:889
  6.4 7.9 %collective-permute-start.4 = (f32[64,640]{1,0:T(8,128)}, f32[64,640]{1,0:T(8,128)S(1)}, u32[]{:S(2)}, u32[]{:S(2)}) collective-permute-start(f32[64,640]{1,0:T(8,128)} %pack_weights.1.refs_0_.pack_ref), channel_id=1, source_target_pairs={{0,4},{1,5},{2,6},{3,7},{4,0},{5,1},{6,2},{7,3},{8,12},{9,13},{10,... | collective-permute-start | bytes 491528 | tf_op jit(solution)/shard_map/ppermute | solution.py:889
  6.9 7.7 %collective-permute-start.2 = (f32[64,640]{1,0:T(8,128)}, f32[64,640]{1,0:T(8,128)S(1)}, u32[]{:S(2)}, u32[]{:S(2)}) collective-permute-start(f32[64,640]{1,0:T(8,128)} %pack_weights.1.refs_0_.pack_ref), channel_id=1, source_target_pairs={{0,2},{1,3},{2,0},{3,1},{4,6},{5,7},{6,4},{7,5},{8,10},{9,11},{10,... | collective-permute-start | bytes 491528 | tf_op jit(solution)/shard_map/ppermute | solution.py:889
  7.0 8.2 %collective-permute-start.1 = (f32[64,640]{1,0:T(8,128)}, f32[64,640]{1,0:T(8,128)S(1)}, u32[]{:S(2)}, u32[]{:S(2)}) collective-permute-start(f32[64,640]{1,0:T(8,128)} %pack_weights.1.refs_0_.pack_ref), channel_id=1, source_target_pairs={{0,1},{1,0},{2,3},{3,2},{4,5},{5,4},{6,7},{7,6},{8,9},{9,8},{10,11... | collective-permute-start | bytes 491528 | tf_op jit(solution)/shard_map/ppermute | solution.py:889
  11.6 5.3 %copy-start.6 = (f32[64,640]{1,0:T(8,128)}, f32[64,640]{1,0:T(8,128)S(1)}, u32[]{:S(2)}) copy-start(f32[64,640]{1,0:T(8,128)S(1)} %collective-permute-done.refs_6_) | copy-start | bytes 491524
  14.3 2.6 %copy-start.7 = (f32[64,640]{1,0:T(8,128)}, f32[64,640]{1,0:T(8,128)S(1)}, u32[]{:S(2)}) copy-start(f32[64,640]{1,0:T(8,128)S(1)} %collective-permute-done.4.refs_4_) | copy-start | bytes 491524
  14.3 1.4 %collective-permute-start.5 = (f32[64,640]{1,0:T(8,128)S(1)}, f32[64,640]{1,0:T(8,128)S(1)}, u32[]{:S(2)}, u32[]{:S(2)}) collective-permute-start(f32[64,640]{1,0:T(8,128)S(1)} %collective-permute-done.4.refs_4_), channel_id=1, source_target_pairs={{0,1},{1,0},{2,3},{3,2},{4,5},{5,4},{6,7},{7,6},{8,9},{9,8},{10,11... | collective-permute-start | bytes 491528 | tf_op jit(solution)/shard_map/ppermute | solution.py:889
  14.6 2.3 %copy-start.8 = (f32[64,640]{1,0:T(8,128)}, f32[64,640]{1,0:T(8,128)S(1)}, u32[]{:S(2)}) copy-start(f32[64,640]{1,0:T(8,128)S(1)} %collective-permute-done.2.refs_2_) | copy-start | bytes 491524
  14.6 1.4 %collective-permute-start.3 = (f32[64,640]{1,0:T(8,128)S(1)}, f32[64,640]{1,0:T(8,128)S(1)}, u32[]{:S(2)}, u32[]{:S(2)}) collective-permute-start(f32[64,640]{1,0:T(8,128)S(1)} %collective-permute-done.2.refs_2_), channel_id=1, source_target_pairs={{0,1},{1,0},{2,3},{3,2},{4,5},{5,4},{6,7},{7,6},{8,9},{9,8},{10,11... | collective-permute-start | bytes 491528 | tf_op jit(solution)/shard_map/ppermute | solution.py:889
  14.8 1.4 %collective-permute-start.6 = (f32[64,640]{1,0:T(8,128)S(1)}, f32[64,640]{1,0:T(8,128)S(1)}, u32[]{:S(2)}, u32[]{:S(2)}) collective-permute-start(f32[64,640]{1,0:T(8,128)S(1)} %collective-permute-done.refs_6_), channel_id=1, source_target_pairs={{0,1},{1,0},{2,3},{3,2},{4,5},{5,4},{6,7},{7,6},{8,9},{9,8},{10,11... | collective-permute-start | bytes 491528 | tf_op jit(solution)/shard_map/ppermute | solution.py:889
  15.1 1.8 %copy-start.9 = (f32[64,640]{1,0:T(8,128)}, f32[64,640]{1,0:T(8,128)S(1)}, u32[]{:S(2)}) copy-start(f32[64,640]{1,0:T(8,128)S(1)} %collective-permute-done.1.refs_1_) | copy-start | bytes 491524
  15.7 1.2 %copy-start.10 = (f32[64,640]{1,0:T(8,128)}, f32[64,640]{1,0:T(8,128)S(1)}, u32[]{:S(2)}) copy-start(f32[64,640]{1,0:T(8,128)S(1)} %collective-permute-done.5.refs_5_) | copy-start | bytes 491524
  16.0 0.9 copy-start.11
  16.2 0.7 copy-start.12
  55.8 2.0 %copy-start = (f32[4,64,640]{2,1,0:T(8,128)S(1)}, f32[4,64,640]{2,1,0:T(8,128)}, u32[]{:S(2)}) copy-start(f32[4,64,640]{2,1,0:T(8,128)} %get-tuple-element.81) | copy-start | bytes 1966084
  55.8 1.9 %collective-permute-start.7 = (bf16[272,640]{1,0:T(8,128)(2,1)}, bf16[272,640]{1,0:T(8,128)(2,1)S(1)}, u32[]{:S(2)}, u32[]{:S(2)}) collective-permute-start(bf16[272,640]{1,0:T(8,128)(2,1)} %get-tuple-element.82), channel_id=1, source_target_pairs={{0,1},{1,0},{2,3},{3,2},{4,5},{5,4},{6,7},{7,6},{8,9},{9,8},{10,11... | collective-permute-start | bytes 1044488 | tf_op jit(solution)/shard_map/ppermute | solution.py:889
  57.9 0.7 copy-start.13
  57.9 0.7 copy-start.5
  58.7 5.6 %collective-permute-start.8 = (bf16[96,640]{1,0:T(8,128)(2,1)S(1)}, bf16[96,640]{1,0:T(8,128)(2,1)S(1)}, u32[]{:S(2)}, u32[]{:S(2)}) collective-permute-start(bf16[96,640]{1,0:T(8,128)(2,1)S(1)} %get-tuple-element.131), channel_id=1, source_target_pairs={{0,2},{1,3},{2,0},{3,1},{4,6},{5,7},{6,4},{7,5},{8,10},{9,11},{10,... | collective-permute-start | bytes 368648 | tf_op jit(solution)/shard_map/ppermute | solution.py:889
  60.4 7.8 %collective-permute-start.9 = (bf16[96,640]{1,0:T(8,128)(2,1)S(1)}, bf16[96,640]{1,0:T(8,128)(2,1)S(1)}, u32[]{:S(2)}, u32[]{:S(2)}) collective-permute-start(bf16[96,640]{1,0:T(8,128)(2,1)S(1)} %get-tuple-element.132), channel_id=1, source_target_pairs={{0,4},{1,5},{2,6},{3,7},{4,0},{5,1},{6,2},{7,3},{8,12},{9,13},{10,... | collective-permute-start | bytes 368648 | tf_op jit(solution)/shard_map/ppermute | solution.py:889
  61.1 7.2 %collective-permute-start.10 = (bf16[96,640]{1,0:T(8,128)(2,1)S(1)}, bf16[96,640]{1,0:T(8,128)(2,1)S(1)}, u32[]{:S(2)}, u32[]{:S(2)}) collective-permute-start(bf16[96,640]{1,0:T(8,128)(2,1)S(1)} %get-tuple-element.133), channel_id=1, source_target_pairs={{0,6},{1,7},{2,4},{3,5},{4,2},{5,3},{6,0},{7,1},{8,14},{9,15},{10,... | collective-permute-start | bytes 368648 | tf_op jit(solution)/shard_map/ppermute | solution.py:889
  64.3 4.1 %copy-start.1 = (bf16[96,640]{1,0:T(8,128)(2,1)}, bf16[96,640]{1,0:T(8,128)(2,1)S(1)}, u32[]{:S(2)}) copy-start(bf16[96,640]{1,0:T(8,128)(2,1)S(1)} %collective-permute-done.8.refs_2_) | copy-start | bytes 368644
  68.3 0.6 copy-start.2
  68.3 0.7 copy-start.3
  68.9 4.4 %collective-permute-start.11 = (bf16[64,640]{1,0:T(8,128)(2,1)S(1)}, bf16[64,640]{1,0:T(8,128)(2,1)S(1)}, u32[]{:S(2)}, u32[]{:S(2)}) collective-permute-start(bf16[64,640]{1,0:T(8,128)(2,1)S(1)} %fusion.3), channel_id=1, source_target_pairs={{0,8},{8,0},{16,24},{24,16},{1,9},{9,1},{17,25},{25,17},{2,10},{10... | collective-permute-start | bytes 245768 | tf_op jit(solution)/shard_map/ppermute | solution.py:889
  73.4 4.7 %copy-start.4 = (bf16[64,640]{1,0:T(8,128)(2,1)}, bf16[64,640]{1,0:T(8,128)(2,1)S(1)}, u32[]{:S(2)}) copy-start(bf16[64,640]{1,0:T(8,128)(2,1)S(1)} %add_convert_fusion.a_ref) | copy-start | bytes 245764
  73.4 5.4 %collective-permute-start.12 = (bf16[64,640]{1,0:T(8,128)(2,1)S(1)}, bf16[64,640]{1,0:T(8,128)(2,1)S(1)}, u32[]{:S(2)}, u32[]{:S(2)}) collective-permute-start(bf16[64,640]{1,0:T(8,128)(2,1)S(1)} %add_convert_fusion.a_ref), channel_id=1, source_target_pairs={{0,16},{8,24},{16,0},{24,8},{1,17},{9,25},{17,1},{25,9},{2,18},{10... | collective-permute-start | bytes 245768 | tf_op jit(solution)/shard_map/ppermute | solution.py:889
  78.8 0.6 copy-start.14
  81.3 1.4 %collective-permute-start.13 = (f32[8,128]{1,0:T(8,128)}, f32[8,128]{1,0:T(8,128)S(1)}, u32[]{:S(2)}, u32[]{:S(2)}) collective-permute-start(f32[8,128]{1,0:T(8,128)} %get-tuple-element.93), channel_id=1, source_target_pairs={{0,1},{1,0},{2,3},{3,2},{4,5},{5,4},{6,7},{7,6},{8,9},{9,8},{10,11... | collective-permute-start | bytes 12296 | tf_op jit(solution)/shard_map/ppermute | solution.py:889
  83.4 5.5 %collective-permute-start.16 = (f32[8,128]{1,0:T(8,128)S(1)}, f32[8,128]{1,0:T(8,128)S(1)}, u32[]{:S(2)}, u32[]{:S(2)}) collective-permute-start(f32[8,128]{1,0:T(8,128)S(1)} %add.23), channel_id=1, source_target_pairs={{0,6},{1,7},{2,4},{3,5},{4,2},{5,3},{6,0},{7,1},{8,14},{9,15},{10,... | collective-permute-start | bytes 12296 | tf_op jit(solution)/shard_map/ppermute | solution.py:889
  84.8 4.0 %collective-permute-start.15 = (f32[8,128]{1,0:T(8,128)S(1)}, f32[8,128]{1,0:T(8,128)S(1)}, u32[]{:S(2)}, u32[]{:S(2)}) collective-permute-start(f32[8,128]{1,0:T(8,128)S(1)} %add.23), channel_id=1, source_target_pairs={{0,4},{1,5},{2,6},{3,7},{4,0},{5,1},{6,2},{7,3},{8,12},{9,13},{10,... | collective-permute-start | bytes 12296 | tf_op jit(solution)/shard_map/ppermute | solution.py:889
  85.2 3.7 %collective-permute-start.14 = (f32[8,128]{1,0:T(8,128)S(1)}, f32[8,128]{1,0:T(8,128)S(1)}, u32[]{:S(2)}, u32[]{:S(2)}) collective-permute-start(f32[8,128]{1,0:T(8,128)S(1)} %add.23), channel_id=1, source_target_pairs={{0,2},{1,3},{2,0},{3,1},{4,6},{5,7},{6,4},{7,5},{8,10},{9,11},{10,... | collective-permute-start | bytes 12296 | tf_op jit(solution)/shard_map/ppermute | solution.py:889

commit v5 on v4

--- a/solution.py
+++ b/solution.py
@@ -561,11 +561,11 @@
     wide = (own + BLOCK) // LANES + 1
     width = channels + LANES
     out_shape = (
-        jax.ShapeDtypeStruct((chips, rows_own, width), F32),
-        jax.ShapeDtypeStruct((chips * rows_own + output_rows(own, channels), width), BF16),
-        jax.ShapeDtypeStruct((output_rows(own, channels), width), BF16),
-        jax.ShapeDtypeStruct((rows_own, LANES), F32),
-        jax.ShapeDtypeStruct((8, channels), F32),
+        pltpu.VMEM((chips, rows_own, width), F32),
+        pltpu.VMEM((chips * rows_own + output_rows(own, channels), width), BF16),
+        pltpu.VMEM((output_rows(own, channels), width), BF16),
+        pltpu.VMEM((rows_own, LANES), F32),
+        pltpu.VMEM((8, channels), F32),
     )
     vmem = pltpu.VMEM
     plan = buffer_plan(own)
@@ -602,7 +602,7 @@
         in_specs=[pl.BlockSpec(memory_space=pltpu.SMEM)] * 2 + [full] * (3 + 2 * chips),
         out_specs=[full] * 5,
         scratch_shapes=scratch,
-        compiler_params=pltpu.CompilerParams(vmem_limit_bytes=63 * 1024 * 1024),
+        compiler_params=pltpu.CompilerParams(vmem_limit_bytes=61 * 1024 * 1024),
         name="flow_block",
     )(me, u3, u2, planes, small, *packs)
 
@@ -885,12 +885,15 @@
     smem = pl.BlockSpec(memory_space=pltpu.SMEM)
     index = me.reshape(1).astype(jnp.int32)
 
+    def near_memory(values):
+        return pltpu.with_memory_space_constraint(values, pltpu.VMEM)
+
     def swap(values, axis, size, bits):
         return lax.ppermute(values, axis, [(j, j ^ bits) for j in range(size)])
 
     pack = pl.pallas_call(
         pack_kernel,
-        out_shape=jax.ShapeDtypeStruct((rows_own, width), F32),
+        out_shape=pltpu.VMEM((rows_own, width), F32),
         in_specs=[full] * 5,
         out_specs=full,
         name="pack_weights",
@@ -899,8 +902,8 @@
     planes, small = pl.pallas_call(
         functools.partial(prepare_kernel, own=own, frames=frames),
         out_shape=(
-            jax.ShapeDtypeStruct((40, own + 2 * HALO), F32),
-            jax.ShapeDtypeStruct((8, LANES), F32),
+            pltpu.VMEM((40, own + 2 * HALO), F32),
+            pltpu.VMEM((8, LANES), F32),
         ),
         in_specs=[smem] * 5 + [full] * 3,
         out_specs=[full] * 2,
@@ -913,7 +916,8 @@
         packs += [values, swap(values, "chan", shards, 1)]
 
     keep, send, og, cols_own, rows = call_main(
-        index, power_u3, power_u2.reshape(1, channels), planes, small, packs, own, channels, chips
+        index, power_u3, power_u2.reshape(1, channels), near_memory(planes), near_memory(small),
+        [near_memory(values) for values in packs], own, channels, chips
     )
 
     got = swap(send, "chan", shards, 1)
@@ -938,7 +942,7 @@
         out_specs=[full] * 3,
         scratch_shapes=[pltpu.VMEM((1, pixels), F32)],
         name="assemble_outputs",
-    )(index, frame_kinds, small_params, *pieces)
+    )(index, frame_kinds, small_params, *[near_memory(piece) for piece in pieces])
     bits = 1
     while 2 * bits < replicas:
         half = (half.astype(F32) + swap(half, "dp", replicas, bits).astype(F32)).astype(BF16)
@@ -951,13 +955,13 @@
     grad, parts = pl.pallas_call(
         functools.partial(norm_kernel, channels=channels),
         out_shape=(
-            jax.ShapeDtypeStruct((rows_own, width), F32),
-            jax.ShapeDtypeStruct((8, LANES), F32),
+            pltpu.VMEM((rows_own, width), F32),
+            pltpu.VMEM((8, LANES), F32),
         ),
         in_specs=[smem] + [full] * 5,
         out_specs=[full] * 2,
         name="norm_parts",
-    )(index, half, other, pack, cols_own, rows)
+    )(index, near_memory(half), near_memory(other), near_memory(pack), near_memory(cols_own), near_memory(rows))
     pair = parts + swap(parts, "chan", shards, 1)
     totals = [pair[0:1]] + [swap(pair, "chan", shards, 2 * m)[0:1] for m in range(1, chips)]
     totals = jnp.concatenate(totals, axis=0)
@@ -966,10 +970,10 @@
         return jax.ShapeDtypeStruct(value.shape, dtype)
 
     arranged_shape = (
-        [like(weight1.T)] * 2
-        + [jax.ShapeDtypeStruct((rows_own, channels), F32)]
-        + [like(weight3)] * 2
-        + [like(biases)]
+        [pltpu.VMEM(weight1.T.shape, F32)] * 2
+        + [pltpu.VMEM((rows_own, channels), F32)]
+        + [pltpu.VMEM(weight3.shape, F32)] * 2
+        + [pltpu.VMEM(biases.shape, F32)]
         + [jax.ShapeDtypeStruct((1, rows_own), F32), jax.ShapeDtypeStruct((1, 27), F32)]
         + [jax.ShapeDtypeStruct((1, channels), F32), jax.ShapeDtypeStruct((1, rows_own), F32)]
         + [jax.ShapeDtypeStruct((1, 3), F32), jax.ShapeDtypeStruct((9, rows_own), F32)]
@@ -980,7 +984,7 @@
         in_specs=[full] * 3,
         out_specs=[full] * len(arranged_shape),
         name="arrange_gradients",
-    )(grad, cols_own, rows)
+    )(near_memory(grad), near_memory(cols_own), near_memory(rows))
     vectors = arranged[6:]
     out_shape = (
         [jax.ShapeDtypeStruct((1, 1), F32)]
@@ -998,7 +1002,7 @@
         out_specs=[full] * len(out_shape),
         name="adam_update",
     )(
-        totals, rows, grad, *arranged[:6],
+        *[near_memory(values) for values in (totals, rows, grad, *arranged[:6])],
         weight1.T, moment_w1.T, second_w1.T, weight2.T, moment_w2.T, second_w2.T,
         weight3, moment_w3, second_w3, moment_bias, second_bias, small_params, moment_small, second_small,
     )

time: 92.6 us -> 83.9 us (0.906)
  Pallas kernels: 51.1 us -> 45 us
  local copies, waits for them, and re-layouts: 2.72 us -> 0.06 us
  waiting for transfers between devices: 19.3 us -> 20.6 us
  other arithmetic: 1.48 us -> 0.2 us
    unnamed x30 -> x0, local copies, waits for them, and re-layouts: 2.65 us -> none
    pallas_call x1, Pallas kernels: 38.9 us -> 37.2 us  [call_main(): pl.pallas_call(functools.partial(main_kernel, own=own, channels=channels,...]
    pallas_call x1, Pallas kernels: 1.82 us -> 0.19 us  [local(): pl.pallas_call(functools.partial(norm_kernel, channels=channels), out_sha...]
    ppermute x17, waiting for transfers between devices: 19.3 us -> 20.6 us  [swap(): return lax.ppermute(values, axis, [(j, j ^ bits) for j in range(size)])]
    pallas_call x1, Pallas kernels: 1.98 us -> 1.03 us  [local(): pl.pallas_call(functools.partial(arrange_kernel, channels=channels), out_...]
  transfers between devices with their start and end apart: 17 -> 17, of which waited for: 12 -> 14; matrix products, arithmetic and copies ran while one was open for 0% -> 0% of each run, Pallas kernels for 7% -> 5%
where the time goes in v5:
time: 83.9 us; the launch traced here: 83.7 us
  Pallas kernels  45 us (54%)
  waiting for transfers between devices  20.6 us (25%)
  starting transfers between devices  16.8 us (20%)
  between operations  0.96 us (1%)
    pallas_call x1, Pallas kernels, call_main(): pl.pallas_call(functools.partial(main_kernel, own=own, channels=channels,...  37.2 us
    ppermute x17, waiting for transfers between devices, swap(): return lax.ppermute(values, axis, [(j, j ^ bits) for j in range(size)])  20.6 us
    ppermute x17, starting transfers between devices, swap(): return lax.ppermute(values, axis, [(j, j ^ bits) for j in range(size)])  16.8 us
    pallas_call x1, Pallas kernels, local(): pl.pallas_call(functools.partial(update_kernel, channels=channels), out_s...  2.48 us
  transfers between devices with their start and end apart: 17, of which 14 were waited for; matrix products, arithmetic and copies ran while one was open for 0% of the time, Pallas kernels for 5%

profile of v5, /device:TPU:0, one launch (start us, length us, event | category | flops | bytes accessed | tf_op | source)
XLA Modules:
  0.0 83.7 jit_solution(17090157840454062048)
XLA Ops:
  0.7 1.2 %pack_weights.1.refs_0_.pack_ref = f32[64,640]{1,0:T(8,128)S(1)} custom-call(f32[27,64]{1,0:T(8,128)} %bitcast.46, f32[64,512]{1,0:T(8,128)} %bitcast.42, f32[27,64]{1,0:T(8,128)} %w3_ref.3, f32[2,64]{1,0:T(2,128)} %bias_ref.1, f32[1,64]{1,0:T(1,128)} %bitcast.51), custom_call_target="tpu_custom_call" | custom-call | tf_op jit(solution)/shard_map/pack_weights/pallas_call | solution.py:894
  1.9 4.0 %collective-permute-start = (f32[64,640]{1,0:T(8,128)S(1)}, f32[64,640]{1,0:T(8,128)S(1)}, u32[]{:S(2)}, u32[]{:S(2)}) collective-permute-start(f32[64,640]{1,0:T(8,128)S(1)} %pack_weights.1.refs_0_.pack_ref), channel_id=1, source_target_pairs={{0,6},{1,7},{2,4},{3,5},{4,2},{5,3},{6,0},{7,1},{8,14},{9,15},{10,... | collective-permute-start | bytes 491528 | tf_op jit(solution)/shard_map/ppermute | solution.py:892
  5.8 0.5 collective-permute-start.4
  6.3 0.1 collective-permute-start.2
  6.5 0.0 collective-permute-start.1
  6.5 1.3 %prepare_planes.1 = (f32[40,2048]{1,0:T(8,128)S(1)}, f32[8,128]{1,0:T(8,128)S(1)}) custom-call(s32[1]{0:T(128)} %bitcast.index_ref, s32[2]{0:T(128)} %kinds_ref.3, s32[2,4]{1,0:T(2,128)} %len_ref.1, f32[2,4]{1,0:T(2,128)} %cot_ref.1, f32[3,3]{1,0:T(4,128)} %small_ref.3, f32[3,8192]{1,0:T(4,128)} %images_ref.1, f32[3,8192]{1,0:T(4,128)} %probes_ref.1, ...), custom_call_target="tpu_custom_call" | custom-call | tf_op jit(solution)/shard_map/prepare_planes/pallas_call | solution.py:902
  7.8 3.0 %collective-permute-done.refs_6_ = f32[64,640]{1,0:T(8,128)S(1)} collective-permute-done((f32[64,640]{1,0:T(8,128)S(1)}, f32[64,640]{1,0:T(8,128)S(1)}, u32[]{:S(2)}, u32[]{:S(2)}) %collective-permute-start) | collective-permute-done | bytes 163872 | tf_op jit(solution)/shard_map/ppermute | solution.py:892
  10.8 2.7 %collective-permute-done.4.refs_4_ = f32[64,640]{1,0:T(8,128)S(1)} collective-permute-done((f32[64,640]{1,0:T(8,128)S(1)}, f32[64,640]{1,0:T(8,128)S(1)}, u32[]{:S(2)}, u32[]{:S(2)}) %collective-permute-start.4) | collective-permute-done | bytes 163872 | tf_op jit(solution)/shard_map/ppermute | solution.py:892
  13.5 0.0 collective-permute-start.5
  13.5 0.3 collective-permute-done.2.refs_2_
  13.8 0.2 collective-permute-start.3
  14.0 0.3 collective-permute-start.6
  14.3 0.0 collective-permute-done.1.refs_1_
  14.3 0.6 collective-permute-done.5.refs_5_
  14.9 0.3 collective-permute-done.3.refs_3_
  15.2 0.2 collective-permute-done.6.refs_7_
  15.4 37.2 %flow_block.1 = (f32[4,64,640]{2,1,0:T(8,128)S(1)}, bf16[272,640]{1,0:T(8,128)(2,1)S(1)}, bf16[16,640]{1,0:T(8,128)(2,1)S(1)}, f32[64,128]{1,0:T(8,128)S(1)}, f32[8,512]{1,0:T(8,128)S(1)}) custom-call(s32[1]{0:T(128)} %bitcast.index_ref, f32[3]{0:T(128)} %u3_ref.1, f32[1,512]{1,0:T(1,128)} %bitcast.50, f32[40,2048]{1,0:T(8,128)S(1)} %get-tuple-element.78.planes_ref, ...), custom_call_target="tpu_custom_call" | custom-call | tf_op jit(solution)/shard_map/flow_block/pallas_call | solution.py:599
  52.6 0.3 collective-permute-start.7
  53.0 1.4 %collective-permute-done.7 = bf16[272,640]{1,0:T(8,128)(2,1)S(1)} collective-permute-done((bf16[272,640]{1,0:T(8,128)(2,1)S(1)}, bf16[272,640]{1,0:T(8,128)(2,1)S(1)}, u32[]{:S(2)}, u32[]{:S(2)}) %collective-permute-start.7) | collective-permute-done | bytes 348192 | tf_op jit(solution)/shard_map/ppermute | solution.py:892
  54.4 0.1 fusion.4
  54.6 1.7 %collective-permute-start.8 = (bf16[96,640]{1,0:T(8,128)(2,1)S(1)}, bf16[96,640]{1,0:T(8,128)(2,1)S(1)}, u32[]{:S(2)}, u32[]{:S(2)}) collective-permute-start(bf16[96,640]{1,0:T(8,128)(2,1)S(1)} %get-tuple-element.131), channel_id=1, source_target_pairs={{0,2},{1,3},{2,0},{3,1},{4,6},{5,7},{6,4},{7,5},{8,10},{9,11},{10,... | collective-permute-start | bytes 368648 | tf_op jit(solution)/shard_map/ppermute | solution.py:892
  56.3 0.7 collective-permute-start.9
  57.0 1.1 %collective-permute-start.10 = (bf16[96,640]{1,0:T(8,128)(2,1)S(1)}, bf16[96,640]{1,0:T(8,128)(2,1)S(1)}, u32[]{:S(2)}, u32[]{:S(2)}) collective-permute-start(bf16[96,640]{1,0:T(8,128)(2,1)S(1)} %get-tuple-element.133), channel_id=1, source_target_pairs={{0,6},{1,7},{2,4},{3,5},{4,2},{5,3},{6,0},{7,1},{8,14},{9,15},{10,... | collective-permute-start | bytes 368648 | tf_op jit(solution)/shard_map/ppermute | solution.py:892
  58.1 2.1 %collective-permute-done.8.refs_2_ = bf16[96,640]{1,0:T(8,128)(2,1)S(1)} collective-permute-done((bf16[96,640]{1,0:T(8,128)(2,1)S(1)}, bf16[96,640]{1,0:T(8,128)(2,1)S(1)}, u32[]{:S(2)}, u32[]{:S(2)}) %collective-permute-start.8) | collective-permute-done | bytes 122912 | tf_op jit(solution)/shard_map/ppermute | solution.py:892
  60.2 3.9 %collective-permute-done.9.refs_3_ = bf16[96,640]{1,0:T(8,128)(2,1)S(1)} collective-permute-done((bf16[96,640]{1,0:T(8,128)(2,1)S(1)}, bf16[96,640]{1,0:T(8,128)(2,1)S(1)}, u32[]{:S(2)}, u32[]{:S(2)}) %collective-permute-start.9) | collective-permute-done | bytes 122912 | tf_op jit(solution)/shard_map/ppermute | solution.py:892
  64.1 0.0 collective-permute-done.10.refs_4_
  64.2 1.6 %collective-permute-start.11 = (bf16[64,640]{1,0:T(8,128)(2,1)S(1)}, bf16[64,640]{1,0:T(8,128)(2,1)S(1)}, u32[]{:S(2)}, u32[]{:S(2)}) collective-permute-start(bf16[64,640]{1,0:T(8,128)(2,1)S(1)} %fusion.3), channel_id=1, source_target_pairs={{0,8},{8,0},{16,24},{24,16},{1,9},{9,1},{17,25},{25,17},{2,10},{10... | collective-permute-start | bytes 245768 | tf_op jit(solution)/shard_map/ppermute | solution.py:892
  65.8 2.9 %collective-permute-done.11 = bf16[64,640]{1,0:T(8,128)(2,1)S(1)} collective-permute-done((bf16[64,640]{1,0:T(8,128)(2,1)S(1)}, bf16[64,640]{1,0:T(8,128)(2,1)S(1)}, u32[]{:S(2)}, u32[]{:S(2)}) %collective-permute-start.11) | collective-permute-done | bytes 81952 | tf_op jit(solution)/shard_map/ppermute | solution.py:892
  68.7 2.6 %collective-permute-start.12 = (bf16[64,640]{1,0:T(8,128)(2,1)S(1)}, bf16[64,640]{1,0:T(8,128)(2,1)S(1)}, u32[]{:S(2)}, u32[]{:S(2)}) collective-permute-start(bf16[64,640]{1,0:T(8,128)(2,1)S(1)} %add_convert_fusion.a_ref), channel_id=1, source_target_pairs={{0,16},{8,24},{16,0},{24,8},{1,17},{9,25},{17,1},{25,9},{2,18},{10... | collective-permute-start | bytes 245768 | tf_op jit(solution)/shard_map/ppermute | solution.py:892
  71.3 1.6 %assemble_outputs.1 = (f32[3,8192]{1,0:T(4,128)}, f32[3,8192]{1,0:T(4,128)}, f32[2,4]{1,0:T(2,128)}) custom-call(s32[1]{0:T(128)} %bitcast.index_ref, s32[2]{0:T(128)} %kinds_ref.3, f32[3,3]{1,0:T(4,128)} %small_ref.3, bf16[16,640]{1,0:T(8,128)(2,1)S(1)} %get-tuple-element.83.refs_0_, bf16[16,640]{1,0:T(8,128)(2,1)S(1)} %slice.58.refs_1_, ...), custom_call_target="tpu_custom_call" | custom-call | tf_op jit(solution)/shard_map/assemble_outputs/pallas_call | solution.py:934
  72.9 1.2 %collective-permute-done.12.b_ref = bf16[64,640]{1,0:T(8,128)(2,1)S(1)} collective-permute-done((bf16[64,640]{1,0:T(8,128)(2,1)S(1)}, bf16[64,640]{1,0:T(8,128)(2,1)S(1)}, u32[]{:S(2)}, u32[]{:S(2)}) %collective-permute-start.12) | collective-permute-done | bytes 81952 | tf_op jit(solution)/shard_map/ppermute | solution.py:892
  74.1 0.2 norm_parts.1
  74.3 0.1 collective-permute-start.13
  74.4 1.2 %collective-permute-done.13 = f32[8,128]{1,0:T(8,128)S(1)} collective-permute-done((f32[8,128]{1,0:T(8,128)S(1)}, f32[8,128]{1,0:T(8,128)S(1)}, u32[]{:S(2)}, u32[]{:S(2)}) %collective-permute-start.13) | collective-permute-done | bytes 4128 | tf_op jit(solution)/shard_map/ppermute | solution.py:892
  75.5 1.5 %collective-permute-start.16 = (f32[8,128]{1,0:T(8,128)S(1)}, f32[8,128]{1,0:T(8,128)S(1)}, u32[]{:S(2)}, u32[]{:S(2)}) collective-permute-start(f32[8,128]{1,0:T(8,128)S(1)} %add.23), channel_id=1, source_target_pairs={{0,6},{1,7},{2,4},{3,5},{4,2},{5,3},{6,0},{7,1},{8,14},{9,15},{10,... | collective-permute-start | bytes 12296 | tf_op jit(solution)/shard_map/ppermute | solution.py:892
  77.0 0.4 collective-permute-start.15
  77.4 1.6 %collective-permute-start.14 = (f32[8,128]{1,0:T(8,128)S(1)}, f32[8,128]{1,0:T(8,128)S(1)}, u32[]{:S(2)}, u32[]{:S(2)}) collective-permute-start(f32[8,128]{1,0:T(8,128)S(1)} %add.23), channel_id=1, source_target_pairs={{0,2},{1,3},{2,0},{3,1},{4,6},{5,7},{6,4},{7,5},{8,10},{9,11},{10,... | collective-permute-start | bytes 12296 | tf_op jit(solution)/shard_map/ppermute | solution.py:892
  79.0 1.0 %arrange_gradients.1 = (f32[27,64]{1,0:T(8,128)S(1)}, f32[27,64]{1,0:T(8,128)S(1)}, f32[64,512]{1,0:T(8,128)S(1)}, f32[27,64]{1,0:T(8,128)S(1)}, f32[27,64]{1,0:...) custom-call(f32[64,640]{1,0:T(8,128)S(1)} %get-tuple-element.94.grad, ...), custom_call_target="tpu_custom_call" | custom-call | tf_op jit(solution)/shard_map/arrange_gradients/pallas_call | solution.py:981
  80.1 0.0 collective-permute-done.16
  80.1 0.6 collective-permute-done.15
  80.6 0.4 collective-permute-done.14
  81.0 2.5 %adam_update.1 = (f32[1,1]{1,0:T(1,128)}, f32[27,64]{1,0:T(8,128)}, f32[27,64]{1,0:T(8,128)}, f32[27,64]{1,0:T(8,128)}, f32[64,512]{1,0:T(8,128)}, /*index=5*/f3...) custom-call(f32[4,128]{1,0:T(4,128)S(1)} %pad_maximum_fusion.6.total, ...), custom_call_target="tpu_custom_call" | custom-call | tf_op jit(solution)/shard_map/adam_update/pallas_call | solution.py:998
  (12 shorter events, 0.2 us)
Async XLA Ops:
  1.9 9.0 %collective-permute-start = (f32[64,640]{1,0:T(8,128)S(1)}, f32[64,640]{1,0:T(8,128)S(1)}, u32[]{:S(2)}, u32[]{:S(2)}) collective-permute-start(f32[64,640]{1,0:T(8,128)S(1)} %pack_weights.1.refs_0_.pack_ref), channel_id=1, source_target_pairs={{0,6},{1,7},{2,4},{3,5},{4,2},{5,3},{6,0},{7,1},{8,14},{9,15},{10,... | collective-permute-start | bytes 491528 | tf_op jit(solution)/shard_map/ppermute | solution.py:892
  5.8 7.7 %collective-permute-start.4 = (f32[64,640]{1,0:T(8,128)S(1)}, f32[64,640]{1,0:T(8,128)S(1)}, u32[]{:S(2)}, u32[]{:S(2)}) collective-permute-start(f32[64,640]{1,0:T(8,128)S(1)} %pack_weights.1.refs_0_.pack_ref), channel_id=1, source_target_pairs={{0,4},{1,5},{2,6},{3,7},{4,0},{5,1},{6,2},{7,3},{8,12},{9,13},{10,... | collective-permute-start | bytes 491528 | tf_op jit(solution)/shard_map/ppermute | solution.py:892
  6.3 7.5 %collective-permute-start.2 = (f32[64,640]{1,0:T(8,128)S(1)}, f32[64,640]{1,0:T(8,128)S(1)}, u32[]{:S(2)}, u32[]{:S(2)}) collective-permute-start(f32[64,640]{1,0:T(8,128)S(1)} %pack_weights.1.refs_0_.pack_ref), channel_id=1, source_target_pairs={{0,2},{1,3},{2,0},{3,1},{4,6},{5,7},{6,4},{7,5},{8,10},{9,11},{10,... | collective-permute-start | bytes 491528 | tf_op jit(solution)/shard_map/ppermute | solution.py:892
  6.5 7.9 %collective-permute-start.1 = (f32[64,640]{1,0:T(8,128)S(1)}, f32[64,640]{1,0:T(8,128)S(1)}, u32[]{:S(2)}, u32[]{:S(2)}) collective-permute-start(f32[64,640]{1,0:T(8,128)S(1)} %pack_weights.1.refs_0_.pack_ref), channel_id=1, source_target_pairs={{0,1},{1,0},{2,3},{3,2},{4,5},{5,4},{6,7},{7,6},{8,9},{9,8},{10,11... | collective-permute-start | bytes 491528 | tf_op jit(solution)/shard_map/ppermute | solution.py:892
  13.5 1.4 %collective-permute-start.5 = (f32[64,640]{1,0:T(8,128)S(1)}, f32[64,640]{1,0:T(8,128)S(1)}, u32[]{:S(2)}, u32[]{:S(2)}) collective-permute-start(f32[64,640]{1,0:T(8,128)S(1)} %collective-permute-done.4.refs_4_), channel_id=1, source_target_pairs={{0,1},{1,0},{2,3},{3,2},{4,5},{5,4},{6,7},{7,6},{8,9},{9,8},{10,11... | collective-permute-start | bytes 491528 | tf_op jit(solution)/shard_map/ppermute | solution.py:892
  13.8 1.4 %collective-permute-start.3 = (f32[64,640]{1,0:T(8,128)S(1)}, f32[64,640]{1,0:T(8,128)S(1)}, u32[]{:S(2)}, u32[]{:S(2)}) collective-permute-start(f32[64,640]{1,0:T(8,128)S(1)} %collective-permute-done.2.refs_2_), channel_id=1, source_target_pairs={{0,1},{1,0},{2,3},{3,2},{4,5},{5,4},{6,7},{7,6},{8,9},{9,8},{10,11... | collective-permute-start | bytes 491528 | tf_op jit(solution)/shard_map/ppermute | solution.py:892
  14.0 1.4 %collective-permute-start.6 = (f32[64,640]{1,0:T(8,128)S(1)}, f32[64,640]{1,0:T(8,128)S(1)}, u32[]{:S(2)}, u32[]{:S(2)}) collective-permute-start(f32[64,640]{1,0:T(8,128)S(1)} %collective-permute-done.refs_6_), channel_id=1, source_target_pairs={{0,1},{1,0},{2,3},{3,2},{4,5},{5,4},{6,7},{7,6},{8,9},{9,8},{10,11... | collective-permute-start | bytes 491528 | tf_op jit(solution)/shard_map/ppermute | solution.py:892
  52.6 1.7 %collective-permute-start.7 = (bf16[272,640]{1,0:T(8,128)(2,1)S(1)}, bf16[272,640]{1,0:T(8,128)(2,1)S(1)}, u32[]{:S(2)}, u32[]{:S(2)}) collective-permute-start(bf16[272,640]{1,0:T(8,128)(2,1)S(1)} %get-tuple-element.82), channel_id=1, source_target_pairs={{0,1},{1,0},{2,3},{3,2},{4,5},{5,4},{6,7},{7,6},{8,9},{9,8},{10,11... | collective-permute-start | bytes 1044488 | tf_op jit(solution)/shard_map/ppermute | solution.py:892
  54.6 5.6 %collective-permute-start.8 = (bf16[96,640]{1,0:T(8,128)(2,1)S(1)}, bf16[96,640]{1,0:T(8,128)(2,1)S(1)}, u32[]{:S(2)}, u32[]{:S(2)}) collective-permute-start(bf16[96,640]{1,0:T(8,128)(2,1)S(1)} %get-tuple-element.131), channel_id=1, source_target_pairs={{0,2},{1,3},{2,0},{3,1},{4,6},{5,7},{6,4},{7,5},{8,10},{9,11},{10,... | collective-permute-start | bytes 368648 | tf_op jit(solution)/shard_map/ppermute | solution.py:892
  56.3 7.8 %collective-permute-start.9 = (bf16[96,640]{1,0:T(8,128)(2,1)S(1)}, bf16[96,640]{1,0:T(8,128)(2,1)S(1)}, u32[]{:S(2)}, u32[]{:S(2)}) collective-permute-start(bf16[96,640]{1,0:T(8,128)(2,1)S(1)} %get-tuple-element.132), channel_id=1, source_target_pairs={{0,4},{1,5},{2,6},{3,7},{4,0},{5,1},{6,2},{7,3},{8,12},{9,13},{10,... | collective-permute-start | bytes 368648 | tf_op jit(solution)/shard_map/ppermute | solution.py:892
  57.0 7.1 %collective-permute-start.10 = (bf16[96,640]{1,0:T(8,128)(2,1)S(1)}, bf16[96,640]{1,0:T(8,128)(2,1)S(1)}, u32[]{:S(2)}, u32[]{:S(2)}) collective-permute-start(bf16[96,640]{1,0:T(8,128)(2,1)S(1)} %get-tuple-element.133), channel_id=1, source_target_pairs={{0,6},{1,7},{2,4},{3,5},{4,2},{5,3},{6,0},{7,1},{8,14},{9,15},{10,... | collective-permute-start | bytes 368648 | tf_op jit(solution)/shard_map/ppermute | solution.py:892
  64.2 4.5 %collective-permute-start.11 = (bf16[64,640]{1,0:T(8,128)(2,1)S(1)}, bf16[64,640]{1,0:T(8,128)(2,1)S(1)}, u32[]{:S(2)}, u32[]{:S(2)}) collective-permute-start(bf16[64,640]{1,0:T(8,128)(2,1)S(1)} %fusion.3), channel_id=1, source_target_pairs={{0,8},{8,0},{16,24},{24,16},{1,9},{9,1},{17,25},{25,17},{2,10},{10... | collective-permute-start | bytes 245768 | tf_op jit(solution)/shard_map/ppermute | solution.py:892
  68.7 5.4 %collective-permute-start.12 = (bf16[64,640]{1,0:T(8,128)(2,1)S(1)}, bf16[64,640]{1,0:T(8,128)(2,1)S(1)}, u32[]{:S(2)}, u32[]{:S(2)}) collective-permute-start(bf16[64,640]{1,0:T(8,128)(2,1)S(1)} %add_convert_fusion.a_ref), channel_id=1, source_target_pairs={{0,16},{8,24},{16,0},{24,8},{1,17},{9,25},{17,1},{25,9},{2,18},{10... | collective-permute-start | bytes 245768 | tf_op jit(solution)/shard_map/ppermute | solution.py:892
  74.3 1.2 %collective-permute-start.13 = (f32[8,128]{1,0:T(8,128)S(1)}, f32[8,128]{1,0:T(8,128)S(1)}, u32[]{:S(2)}, u32[]{:S(2)}) collective-permute-start(f32[8,128]{1,0:T(8,128)S(1)} %get-tuple-element.93), channel_id=1, source_target_pairs={{0,1},{1,0},{2,3},{3,2},{4,5},{5,4},{6,7},{7,6},{8,9},{9,8},{10,11... | collective-permute-start | bytes 12296 | tf_op jit(solution)/shard_map/ppermute | solution.py:892
  75.5 4.5 %collective-permute-start.16 = (f32[8,128]{1,0:T(8,128)S(1)}, f32[8,128]{1,0:T(8,128)S(1)}, u32[]{:S(2)}, u32[]{:S(2)}) collective-permute-start(f32[8,128]{1,0:T(8,128)S(1)} %add.23), channel_id=1, source_target_pairs={{0,6},{1,7},{2,4},{3,5},{4,2},{5,3},{6,0},{7,1},{8,14},{9,15},{10,... | collective-permute-start | bytes 12296 | tf_op jit(solution)/shard_map/ppermute | solution.py:892
  77.0 3.6 %collective-permute-start.15 = (f32[8,128]{1,0:T(8,128)S(1)}, f32[8,128]{1,0:T(8,128)S(1)}, u32[]{:S(2)}, u32[]{:S(2)}) collective-permute-start(f32[8,128]{1,0:T(8,128)S(1)} %add.23), channel_id=1, source_target_pairs={{0,4},{1,5},{2,6},{3,7},{4,0},{5,1},{6,2},{7,3},{8,12},{9,13},{10,... | collective-permute-start | bytes 12296 | tf_op jit(solution)/shard_map/ppermute | solution.py:892
  77.4 3.6 %collective-permute-start.14 = (f32[8,128]{1,0:T(8,128)S(1)}, f32[8,128]{1,0:T(8,128)S(1)}, u32[]{:S(2)}, u32[]{:S(2)}) collective-permute-start(f32[8,128]{1,0:T(8,128)S(1)} %add.23), channel_id=1, source_target_pairs={{0,2},{1,3},{2,0},{3,1},{4,6},{5,7},{6,4},{7,5},{8,10},{9,11},{10,... | collective-permute-start | bytes 12296 | tf_op jit(solution)/shard_map/ppermute | solution.py:892

commit v6 on v5

--- a/solution.py
+++ b/solution.py
@@ -608,8 +608,9 @@
 
 
 def assemble_kernel(index_ref, kinds_ref, small_ref, *refs, own, channels, chips, frames):
-    pieces = refs[: chips + 1]
-    z_ref, gin_ref, logdet_ref, dens_s = refs[chips + 1 :]
+    count = chips + 1 + (chips > 1)
+    pieces = refs[:count]
+    z_ref, gin_ref, logdet_ref, dens_s = refs[count:]
     me = index_ref[0]
     lines = max(own // channels, 1)
     size = min(own, channels)
@@ -617,12 +618,12 @@
     for m in range(chips):
         for b in range(2):
             shard = jnp.bitwise_xor(me, 2 * m + b)
-            if m == 0:
-                block = pieces[b][...]
+            if b == 0:
+                block = pieces[m][pieces[m].shape[0] - rows :]
+            elif m == 0:
+                block = pieces[chips][...]
             else:
-                message = pieces[m + 1]
-                first = message.shape[0] - (2 - b) * rows
-                block = message[first : first + rows]
+                block = pieces[chips + 1][(m - 1) * rows : m * rows]
             block = block.astype(F32)
             for c in range(lines):
                 lanes = pl.ds(pl.multiple_of(shard * own + c * size, LANES), size)
@@ -709,7 +710,13 @@
     return (param - LR_RATE * update, new_moment, new_second)
 
 
-def arrange_kernel(
+def arrange_kernel(grad_ref, cols_ref, rows_ref, *refs, channels):
+    for source, kept in zip(refs[:9], refs[9:18]):
+        kept[...] = source[...]
+    arrange_gradients(grad_ref, cols_ref, rows_ref, *refs[18:], channels=channels)
+
+
+def arrange_gradients(
     grad_ref, cols_ref, rows_ref,
     g1_out, o1_out, o2_out, g3_out, o3_out, bias_out, u1_out, v1_out, u2_out, v2_out, u3_out, v3_out, *, channels,
 ):
@@ -924,12 +931,16 @@
     og_other = got[chips * rows_own :]
     summed = keep + got[: chips * rows_own].reshape(keep.shape).astype(F32)
     total = summed[0]
-    pieces = [og, og_other]
+    near_og = [og]
     for m in range(1, chips):
-        message = jnp.concatenate([summed[m].astype(BF16), og, og_other], axis=0)
+        message = jnp.concatenate([summed[m].astype(BF16), og], axis=0)
         message = swap(message, "chan", shards, 2 * m)
         total = total + message[:rows_own].astype(F32)
-        pieces.append(message)
+        near_og.append(message)
+    tails = [message[rows_own:] for message in near_og[1:]]
+    pieces = near_og + [og_other]
+    if tails:
+        pieces.append(swap(jnp.concatenate(tails, axis=0), "chan", shards, 1))
     half = total.astype(BF16)
     assembled = pl.pallas_call(
         functools.partial(assemble_kernel, own=own, channels=channels, chips=chips, frames=frames),
@@ -938,7 +949,7 @@
             jax.ShapeDtypeStruct((3, pixels), F32),
             jax.ShapeDtypeStruct((frames, 4), F32),
         ),
-        in_specs=[smem] * 3 + [full] * (chips + 1),
+        in_specs=[smem] * 3 + [full] * len(pieces),
         out_specs=[full] * 3,
         scratch_shapes=[pltpu.VMEM((1, pixels), F32)],
         name="assemble_outputs",
@@ -978,13 +989,18 @@
         + [jax.ShapeDtypeStruct((1, channels), F32), jax.ShapeDtypeStruct((1, rows_own), F32)]
         + [jax.ShapeDtypeStruct((1, 3), F32), jax.ShapeDtypeStruct((9, rows_own), F32)]
     )
+    state = (
+        weight1.T, moment_w1.T, second_w1.T, weight2.T, moment_w2.T, second_w2.T, weight3, moment_w3, second_w3,
+    )
+    arranged_shape = [pltpu.VMEM(value.shape, F32) for value in state] + arranged_shape
     arranged = pl.pallas_call(
         functools.partial(arrange_kernel, channels=channels),
         out_shape=arranged_shape,
-        in_specs=[full] * 3,
+        in_specs=[full] * 12,
         out_specs=[full] * len(arranged_shape),
         name="arrange_gradients",
-    )(near_memory(grad), near_memory(cols_own), near_memory(rows))
+    )(near_memory(grad), near_memory(cols_own), near_memory(rows), *state)
+    state, arranged = arranged[:9], arranged[9:]
     vectors = arranged[6:]
     out_shape = (
         [jax.ShapeDtypeStruct((1, 1), F32)]
@@ -1003,8 +1019,7 @@
         name="adam_update",
     )(
         *[near_memory(values) for values in (totals, rows, grad, *arranged[:6])],
-        weight1.T, moment_w1.T, second_w1.T, weight2.T, moment_w2.T, second_w2.T,
-        weight3, moment_w3, second_w3, moment_bias, second_bias, small_params, moment_small, second_small,
+        *[near_memory(values) for values in state], moment_bias, second_bias, small_params, moment_small, second_small,
     )
     norm, updates = done[0], list(done[1:])
     for slot in (0, 1, 2, 3, 4, 5, 15, 16):

time: 83.9 us -> 83.1 us (level)
  waiting for transfers between devices: 20.6 us -> 18.8 us
    ppermute x17 -> x18, waiting for transfers between devices: 20.6 us -> 18.8 us  [swap(): return lax.ppermute(values, axis, [(j, j ^ bits) for j in range(size)])]
    pallas_call x1, Pallas kernels: 1.03 us -> 2.15 us  [local(): pl.pallas_call(functools.partial(arrange_kernel, channels=channels), out_...]
    ppermute x17 -> x18, starting transfers between devices: 16.8 us -> 17.1 us  [swap(): return lax.ppermute(values, axis, [(j, j ^ bits) for j in range(size)])]
  transfers between devices with their start and end apart: 17 -> 18, of which waited for: 14 -> 13; matrix products, arithmetic and copies ran while one was open for 0% -> 0% of each run, Pallas kernels for 5% -> 6%
where the time goes in v6:
time: 83.1 us; the launch traced here: 82.9 us
  Pallas kernels  45.7 us (55%)
  waiting for transfers between devices  18.8 us (23%)
  starting transfers between devices  17.1 us (21%)
  between operations  1.02 us (1%)
    pallas_call x1, Pallas kernels, call_main(): pl.pallas_call(functools.partial(main_kernel, own=own, channels=channels,...  37.2 us
    ppermute x18, waiting for transfers between devices, swap(): return lax.ppermute(values, axis, [(j, j ^ bits) for j in range(size)])  18.8 us
    ppermute x18, starting transfers between devices, swap(): return lax.ppermute(values, axis, [(j, j ^ bits) for j in range(size)])  17.1 us
    pallas_call x1, Pallas kernels, local(): pl.pallas_call(functools.partial(arrange_kernel, channels=channels), out_...  2.15 us
    pallas_call x1, Pallas kernels, local(): pl.pallas_call(functools.partial(update_kernel, channels=channels), out_s...  2.06 us
  transfers between devices with their start and end apart: 18, of which 13 were waited for; matrix products, arithmetic and copies ran while one was open for 0% of the time, Pallas kernels for 6%

profile of v6, /device:TPU:0, one launch (start us, length us, event | category | flops | bytes accessed | tf_op | source)
XLA Modules:
  0.0 82.9 jit_solution(8614675044830582668)
XLA Ops:
  0.7 1.2 %pack_weights.1.refs_0_.pack_ref = f32[64,640]{1,0:T(8,128)S(1)} custom-call(f32[27,64]{1,0:T(8,128)} %bitcast.46, f32[64,512]{1,0:T(8,128)} %bitcast.42, f32[27,64]{1,0:T(8,128)} %refs_6_.1, f32[2,64]{1,0:T(2,128)} %bias_ref.1, f32[1,64]{1,0:T(1,128)} %bitcast.51), custom_call_target="tpu_custom_call" | custom-call | tf_op jit(solution)/shard_map/pack_weights/pallas_call | solution.py:901
  1.9 4.0 %collective-permute-start = (f32[64,640]{1,0:T(8,128)S(1)}, f32[64,640]{1,0:T(8,128)S(1)}, u32[]{:S(2)}, u32[]{:S(2)}) collective-permute-start(f32[64,640]{1,0:T(8,128)S(1)} %pack_weights.1.refs_0_.pack_ref), channel_id=1, source_target_pairs={{0,6},{1,7},{2,4},{3,5},{4,2},{5,3},{6,0},{7,1},{8,14},{9,15},{10,... | collective-permute-start | bytes 491528 | tf_op jit(solution)/shard_map/ppermute | solution.py:899
  5.8 0.5 collective-permute-start.4
  6.3 0.1 collective-permute-start.2
  6.5 0.0 collective-permute-start.1
  6.5 1.3 %prepare_planes.1 = (f32[40,2048]{1,0:T(8,128)S(1)}, f32[8,128]{1,0:T(8,128)S(1)}) custom-call(s32[1]{0:T(128)} %bitcast.index_ref, s32[2]{0:T(128)} %kinds_ref.3, s32[2,4]{1,0:T(2,128)} %len_ref.1, f32[2,4]{1,0:T(2,128)} %cot_ref.1, f32[3,3]{1,0:T(4,128)} %small_ref.3, f32[3,8192]{1,0:T(4,128)} %images_ref.1, f32[3,8192]{1,0:T(4,128)} %probes_ref.1, ...), custom_call_target="tpu_custom_call" | custom-call | tf_op jit(solution)/shard_map/prepare_planes/pallas_call | solution.py:909
  7.8 3.0 %collective-permute-done.refs_6_ = f32[64,640]{1,0:T(8,128)S(1)} collective-permute-done((f32[64,640]{1,0:T(8,128)S(1)}, f32[64,640]{1,0:T(8,128)S(1)}, u32[]{:S(2)}, u32[]{:S(2)}) %collective-permute-start) | collective-permute-done | bytes 163872 | tf_op jit(solution)/shard_map/ppermute | solution.py:899
  10.8 2.7 %collective-permute-done.4.refs_4_ = f32[64,640]{1,0:T(8,128)S(1)} collective-permute-done((f32[64,640]{1,0:T(8,128)S(1)}, f32[64,640]{1,0:T(8,128)S(1)}, u32[]{:S(2)}, u32[]{:S(2)}) %collective-permute-start.4) | collective-permute-done | bytes 163872 | tf_op jit(solution)/shard_map/ppermute | solution.py:899
  13.5 0.0 collective-permute-start.5
  13.5 0.3 collective-permute-done.2.refs_2_
  13.8 0.2 collective-permute-start.3
  14.0 0.3 collective-permute-start.6
  14.3 0.0 collective-permute-done.1.refs_1_
  14.3 0.6 collective-permute-done.5.refs_5_
  14.9 0.3 collective-permute-done.3.refs_3_
  15.2 0.2 collective-permute-done.6.refs_7_
  15.4 37.2 %flow_block.1 = (f32[4,64,640]{2,1,0:T(8,128)S(1)}, bf16[272,640]{1,0:T(8,128)(2,1)S(1)}, bf16[16,640]{1,0:T(8,128)(2,1)S(1)}, f32[64,128]{1,0:T(8,128)S(1)}, f32[8,512]{1,0:T(8,128)S(1)}) custom-call(s32[1]{0:T(128)} %bitcast.index_ref, f32[3]{0:T(128)} %u3_ref.1, f32[1,512]{1,0:T(1,128)} %bitcast.50, f32[40,2048]{1,0:T(8,128)S(1)} %get-tuple-element.87.planes_ref, ...), custom_call_target="tpu_custom_call" | custom-call | tf_op jit(solution)/shard_map/flow_block/pallas_call | solution.py:599
  52.6 0.3 collective-permute-start.7
  53.0 1.4 %collective-permute-done.7 = bf16[272,640]{1,0:T(8,128)(2,1)S(1)} collective-permute-done((bf16[272,640]{1,0:T(8,128)(2,1)S(1)}, bf16[272,640]{1,0:T(8,128)(2,1)S(1)}, u32[]{:S(2)}, u32[]{:S(2)}) %collective-permute-start.7) | collective-permute-done | bytes 348192 | tf_op jit(solution)/shard_map/ppermute | solution.py:899
  54.4 0.1 fusion.4
  54.5 1.7 %collective-permute-start.8 = (bf16[80,640]{1,0:T(8,128)(2,1)S(1)}, bf16[80,640]{1,0:T(8,128)(2,1)S(1)}, u32[]{:S(2)}, u32[]{:S(2)}) collective-permute-start(bf16[80,640]{1,0:T(8,128)(2,1)S(1)} %get-tuple-element.149), channel_id=1, source_target_pairs={{0,2},{1,3},{2,0},{3,1},{4,6},{5,7},{6,4},{7,5},{8,10},{9,11},{10,... | collective-permute-start | bytes 307208 | tf_op jit(solution)/shard_map/ppermute | solution.py:899
  56.3 0.7 collective-permute-start.9
  57.0 1.1 %collective-permute-start.10 = (bf16[80,640]{1,0:T(8,128)(2,1)S(1)}, bf16[80,640]{1,0:T(8,128)(2,1)S(1)}, u32[]{:S(2)}, u32[]{:S(2)}) collective-permute-start(bf16[80,640]{1,0:T(8,128)(2,1)S(1)} %get-tuple-element.151), channel_id=1, source_target_pairs={{0,6},{1,7},{2,4},{3,5},{4,2},{5,3},{6,0},{7,1},{8,14},{9,15},{10,... | collective-permute-start | bytes 307208 | tf_op jit(solution)/shard_map/ppermute | solution.py:899
  58.1 1.6 %collective-permute-done.8.refs_1_ = bf16[80,640]{1,0:T(8,128)(2,1)S(1)} collective-permute-done((bf16[80,640]{1,0:T(8,128)(2,1)S(1)}, bf16[80,640]{1,0:T(8,128)(2,1)S(1)}, u32[]{:S(2)}, u32[]{:S(2)}) %collective-permute-start.8) | collective-permute-done | bytes 102432 | tf_op jit(solution)/shard_map/ppermute | solution.py:899
  59.7 3.5 %collective-permute-done.9.refs_2_ = bf16[80,640]{1,0:T(8,128)(2,1)S(1)} collective-permute-done((bf16[80,640]{1,0:T(8,128)(2,1)S(1)}, bf16[80,640]{1,0:T(8,128)(2,1)S(1)}, u32[]{:S(2)}, u32[]{:S(2)}) %collective-permute-start.9) | collective-permute-done | bytes 102432 | tf_op jit(solution)/shard_map/ppermute | solution.py:899
  63.2 0.0 collective-permute-done.10.refs_3_
  63.2 0.1 fusion.3
  63.3 1.6 %collective-permute-start.11 = (bf16[64,640]{1,0:T(8,128)(2,1)S(1)}, bf16[64,640]{1,0:T(8,128)(2,1)S(1)}, u32[]{:S(2)}, u32[]{:S(2)}) collective-permute-start(bf16[64,640]{1,0:T(8,128)(2,1)S(1)} %fusion.3), channel_id=1, source_target_pairs={{0,8},{8,0},{16,24},{24,16},{1,9},{9,1},{17,25},{25,17},{2,10},{10... | collective-permute-start | bytes 245768 | tf_op jit(solution)/shard_map/ppermute | solution.py:899
  64.9 0.0 slice-start.1
  65.0 0.0 slice-start.2
  65.0 2.8 %collective-permute-done.11 = bf16[64,640]{1,0:T(8,128)(2,1)S(1)} collective-permute-done((bf16[64,640]{1,0:T(8,128)(2,1)S(1)}, bf16[64,640]{1,0:T(8,128)(2,1)S(1)}, u32[]{:S(2)}, u32[]{:S(2)}) %collective-permute-start.11) | collective-permute-done | bytes 81952 | tf_op jit(solution)/shard_map/ppermute | solution.py:899
  67.8 0.0 copy-start.1
  67.8 2.6 %collective-permute-start.12 = (bf16[64,640]{1,0:T(8,128)(2,1)S(1)}, bf16[64,640]{1,0:T(8,128)(2,1)S(1)}, u32[]{:S(2)}, u32[]{:S(2)}) collective-permute-start(bf16[64,640]{1,0:T(8,128)(2,1)S(1)} %add_convert_fusion.a_ref), channel_id=1, source_target_pairs={{0,16},{8,24},{16,0},{24,8},{1,17},{9,25},{17,1},{25,9},{2,18},{10... | collective-permute-start | bytes 245768 | tf_op jit(solution)/shard_map/ppermute | solution.py:899
  70.5 0.1 collective-permute-start.13
  70.6 1.2 %collective-permute-done.13.refs_5_ = bf16[48,640]{1,0:T(8,128)(2,1)S(1)} collective-permute-done((bf16[48,640]{1,0:T(8,128)(2,1)S(1)}, bf16[48,640]{1,0:T(8,128)(2,1)S(1)}, u32[]{:S(2)}, u32[]{:S(2)}) %collective-permute-start.13) | collective-permute-done | bytes 61472 | tf_op jit(solution)/shard_map/ppermute | solution.py:899
  71.8 1.6 %assemble_outputs.1 = (f32[3,8192]{1,0:T(4,128)}, f32[3,8192]{1,0:T(4,128)}, f32[2,4]{1,0:T(2,128)}) custom-call(s32[1]{0:T(128)} %bitcast.index_ref, s32[2]{0:T(128)} %kinds_ref.3, f32[3,3]{1,0:T(4,128)} %small_ref.3, bf16[16,640]{1,0:T(8,128)(2,1)S(1)} %get-tuple-element.92.refs_0_, bf16[80,640]{1,0:T(8,128)(2,1)S(1)} %copy-done.1, ...), custom_call_target="tpu_custom_call" | custom-call | tf_op jit(solution)/shard_map/assemble_outputs/pallas_call | solution.py:945
  73.4 0.0 collective-permute-done.12.b_ref
  73.4 0.2 norm_parts.1
  73.6 0.2 collective-permute-start.14
  73.9 1.0 %collective-permute-done.14 = f32[8,128]{1,0:T(8,128)S(1)} collective-permute-done((f32[8,128]{1,0:T(8,128)S(1)}, f32[8,128]{1,0:T(8,128)S(1)}, u32[]{:S(2)}, u32[]{:S(2)}) %collective-permute-start.14) | collective-permute-done | bytes 4128 | tf_op jit(solution)/shard_map/ppermute | solution.py:899
  74.9 1.5 %collective-permute-start.17 = (f32[8,128]{1,0:T(8,128)S(1)}, f32[8,128]{1,0:T(8,128)S(1)}, u32[]{:S(2)}, u32[]{:S(2)}) collective-permute-start(f32[8,128]{1,0:T(8,128)S(1)} %add.23), channel_id=1, source_target_pairs={{0,6},{1,7},{2,4},{3,5},{4,2},{5,3},{6,0},{7,1},{8,14},{9,15},{10,... | collective-permute-start | bytes 12296 | tf_op jit(solution)/shard_map/ppermute | solution.py:899
  76.4 0.7 collective-permute-start.16
  77.0 1.3 %collective-permute-start.15 = (f32[8,128]{1,0:T(8,128)S(1)}, f32[8,128]{1,0:T(8,128)S(1)}, u32[]{:S(2)}, u32[]{:S(2)}) collective-permute-start(f32[8,128]{1,0:T(8,128)S(1)} %add.23), channel_id=1, source_target_pairs={{0,2},{1,3},{2,0},{3,1},{4,6},{5,7},{6,4},{7,5},{8,10},{9,11},{10,... | collective-permute-start | bytes 12296 | tf_op jit(solution)/shard_map/ppermute | solution.py:899
  78.4 2.2 %arrange_gradients.1 = (f32[27,64]{1,0:T(8,128)S(1)}, f32[27,64]{1,0:T(8,128)S(1)}, f32[27,64]{1,0:T(8,128)S(1)}, f32[64,512]{1,0:T(8,128)S(1)}, f32[64,512]{1,0...) custom-call(f32[64,640]{1,0:T(8,128)S(1)} %get-tuple-element.103.gra, ...), custom_call_target="tpu_custom_call" | custom-call | tf_op jit(solution)/shard_map/arrange_gradients/pallas_call | solution.py:996
  80.5 0.0 collective-permute-done.17
  80.6 0.0 collective-permute-done.16
  80.6 0.1 collective-permute-done.15
  80.7 2.1 %adam_update.1 = (f32[1,1]{1,0:T(1,128)}, f32[27,64]{1,0:T(8,128)}, f32[27,64]{1,0:T(8,128)}, f32[27,64]{1,0:T(8,128)}, f32[64,512]{1,0:T(8,128)}, /*index=5*/f3...) custom-call(f32[4,128]{1,0:T(4,128)S(1)} %pad_maximum_fusion.4.total, ...), custom_call_target="tpu_custom_call" | custom-call | tf_op jit(solution)/shard_map/adam_update/pallas_call | solution.py:1014
  (27 shorter events, 0.2 us)
Async XLA Ops:
  1.9 9.0 %collective-permute-start = (f32[64,640]{1,0:T(8,128)S(1)}, f32[64,640]{1,0:T(8,128)S(1)}, u32[]{:S(2)}, u32[]{:S(2)}) collective-permute-start(f32[64,640]{1,0:T(8,128)S(1)} %pack_weights.1.refs_0_.pack_ref), channel_id=1, source_target_pairs={{0,6},{1,7},{2,4},{3,5},{4,2},{5,3},{6,0},{7,1},{8,14},{9,15},{10,... | collective-permute-start | bytes 491528 | tf_op jit(solution)/shard_map/ppermute | solution.py:899
  5.8 7.7 %collective-permute-start.4 = (f32[64,640]{1,0:T(8,128)S(1)}, f32[64,640]{1,0:T(8,128)S(1)}, u32[]{:S(2)}, u32[]{:S(2)}) collective-permute-start(f32[64,640]{1,0:T(8,128)S(1)} %pack_weights.1.refs_0_.pack_ref), channel_id=1, source_target_pairs={{0,4},{1,5},{2,6},{3,7},{4,0},{5,1},{6,2},{7,3},{8,12},{9,13},{10,... | collective-permute-start | bytes 491528 | tf_op jit(solution)/shard_map/ppermute | solution.py:899
  6.3 7.5 %collective-permute-start.2 = (f32[64,640]{1,0:T(8,128)S(1)}, f32[64,640]{1,0:T(8,128)S(1)}, u32[]{:S(2)}, u32[]{:S(2)}) collective-permute-start(f32[64,640]{1,0:T(8,128)S(1)} %pack_weights.1.refs_0_.pack_ref), channel_id=1, source_target_pairs={{0,2},{1,3},{2,0},{3,1},{4,6},{5,7},{6,4},{7,5},{8,10},{9,11},{10,... | collective-permute-start | bytes 491528 | tf_op jit(solution)/shard_map/ppermute | solution.py:899
  6.5 7.9 %collective-permute-start.1 = (f32[64,640]{1,0:T(8,128)S(1)}, f32[64,640]{1,0:T(8,128)S(1)}, u32[]{:S(2)}, u32[]{:S(2)}) collective-permute-start(f32[64,640]{1,0:T(8,128)S(1)} %pack_weights.1.refs_0_.pack_ref), channel_id=1, source_target_pairs={{0,1},{1,0},{2,3},{3,2},{4,5},{5,4},{6,7},{7,6},{8,9},{9,8},{10,11... | collective-permute-start | bytes 491528 | tf_op jit(solution)/shard_map/ppermute | solution.py:899
  13.5 1.4 %collective-permute-start.5 = (f32[64,640]{1,0:T(8,128)S(1)}, f32[64,640]{1,0:T(8,128)S(1)}, u32[]{:S(2)}, u32[]{:S(2)}) collective-permute-start(f32[64,640]{1,0:T(8,128)S(1)} %collective-permute-done.4.refs_4_), channel_id=1, source_target_pairs={{0,1},{1,0},{2,3},{3,2},{4,5},{5,4},{6,7},{7,6},{8,9},{9,8},{10,11... | collective-permute-start | bytes 491528 | tf_op jit(solution)/shard_map/ppermute | solution.py:899
  13.8 1.4 %collective-permute-start.3 = (f32[64,640]{1,0:T(8,128)S(1)}, f32[64,640]{1,0:T(8,128)S(1)}, u32[]{:S(2)}, u32[]{:S(2)}) collective-permute-start(f32[64,640]{1,0:T(8,128)S(1)} %collective-permute-done.2.refs_2_), channel_id=1, source_target_pairs={{0,1},{1,0},{2,3},{3,2},{4,5},{5,4},{6,7},{7,6},{8,9},{9,8},{10,11... | collective-permute-start | bytes 491528 | tf_op jit(solution)/shard_map/ppermute | solution.py:899
  14.0 1.4 %collective-permute-start.6 = (f32[64,640]{1,0:T(8,128)S(1)}, f32[64,640]{1,0:T(8,128)S(1)}, u32[]{:S(2)}, u32[]{:S(2)}) collective-permute-start(f32[64,640]{1,0:T(8,128)S(1)} %collective-permute-done.refs_6_), channel_id=1, source_target_pairs={{0,1},{1,0},{2,3},{3,2},{4,5},{5,4},{6,7},{7,6},{8,9},{9,8},{10,11... | collective-permute-start | bytes 491528 | tf_op jit(solution)/shard_map/ppermute | solution.py:899
  52.6 1.7 %collective-permute-start.7 = (bf16[272,640]{1,0:T(8,128)(2,1)S(1)}, bf16[272,640]{1,0:T(8,128)(2,1)S(1)}, u32[]{:S(2)}, u32[]{:S(2)}) collective-permute-start(bf16[272,640]{1,0:T(8,128)(2,1)S(1)} %get-tuple-element.91), channel_id=1, source_target_pairs={{0,1},{1,0},{2,3},{3,2},{4,5},{5,4},{6,7},{7,6},{8,9},{9,8},{10,11... | collective-permute-start | bytes 1044488 | tf_op jit(solution)/shard_map/ppermute | solution.py:899
  54.5 5.1 %collective-permute-start.8 = (bf16[80,640]{1,0:T(8,128)(2,1)S(1)}, bf16[80,640]{1,0:T(8,128)(2,1)S(1)}, u32[]{:S(2)}, u32[]{:S(2)}) collective-permute-start(bf16[80,640]{1,0:T(8,128)(2,1)S(1)} %get-tuple-element.149), channel_id=1, source_target_pairs={{0,2},{1,3},{2,0},{3,1},{4,6},{5,7},{6,4},{7,5},{8,10},{9,11},{10,... | collective-permute-start | bytes 307208 | tf_op jit(solution)/shard_map/ppermute | solution.py:899
  56.3 7.0 %collective-permute-start.9 = (bf16[80,640]{1,0:T(8,128)(2,1)S(1)}, bf16[80,640]{1,0:T(8,128)(2,1)S(1)}, u32[]{:S(2)}, u32[]{:S(2)}) collective-permute-start(bf16[80,640]{1,0:T(8,128)(2,1)S(1)} %get-tuple-element.150), channel_id=1, source_target_pairs={{0,4},{1,5},{2,6},{3,7},{4,0},{5,1},{6,2},{7,3},{8,12},{9,13},{10,... | collective-permute-start | bytes 307208 | tf_op jit(solution)/shard_map/ppermute | solution.py:899
  57.0 6.2 %collective-permute-start.10 = (bf16[80,640]{1,0:T(8,128)(2,1)S(1)}, bf16[80,640]{1,0:T(8,128)(2,1)S(1)}, u32[]{:S(2)}, u32[]{:S(2)}) collective-permute-start(bf16[80,640]{1,0:T(8,128)(2,1)S(1)} %get-tuple-element.151), channel_id=1, source_target_pairs={{0,6},{1,7},{2,4},{3,5},{4,2},{5,3},{6,0},{7,1},{8,14},{9,15},{10,... | collective-permute-start | bytes 307208 | tf_op jit(solution)/shard_map/ppermute | solution.py:899
  59.7 5.3 %copy-start = (bf16[80,640]{1,0:T(8,128)(2,1)}, bf16[80,640]{1,0:T(8,128)(2,1)S(1)}, u32[]{:S(2)}) copy-start(bf16[80,640]{1,0:T(8,128)(2,1)S(1)} %collective-permute-done.8.refs_1_) | copy-start | bytes 307204
  63.2 1.7 %copy-start.2 = (bf16[80,640]{1,0:T(8,128)(2,1)}, bf16[80,640]{1,0:T(8,128)(2,1)S(1)}, u32[]{:S(2)}) copy-start(bf16[80,640]{1,0:T(8,128)(2,1)S(1)} %collective-permute-done.9.refs_2_) | copy-start | bytes 307204
  63.2 1.7 %copy-start.4 = (bf16[80,640]{1,0:T(8,128)(2,1)}, bf16[80,640]{1,0:T(8,128)(2,1)S(1)}, u32[]{:S(2)}) copy-start(bf16[80,640]{1,0:T(8,128)(2,1)S(1)} %collective-permute-done.10.refs_3_) | copy-start | bytes 307204
  63.3 4.5 %collective-permute-start.11 = (bf16[64,640]{1,0:T(8,128)(2,1)S(1)}, bf16[64,640]{1,0:T(8,128)(2,1)S(1)}, u32[]{:S(2)}, u32[]{:S(2)}) collective-permute-start(bf16[64,640]{1,0:T(8,128)(2,1)S(1)} %fusion.3), channel_id=1, source_target_pairs={{0,8},{8,0},{16,24},{24,16},{1,9},{9,1},{17,25},{25,17},{2,10},{10... | collective-permute-start | bytes 245768 | tf_op jit(solution)/shard_map/ppermute | solution.py:899
  64.9 5.5 %slice-start = ((bf16[80,640]{1,0:T(8,128)(2,1)}), bf16[16,640]{1,0:T(8,128)(2,1)S(1)}, s32[]{:S(2)}) async-start(bf16[80,640]{1,0:T(8,128)(2,1)} %copy-done), calls=%async_computation | async-start | bytes 40960 | tf_op jit(solution)/shard_map/slice | solution.py:940
  64.9 5.5 %slice-start.1 = ((bf16[80,640]{1,0:T(8,128)(2,1)}), bf16[16,640]{1,0:T(8,128)(2,1)S(1)}, s32[]{:S(2)}) async-start(bf16[80,640]{1,0:T(8,128)(2,1)} %copy-done.2), calls=%async_computation.1 | async-start | bytes 40960 | tf_op jit(solution)/shard_map/slice | solution.py:940
  65.0 5.5 %slice-start.2 = ((bf16[80,640]{1,0:T(8,128)(2,1)}), bf16[16,640]{1,0:T(8,128)(2,1)S(1)}, s32[]{:S(2)}) async-start(bf16[80,640]{1,0:T(8,128)(2,1)} %copy-done.4), calls=%async_computation.2 | async-start | bytes 40960 | tf_op jit(solution)/shard_map/slice | solution.py:940
  67.8 4.0 %copy-start.3 = (bf16[80,640]{1,0:T(8,128)(2,1)S(1)}, bf16[80,640]{1,0:T(8,128)(2,1)}, u32[]{:S(2)}) copy-start(bf16[80,640]{1,0:T(8,128)(2,1)} %copy-done.2) | copy-start | bytes 307204
  67.8 4.0 %copy-start.5 = (bf16[80,640]{1,0:T(8,128)(2,1)S(1)}, bf16[80,640]{1,0:T(8,128)(2,1)}, u32[]{:S(2)}) copy-start(bf16[80,640]{1,0:T(8,128)(2,1)} %copy-done.4) | copy-start | bytes 307204
  67.8 4.0 %copy-start.1 = (bf16[80,640]{1,0:T(8,128)(2,1)S(1)}, bf16[80,640]{1,0:T(8,128)(2,1)}, u32[]{:S(2)}) copy-start(bf16[80,640]{1,0:T(8,128)(2,1)} %copy-done) | copy-start | bytes 307204
  67.8 5.6 %collective-permute-start.12 = (bf16[64,640]{1,0:T(8,128)(2,1)S(1)}, bf16[64,640]{1,0:T(8,128)(2,1)S(1)}, u32[]{:S(2)}, u32[]{:S(2)}) collective-permute-start(bf16[64,640]{1,0:T(8,128)(2,1)S(1)} %add_convert_fusion.a_ref), channel_id=1, source_target_pairs={{0,16},{8,24},{16,0},{24,8},{1,17},{9,25},{17,1},{25,9},{2,18},{10... | collective-permute-start | bytes 245768 | tf_op jit(solution)/shard_map/ppermute | solution.py:899
  70.5 1.3 %collective-permute-start.13 = (bf16[48,640]{1,0:T(8,128)(2,1)S(1)}, bf16[48,640]{1,0:T(8,128)(2,1)S(1)}, u32[]{:S(2)}, u32[]{:S(2)}) collective-permute-start(bf16[48,640]{1,0:T(8,128)(2,1)S(1)} %pad_maximum_fusion.3), channel_id=1, source_target_pairs={{0,1},{1,0},{2,3},{3,2},{4,5},{5,4},{6,7},{7,6},{8,9},{9,8},{10,11... | collective-permute-start | bytes 184328 | tf_op jit(solution)/shard_map/ppermute | solution.py:899
  73.6 1.2 %collective-permute-start.14 = (f32[8,128]{1,0:T(8,128)S(1)}, f32[8,128]{1,0:T(8,128)S(1)}, u32[]{:S(2)}, u32[]{:S(2)}) collective-permute-start(f32[8,128]{1,0:T(8,128)S(1)} %get-tuple-element.102), channel_id=1, source_target_pairs={{0,1},{1,0},{2,3},{3,2},{4,5},{5,4},{6,7},{7,6},{8,9},{9,8},{10,11... | collective-permute-start | bytes 12296 | tf_op jit(solution)/shard_map/ppermute | solution.py:899
  74.9 5.7 %collective-permute-start.17 = (f32[8,128]{1,0:T(8,128)S(1)}, f32[8,128]{1,0:T(8,128)S(1)}, u32[]{:S(2)}, u32[]{:S(2)}) collective-permute-start(f32[8,128]{1,0:T(8,128)S(1)} %add.23), channel_id=1, source_target_pairs={{0,6},{1,7},{2,4},{3,5},{4,2},{5,3},{6,0},{7,1},{8,14},{9,15},{10,... | collective-permute-start | bytes 12296 | tf_op jit(solution)/shard_map/ppermute | solution.py:899
  76.4 4.2 %collective-permute-start.16 = (f32[8,128]{1,0:T(8,128)S(1)}, f32[8,128]{1,0:T(8,128)S(1)}, u32[]{:S(2)}, u32[]{:S(2)}) collective-permute-start(f32[8,128]{1,0:T(8,128)S(1)} %add.23), channel_id=1, source_target_pairs={{0,4},{1,5},{2,6},{3,7},{4,0},{5,1},{6,2},{7,3},{8,12},{9,13},{10,... | collective-permute-start | bytes 12296 | tf_op jit(solution)/shard_map/ppermute | solution.py:899
  77.0 3.6 %collective-permute-start.15 = (f32[8,128]{1,0:T(8,128)S(1)}, f32[8,128]{1,0:T(8,128)S(1)}, u32[]{:S(2)}, u32[]{:S(2)}) collective-permute-start(f32[8,128]{1,0:T(8,128)S(1)} %add.23), channel_id=1, source_target_pairs={{0,2},{1,3},{2,0},{3,1},{4,6},{5,7},{6,4},{7,5},{8,10},{9,11},{10,... | collective-permute-start | bytes 12296 | tf_op jit(solution)/shard_map/ppermute | solution.py:899

commit v7 on v6

--- a/solution.py
+++ b/solution.py
@@ -180,30 +180,42 @@
     head = (lane % 8 == 4) & (lane < TAP_ROWS)
     u1 = tile[:, TAP_ROWS : TAP_ROWS + 1]
     u2 = u2_ref[...]
-    u3 = jnp.zeros((1, LANES), F32)
-    for o in range(3):
-        u3 = jnp.where(is_three & (lane % 8 == 4 + o), u3_ref[o], u3)
+    gram = {}
+    for gap in range(3):
+        other = pltpu.roll(taps_three, LANES - gap, 1) if gap else taps_three
+        line = all_sum(taps_three * other, axis=0)
+        for shift in (64, 32, 16, 8):
+            line = line + pltpu.roll(line, shift, 1)
+        for o in range(3 - gap):
+            gram[o, o + gap] = gram[o + gap, o] = line[:, 4 + o : 5 + o]
+    u3 = [jnp.full((1, 1), u3_ref[o], F32) for o in range(3)]
     for _ in range(2):
         v1 = all_sum(taps_one * u1, axis=0)
         v2 = all_sum(w2t * u2, axis=1)
-        mixed = taps_three * u3
-        mixed = mixed + pltpu.roll(mixed, LANES - 1, 1) + pltpu.roll(mixed, LANES - 2, 1)
-        v3 = jnp.where(head, mixed, 0.0)
+        before3 = u3
+        m3 = [sum(gram[o, p] * u3[p] for p in range(3)) for o in range(3)]
+        v3_square = jnp.maximum(sum(m3[o] * u3[o] for o in range(3)), 0.0)
         v1 = normed_by(v1, all_sum(v1 * v1))
         v2 = normed_by(v2, all_sum(v2 * v2))
-        v3 = normed_by(v3, all_sum(all_sum(v3 * v3, axis=0), axis=1))
+        m3 = [normed_by(value, v3_square) for value in m3]
         m1 = all_sum(taps_one * v1, axis=1)
         m2 = all_sum(w2t * v2, axis=0)
-        spread = v3 + pltpu.roll(v3, 1, 1) + pltpu.roll(v3, 2, 1)
-        m3 = all_sum(taps_three * spread, axis=0)
-        for shift in (64, 32, 16, 8):
-            m3 = m3 + pltpu.roll(m3, shift, 1)
         square1 = all_sum(m1 * m1)
         square2 = all_sum(m2 * m2)
-        square3 = all_sum(jnp.where((lane >= 4) & (lane < 7), m3 * m3, 0.0))
+        square3 = sum(value * value for value in m3)
         u1 = normed_by(m1, square1)
         u2 = normed_by(m2, square2)
-        u3 = jnp.where(is_three, normed_by(m3, square3), 0.0)
+        u3 = [normed_by(value, square3) for value in m3]
+    def three_lanes(values):
+        line = jnp.zeros((1, LANES), F32)
+        for o in range(3):
+            line = jnp.where(is_three & (lane % 8 == 4 + o), values[o], line)
+        return line
+
+    mixed = taps_three * normed_by(three_lanes(before3), v3_square)
+    mixed = mixed + pltpu.roll(mixed, LANES - 1, 1) + pltpu.roll(mixed, LANES - 2, 1)
+    v3 = jnp.where(head, mixed, 0.0)
+    u3 = three_lanes(u3)
     sigma1 = jnp.sqrt(square1)
     sigma2 = jnp.sqrt(square2)
     sigma3 = jnp.sqrt(square3)

time: 83.1 us -> 82.8 us (level)
  no operation moved by 1% of the time
where the time goes in v7:
time: 82.8 us; the launch traced here: 82.5 us
  Pallas kernels  45.4 us (55%)
  waiting for transfers between devices  18.7 us (23%)
  starting transfers between devices  17.1 us (21%)
  between operations  1.02 us (1%)
    pallas_call x1, Pallas kernels, call_main(): pl.pallas_call(functools.partial(main_kernel, own=own, channels=channels,...  36.8 us
    ppermute x18, waiting for transfers between devices, swap(): return lax.ppermute(values, axis, [(j, j ^ bits) for j in range(size)])  18.7 us
    ppermute x18, starting transfers between devices, swap(): return lax.ppermute(values, axis, [(j, j ^ bits) for j in range(size)])  17.1 us
    pallas_call x1, Pallas kernels, local(): pl.pallas_call(functools.partial(arrange_kernel, channels=channels), out_...  2.15 us
    pallas_call x1, Pallas kernels, local(): pl.pallas_call(functools.partial(update_kernel, channels=channels), out_s...  2.06 us
  transfers between devices with their start and end apart: 18, of which 13 were waited for; matrix products, arithmetic and copies ran while one was open for 0% of the time, Pallas kernels for 6%

profile of v7, /device:TPU:0, one launch (start us, length us, event | category | flops | bytes accessed | tf_op | source)
XLA Modules:
  0.0 82.5 jit_solution(6979025466534697225)
XLA Ops:
  0.7 1.2 %pack_weights.1.refs_0_.pack_ref = f32[64,640]{1,0:T(8,128)S(1)} custom-call(f32[27,64]{1,0:T(8,128)} %bitcast.46, f32[64,512]{1,0:T(8,128)} %bitcast.42, f32[27,64]{1,0:T(8,128)} %refs_6_.1, f32[2,64]{1,0:T(2,128)} %bias_ref.1, f32[1,64]{1,0:T(1,128)} %bitcast.51), custom_call_target="tpu_custom_call" | custom-call | tf_op jit(solution)/shard_map/pack_weights/pallas_call | solution.py:913
  1.9 4.0 %collective-permute-start = (f32[64,640]{1,0:T(8,128)S(1)}, f32[64,640]{1,0:T(8,128)S(1)}, u32[]{:S(2)}, u32[]{:S(2)}) collective-permute-start(f32[64,640]{1,0:T(8,128)S(1)} %pack_weights.1.refs_0_.pack_ref), channel_id=1, source_target_pairs={{0,6},{1,7},{2,4},{3,5},{4,2},{5,3},{6,0},{7,1},{8,14},{9,15},{10,... | collective-permute-start | bytes 491528 | tf_op jit(solution)/shard_map/ppermute | solution.py:911
  5.8 0.5 collective-permute-start.4
  6.3 0.1 collective-permute-start.2
  6.5 0.0 collective-permute-start.1
  6.5 1.3 %prepare_planes.1 = (f32[40,2048]{1,0:T(8,128)S(1)}, f32[8,128]{1,0:T(8,128)S(1)}) custom-call(s32[1]{0:T(128)} %bitcast.index_ref, s32[2]{0:T(128)} %kinds_ref.3, s32[2,4]{1,0:T(2,128)} %len_ref.1, f32[2,4]{1,0:T(2,128)} %cot_ref.1, f32[3,3]{1,0:T(4,128)} %small_ref.3, f32[3,8192]{1,0:T(4,128)} %images_ref.1, f32[3,8192]{1,0:T(4,128)} %probes_ref.1, ...), custom_call_target="tpu_custom_call" | custom-call | tf_op jit(solution)/shard_map/prepare_planes/pallas_call | solution.py:921
  7.8 3.0 %collective-permute-done.refs_6_ = f32[64,640]{1,0:T(8,128)S(1)} collective-permute-done((f32[64,640]{1,0:T(8,128)S(1)}, f32[64,640]{1,0:T(8,128)S(1)}, u32[]{:S(2)}, u32[]{:S(2)}) %collective-permute-start) | collective-permute-done | bytes 163872 | tf_op jit(solution)/shard_map/ppermute | solution.py:911
  10.8 2.7 %collective-permute-done.4.refs_4_ = f32[64,640]{1,0:T(8,128)S(1)} collective-permute-done((f32[64,640]{1,0:T(8,128)S(1)}, f32[64,640]{1,0:T(8,128)S(1)}, u32[]{:S(2)}, u32[]{:S(2)}) %collective-permute-start.4) | collective-permute-done | bytes 163872 | tf_op jit(solution)/shard_map/ppermute | solution.py:911
  13.5 0.0 collective-permute-start.5
  13.5 0.3 collective-permute-done.2.refs_2_
  13.8 0.2 collective-permute-start.3
  14.0 0.3 collective-permute-start.6
  14.3 0.0 collective-permute-done.1.refs_1_
  14.3 0.6 collective-permute-done.5.refs_5_
  14.9 0.3 collective-permute-done.3.refs_3_
  15.2 0.2 collective-permute-done.6.refs_7_
  15.4 36.8 %flow_block.1 = (f32[4,64,640]{2,1,0:T(8,128)S(1)}, bf16[272,640]{1,0:T(8,128)(2,1)S(1)}, bf16[16,640]{1,0:T(8,128)(2,1)S(1)}, f32[64,128]{1,0:T(8,128)S(1)}, f32[8,512]{1,0:T(8,128)S(1)}) custom-call(s32[1]{0:T(128)} %bitcast.index_ref, f32[3]{0:T(128)} %u3_ref.1, f32[1,512]{1,0:T(1,128)} %bitcast.50, f32[40,2048]{1,0:T(8,128)S(1)} %get-tuple-element.87.planes_ref, ...), custom_call_target="tpu_custom_call" | custom-call | tf_op jit(solution)/shard_map/flow_block/pallas_call | solution.py:611
  52.3 0.3 collective-permute-start.7
  52.6 1.4 %collective-permute-done.7 = bf16[272,640]{1,0:T(8,128)(2,1)S(1)} collective-permute-done((bf16[272,640]{1,0:T(8,128)(2,1)S(1)}, bf16[272,640]{1,0:T(8,128)(2,1)S(1)}, u32[]{:S(2)}, u32[]{:S(2)}) %collective-permute-start.7) | collective-permute-done | bytes 348192 | tf_op jit(solution)/shard_map/ppermute | solution.py:911
  54.0 0.1 fusion.4
  54.2 1.7 %collective-permute-start.8 = (bf16[80,640]{1,0:T(8,128)(2,1)S(1)}, bf16[80,640]{1,0:T(8,128)(2,1)S(1)}, u32[]{:S(2)}, u32[]{:S(2)}) collective-permute-start(bf16[80,640]{1,0:T(8,128)(2,1)S(1)} %get-tuple-element.149), channel_id=1, source_target_pairs={{0,2},{1,3},{2,0},{3,1},{4,6},{5,7},{6,4},{7,5},{8,10},{9,11},{10,... | collective-permute-start | bytes 307208 | tf_op jit(solution)/shard_map/ppermute | solution.py:911
  55.9 0.7 collective-permute-start.9
  56.6 1.1 %collective-permute-start.10 = (bf16[80,640]{1,0:T(8,128)(2,1)S(1)}, bf16[80,640]{1,0:T(8,128)(2,1)S(1)}, u32[]{:S(2)}, u32[]{:S(2)}) collective-permute-start(bf16[80,640]{1,0:T(8,128)(2,1)S(1)} %get-tuple-element.151), channel_id=1, source_target_pairs={{0,6},{1,7},{2,4},{3,5},{4,2},{5,3},{6,0},{7,1},{8,14},{9,15},{10,... | collective-permute-start | bytes 307208 | tf_op jit(solution)/shard_map/ppermute | solution.py:911
  57.8 1.6 %collective-permute-done.8.refs_1_ = bf16[80,640]{1,0:T(8,128)(2,1)S(1)} collective-permute-done((bf16[80,640]{1,0:T(8,128)(2,1)S(1)}, bf16[80,640]{1,0:T(8,128)(2,1)S(1)}, u32[]{:S(2)}, u32[]{:S(2)}) %collective-permute-start.8) | collective-permute-done | bytes 102432 | tf_op jit(solution)/shard_map/ppermute | solution.py:911
  59.3 3.5 %collective-permute-done.9.refs_2_ = bf16[80,640]{1,0:T(8,128)(2,1)S(1)} collective-permute-done((bf16[80,640]{1,0:T(8,128)(2,1)S(1)}, bf16[80,640]{1,0:T(8,128)(2,1)S(1)}, u32[]{:S(2)}, u32[]{:S(2)}) %collective-permute-start.9) | collective-permute-done | bytes 102432 | tf_op jit(solution)/shard_map/ppermute | solution.py:911
  62.9 0.0 collective-permute-done.10.refs_3_
  62.9 0.1 fusion.3
  62.9 1.6 %collective-permute-start.11 = (bf16[64,640]{1,0:T(8,128)(2,1)S(1)}, bf16[64,640]{1,0:T(8,128)(2,1)S(1)}, u32[]{:S(2)}, u32[]{:S(2)}) collective-permute-start(bf16[64,640]{1,0:T(8,128)(2,1)S(1)} %fusion.3), channel_id=1, source_target_pairs={{0,8},{8,0},{16,24},{24,16},{1,9},{9,1},{17,25},{25,17},{2,10},{10... | collective-permute-start | bytes 245768 | tf_op jit(solution)/shard_map/ppermute | solution.py:911
  64.6 0.0 slice-start.1
  64.6 0.0 slice-start.2
  64.6 2.8 %collective-permute-done.11 = bf16[64,640]{1,0:T(8,128)(2,1)S(1)} collective-permute-done((bf16[64,640]{1,0:T(8,128)(2,1)S(1)}, bf16[64,640]{1,0:T(8,128)(2,1)S(1)}, u32[]{:S(2)}, u32[]{:S(2)}) %collective-permute-start.11) | collective-permute-done | bytes 81952 | tf_op jit(solution)/shard_map/ppermute | solution.py:911
  67.5 0.0 copy-start.1
  67.5 2.7 %collective-permute-start.12 = (bf16[64,640]{1,0:T(8,128)(2,1)S(1)}, bf16[64,640]{1,0:T(8,128)(2,1)S(1)}, u32[]{:S(2)}, u32[]{:S(2)}) collective-permute-start(bf16[64,640]{1,0:T(8,128)(2,1)S(1)} %add_convert_fusion.a_ref), channel_id=1, source_target_pairs={{0,16},{8,24},{16,0},{24,8},{1,17},{9,25},{17,1},{25,9},{2,18},{10... | collective-permute-start | bytes 245768 | tf_op jit(solution)/shard_map/ppermute | solution.py:911
  70.2 0.1 collective-permute-start.13
  70.2 1.2 %collective-permute-done.13.refs_5_ = bf16[48,640]{1,0:T(8,128)(2,1)S(1)} collective-permute-done((bf16[48,640]{1,0:T(8,128)(2,1)S(1)}, bf16[48,640]{1,0:T(8,128)(2,1)S(1)}, u32[]{:S(2)}, u32[]{:S(2)}) %collective-permute-start.13) | collective-permute-done | bytes 61472 | tf_op jit(solution)/shard_map/ppermute | solution.py:911
  71.5 1.6 %assemble_outputs.1 = (f32[3,8192]{1,0:T(4,128)}, f32[3,8192]{1,0:T(4,128)}, f32[2,4]{1,0:T(2,128)}) custom-call(s32[1]{0:T(128)} %bitcast.index_ref, s32[2]{0:T(128)} %kinds_ref.3, f32[3,3]{1,0:T(4,128)} %small_ref.3, bf16[16,640]{1,0:T(8,128)(2,1)S(1)} %get-tuple-element.92.refs_0_, bf16[80,640]{1,0:T(8,128)(2,1)S(1)} %copy-done.1, ...), custom_call_target="tpu_custom_call" | custom-call | tf_op jit(solution)/shard_map/assemble_outputs/pallas_call | solution.py:957
  73.1 0.0 collective-permute-done.12.b_ref
  73.1 0.2 norm_parts.1
  73.3 0.2 collective-permute-start.14
  73.5 1.0 %collective-permute-done.14 = f32[8,128]{1,0:T(8,128)S(1)} collective-permute-done((f32[8,128]{1,0:T(8,128)S(1)}, f32[8,128]{1,0:T(8,128)S(1)}, u32[]{:S(2)}, u32[]{:S(2)}) %collective-permute-start.14) | collective-permute-done | bytes 4128 | tf_op jit(solution)/shard_map/ppermute | solution.py:911
  74.5 1.5 %collective-permute-start.17 = (f32[8,128]{1,0:T(8,128)S(1)}, f32[8,128]{1,0:T(8,128)S(1)}, u32[]{:S(2)}, u32[]{:S(2)}) collective-permute-start(f32[8,128]{1,0:T(8,128)S(1)} %add.23), channel_id=1, source_target_pairs={{0,6},{1,7},{2,4},{3,5},{4,2},{5,3},{6,0},{7,1},{8,14},{9,15},{10,... | collective-permute-start | bytes 12296 | tf_op jit(solution)/shard_map/ppermute | solution.py:911
  76.0 0.6 collective-permute-start.16
  76.7 1.3 %collective-permute-start.15 = (f32[8,128]{1,0:T(8,128)S(1)}, f32[8,128]{1,0:T(8,128)S(1)}, u32[]{:S(2)}, u32[]{:S(2)}) collective-permute-start(f32[8,128]{1,0:T(8,128)S(1)} %add.23), channel_id=1, source_target_pairs={{0,2},{1,3},{2,0},{3,1},{4,6},{5,7},{6,4},{7,5},{8,10},{9,11},{10,... | collective-permute-start | bytes 12296 | tf_op jit(solution)/shard_map/ppermute | solution.py:911
  78.0 2.2 %arrange_gradients.1 = (f32[27,64]{1,0:T(8,128)S(1)}, f32[27,64]{1,0:T(8,128)S(1)}, f32[27,64]{1,0:T(8,128)S(1)}, f32[64,512]{1,0:T(8,128)S(1)}, f32[64,512]{1,0...) custom-call(f32[64,640]{1,0:T(8,128)S(1)} %get-tuple-element.103.gra, ...), custom_call_target="tpu_custom_call" | custom-call | tf_op jit(solution)/shard_map/arrange_gradients/pallas_call | solution.py:1008
  80.2 0.0 collective-permute-done.17
  80.2 0.0 collective-permute-done.16
  80.2 0.1 collective-permute-done.15
  80.3 2.1 %adam_update.1 = (f32[1,1]{1,0:T(1,128)}, f32[27,64]{1,0:T(8,128)}, f32[27,64]{1,0:T(8,128)}, f32[27,64]{1,0:T(8,128)}, f32[64,512]{1,0:T(8,128)}, /*index=5*/f3...) custom-call(f32[4,128]{1,0:T(4,128)S(1)} %pad_maximum_fusion.4.total, ...), custom_call_target="tpu_custom_call" | custom-call | tf_op jit(solution)/shard_map/adam_update/pallas_call | solution.py:1026
  (27 shorter events, 0.2 us)
Async XLA Ops:
  1.9 9.0 %collective-permute-start = (f32[64,640]{1,0:T(8,128)S(1)}, f32[64,640]{1,0:T(8,128)S(1)}, u32[]{:S(2)}, u32[]{:S(2)}) collective-permute-start(f32[64,640]{1,0:T(8,128)S(1)} %pack_weights.1.refs_0_.pack_ref), channel_id=1, source_target_pairs={{0,6},{1,7},{2,4},{3,5},{4,2},{5,3},{6,0},{7,1},{8,14},{9,15},{10,... | collective-permute-start | bytes 491528 | tf_op jit(solution)/shard_map/ppermute | solution.py:911
  5.8 7.7 %collective-permute-start.4 = (f32[64,640]{1,0:T(8,128)S(1)}, f32[64,640]{1,0:T(8,128)S(1)}, u32[]{:S(2)}, u32[]{:S(2)}) collective-permute-start(f32[64,640]{1,0:T(8,128)S(1)} %pack_weights.1.refs_0_.pack_ref), channel_id=1, source_target_pairs={{0,4},{1,5},{2,6},{3,7},{4,0},{5,1},{6,2},{7,3},{8,12},{9,13},{10,... | collective-permute-start | bytes 491528 | tf_op jit(solution)/shard_map/ppermute | solution.py:911
  6.3 7.5 %collective-permute-start.2 = (f32[64,640]{1,0:T(8,128)S(1)}, f32[64,640]{1,0:T(8,128)S(1)}, u32[]{:S(2)}, u32[]{:S(2)}) collective-permute-start(f32[64,640]{1,0:T(8,128)S(1)} %pack_weights.1.refs_0_.pack_ref), channel_id=1, source_target_pairs={{0,2},{1,3},{2,0},{3,1},{4,6},{5,7},{6,4},{7,5},{8,10},{9,11},{10,... | collective-permute-start | bytes 491528 | tf_op jit(solution)/shard_map/ppermute | solution.py:911
  6.5 7.9 %collective-permute-start.1 = (f32[64,640]{1,0:T(8,128)S(1)}, f32[64,640]{1,0:T(8,128)S(1)}, u32[]{:S(2)}, u32[]{:S(2)}) collective-permute-start(f32[64,640]{1,0:T(8,128)S(1)} %pack_weights.1.refs_0_.pack_ref), channel_id=1, source_target_pairs={{0,1},{1,0},{2,3},{3,2},{4,5},{5,4},{6,7},{7,6},{8,9},{9,8},{10,11... | collective-permute-start | bytes 491528 | tf_op jit(solution)/shard_map/ppermute | solution.py:911
  13.5 1.4 %collective-permute-start.5 = (f32[64,640]{1,0:T(8,128)S(1)}, f32[64,640]{1,0:T(8,128)S(1)}, u32[]{:S(2)}, u32[]{:S(2)}) collective-permute-start(f32[64,640]{1,0:T(8,128)S(1)} %collective-permute-done.4.refs_4_), channel_id=1, source_target_pairs={{0,1},{1,0},{2,3},{3,2},{4,5},{5,4},{6,7},{7,6},{8,9},{9,8},{10,11... | collective-permute-start | bytes 491528 | tf_op jit(solution)/shard_map/ppermute | solution.py:911
  13.8 1.4 %collective-permute-start.3 = (f32[64,640]{1,0:T(8,128)S(1)}, f32[64,640]{1,0:T(8,128)S(1)}, u32[]{:S(2)}, u32[]{:S(2)}) collective-permute-start(f32[64,640]{1,0:T(8,128)S(1)} %collective-permute-done.2.refs_2_), channel_id=1, source_target_pairs={{0,1},{1,0},{2,3},{3,2},{4,5},{5,4},{6,7},{7,6},{8,9},{9,8},{10,11... | collective-permute-start | bytes 491528 | tf_op jit(solution)/shard_map/ppermute | solution.py:911
  14.0 1.4 %collective-permute-start.6 = (f32[64,640]{1,0:T(8,128)S(1)}, f32[64,640]{1,0:T(8,128)S(1)}, u32[]{:S(2)}, u32[]{:S(2)}) collective-permute-start(f32[64,640]{1,0:T(8,128)S(1)} %collective-permute-done.refs_6_), channel_id=1, source_target_pairs={{0,1},{1,0},{2,3},{3,2},{4,5},{5,4},{6,7},{7,6},{8,9},{9,8},{10,11... | collective-permute-start | bytes 491528 | tf_op jit(solution)/shard_map/ppermute | solution.py:911
  52.3 1.7 %collective-permute-start.7 = (bf16[272,640]{1,0:T(8,128)(2,1)S(1)}, bf16[272,640]{1,0:T(8,128)(2,1)S(1)}, u32[]{:S(2)}, u32[]{:S(2)}) collective-permute-start(bf16[272,640]{1,0:T(8,128)(2,1)S(1)} %get-tuple-element.91), channel_id=1, source_target_pairs={{0,1},{1,0},{2,3},{3,2},{4,5},{5,4},{6,7},{7,6},{8,9},{9,8},{10,11... | collective-permute-start | bytes 1044488 | tf_op jit(solution)/shard_map/ppermute | solution.py:911
  54.2 5.1 %collective-permute-start.8 = (bf16[80,640]{1,0:T(8,128)(2,1)S(1)}, bf16[80,640]{1,0:T(8,128)(2,1)S(1)}, u32[]{:S(2)}, u32[]{:S(2)}) collective-permute-start(bf16[80,640]{1,0:T(8,128)(2,1)S(1)} %get-tuple-element.149), channel_id=1, source_target_pairs={{0,2},{1,3},{2,0},{3,1},{4,6},{5,7},{6,4},{7,5},{8,10},{9,11},{10,... | collective-permute-start | bytes 307208 | tf_op jit(solution)/shard_map/ppermute | solution.py:911
  55.9 6.9 %collective-permute-start.9 = (bf16[80,640]{1,0:T(8,128)(2,1)S(1)}, bf16[80,640]{1,0:T(8,128)(2,1)S(1)}, u32[]{:S(2)}, u32[]{:S(2)}) collective-permute-start(bf16[80,640]{1,0:T(8,128)(2,1)S(1)} %get-tuple-element.150), channel_id=1, source_target_pairs={{0,4},{1,5},{2,6},{3,7},{4,0},{5,1},{6,2},{7,3},{8,12},{9,13},{10,... | collective-permute-start | bytes 307208 | tf_op jit(solution)/shard_map/ppermute | solution.py:911
  56.6 6.2 %collective-permute-start.10 = (bf16[80,640]{1,0:T(8,128)(2,1)S(1)}, bf16[80,640]{1,0:T(8,128)(2,1)S(1)}, u32[]{:S(2)}, u32[]{:S(2)}) collective-permute-start(bf16[80,640]{1,0:T(8,128)(2,1)S(1)} %get-tuple-element.151), channel_id=1, source_target_pairs={{0,6},{1,7},{2,4},{3,5},{4,2},{5,3},{6,0},{7,1},{8,14},{9,15},{10,... | collective-permute-start | bytes 307208 | tf_op jit(solution)/shard_map/ppermute | solution.py:911
  59.3 5.2 %copy-start = (bf16[80,640]{1,0:T(8,128)(2,1)}, bf16[80,640]{1,0:T(8,128)(2,1)S(1)}, u32[]{:S(2)}) copy-start(bf16[80,640]{1,0:T(8,128)(2,1)S(1)} %collective-permute-done.8.refs_1_) | copy-start | bytes 307204
  62.9 1.7 %copy-start.2 = (bf16[80,640]{1,0:T(8,128)(2,1)}, bf16[80,640]{1,0:T(8,128)(2,1)S(1)}, u32[]{:S(2)}) copy-start(bf16[80,640]{1,0:T(8,128)(2,1)S(1)} %collective-permute-done.9.refs_2_) | copy-start | bytes 307204
  62.9 1.7 %copy-start.4 = (bf16[80,640]{1,0:T(8,128)(2,1)}, bf16[80,640]{1,0:T(8,128)(2,1)S(1)}, u32[]{:S(2)}) copy-start(bf16[80,640]{1,0:T(8,128)(2,1)S(1)} %collective-permute-done.10.refs_3_) | copy-start | bytes 307204
  62.9 4.5 %collective-permute-start.11 = (bf16[64,640]{1,0:T(8,128)(2,1)S(1)}, bf16[64,640]{1,0:T(8,128)(2,1)S(1)}, u32[]{:S(2)}, u32[]{:S(2)}) collective-permute-start(bf16[64,640]{1,0:T(8,128)(2,1)S(1)} %fusion.3), channel_id=1, source_target_pairs={{0,8},{8,0},{16,24},{24,16},{1,9},{9,1},{17,25},{25,17},{2,10},{10... | collective-permute-start | bytes 245768 | tf_op jit(solution)/shard_map/ppermute | solution.py:911
  64.6 5.6 %slice-start = ((bf16[80,640]{1,0:T(8,128)(2,1)}), bf16[16,640]{1,0:T(8,128)(2,1)S(1)}, s32[]{:S(2)}) async-start(bf16[80,640]{1,0:T(8,128)(2,1)} %copy-done), calls=%async_computation | async-start | bytes 40960 | tf_op jit(solution)/shard_map/slice | solution.py:952
  64.6 5.6 %slice-start.1 = ((bf16[80,640]{1,0:T(8,128)(2,1)}), bf16[16,640]{1,0:T(8,128)(2,1)S(1)}, s32[]{:S(2)}) async-start(bf16[80,640]{1,0:T(8,128)(2,1)} %copy-done.2), calls=%async_computation.1 | async-start | bytes 40960 | tf_op jit(solution)/shard_map/slice | solution.py:952
  64.6 5.5 %slice-start.2 = ((bf16[80,640]{1,0:T(8,128)(2,1)}), bf16[16,640]{1,0:T(8,128)(2,1)S(1)}, s32[]{:S(2)}) async-start(bf16[80,640]{1,0:T(8,128)(2,1)} %copy-done.4), calls=%async_computation.2 | async-start | bytes 40960 | tf_op jit(solution)/shard_map/slice | solution.py:952
  67.4 4.0 %copy-start.3 = (bf16[80,640]{1,0:T(8,128)(2,1)S(1)}, bf16[80,640]{1,0:T(8,128)(2,1)}, u32[]{:S(2)}) copy-start(bf16[80,640]{1,0:T(8,128)(2,1)} %copy-done.2) | copy-start | bytes 307204
  67.4 4.0 %copy-start.5 = (bf16[80,640]{1,0:T(8,128)(2,1)S(1)}, bf16[80,640]{1,0:T(8,128)(2,1)}, u32[]{:S(2)}) copy-start(bf16[80,640]{1,0:T(8,128)(2,1)} %copy-done.4) | copy-start | bytes 307204
  67.5 4.0 %copy-start.1 = (bf16[80,640]{1,0:T(8,128)(2,1)S(1)}, bf16[80,640]{1,0:T(8,128)(2,1)}, u32[]{:S(2)}) copy-start(bf16[80,640]{1,0:T(8,128)(2,1)} %copy-done) | copy-start | bytes 307204
  67.5 5.6 %collective-permute-start.12 = (bf16[64,640]{1,0:T(8,128)(2,1)S(1)}, bf16[64,640]{1,0:T(8,128)(2,1)S(1)}, u32[]{:S(2)}, u32[]{:S(2)}) collective-permute-start(bf16[64,640]{1,0:T(8,128)(2,1)S(1)} %add_convert_fusion.a_ref), channel_id=1, source_target_pairs={{0,16},{8,24},{16,0},{24,8},{1,17},{9,25},{17,1},{25,9},{2,18},{10... | collective-permute-start | bytes 245768 | tf_op jit(solution)/shard_map/ppermute | solution.py:911
  70.2 1.3 %collective-permute-start.13 = (bf16[48,640]{1,0:T(8,128)(2,1)S(1)}, bf16[48,640]{1,0:T(8,128)(2,1)S(1)}, u32[]{:S(2)}, u32[]{:S(2)}) collective-permute-start(bf16[48,640]{1,0:T(8,128)(2,1)S(1)} %pad_maximum_fusion.3), channel_id=1, source_target_pairs={{0,1},{1,0},{2,3},{3,2},{4,5},{5,4},{6,7},{7,6},{8,9},{9,8},{10,11... | collective-permute-start | bytes 184328 | tf_op jit(solution)/shard_map/ppermute | solution.py:911
  73.3 1.2 %collective-permute-start.14 = (f32[8,128]{1,0:T(8,128)S(1)}, f32[8,128]{1,0:T(8,128)S(1)}, u32[]{:S(2)}, u32[]{:S(2)}) collective-permute-start(f32[8,128]{1,0:T(8,128)S(1)} %get-tuple-element.102), channel_id=1, source_target_pairs={{0,1},{1,0},{2,3},{3,2},{4,5},{5,4},{6,7},{7,6},{8,9},{9,8},{10,11... | collective-permute-start | bytes 12296 | tf_op jit(solution)/shard_map/ppermute | solution.py:911
  74.5 5.7 %collective-permute-start.17 = (f32[8,128]{1,0:T(8,128)S(1)}, f32[8,128]{1,0:T(8,128)S(1)}, u32[]{:S(2)}, u32[]{:S(2)}) collective-permute-start(f32[8,128]{1,0:T(8,128)S(1)} %add.23), channel_id=1, source_target_pairs={{0,6},{1,7},{2,4},{3,5},{4,2},{5,3},{6,0},{7,1},{8,14},{9,15},{10,... | collective-permute-start | bytes 12296 | tf_op jit(solution)/shard_map/ppermute | solution.py:911
  76.0 4.2 %collective-permute-start.16 = (f32[8,128]{1,0:T(8,128)S(1)}, f32[8,128]{1,0:T(8,128)S(1)}, u32[]{:S(2)}, u32[]{:S(2)}) collective-permute-start(f32[8,128]{1,0:T(8,128)S(1)} %add.23), channel_id=1, source_target_pairs={{0,4},{1,5},{2,6},{3,7},{4,0},{5,1},{6,2},{7,3},{8,12},{9,13},{10,... | collective-permute-start | bytes 12296 | tf_op jit(solution)/shard_map/ppermute | solution.py:911
  76.7 3.6 %collective-permute-start.15 = (f32[8,128]{1,0:T(8,128)S(1)}, f32[8,128]{1,0:T(8,128)S(1)}, u32[]{:S(2)}, u32[]{:S(2)}) collective-permute-start(f32[8,128]{1,0:T(8,128)S(1)} %add.23), channel_id=1, source_target_pairs={{0,2},{1,3},{2,0},{3,1},{4,6},{5,7},{6,4},{7,5},{8,10},{9,11},{10,... | collective-permute-start | bytes 12296 | tf_op jit(solution)/shard_map/ppermute | solution.py:911
